TPU v7x, 32 devices: a whole 2x2x4 slice. The times are simulated.
32 devices in a mesh: dp: 8 (over z, x), seq: 4 (over y, core).
Axes of the slice: x: 2, y: 2, z: 4, core: 2. Of those that a mesh axis runs over, the one named last changes fastest.
Arguments:
- tokens: bfloat16 [2, 8, 1024, 1024], P(None, 'dp', 'seq'), may hold values from -6 to 6
- segment_ids: int32 [2, 8, 1024], P(None, 'dp', 'seq'), may hold values from 0 to 15, never falling along the last dimension, each value on 1 to 512 neighbouring positions
- cotangent: bfloat16 [2, 8, 1024, 1024], P(None, 'dp', 'seq'), may hold values from -6 to 6
- query_proj: bfloat16 [1024, 1024], P(('dp', 'seq')), may hold values from -0.1875 to 0.1875
- key_proj: bfloat16 [1024, 1024], P(('dp', 'seq')), may hold values from -0.1875 to 0.1875
- value_proj: bfloat16 [1024, 1024], P(('dp', 'seq')), may hold values from -0.1875 to 0.1875
- out_proj: bfloat16 [1024, 1024], P(('dp', 'seq')), may hold values from -0.5 to 0.5
- value_bias: bfloat16 [1024], P(('dp', 'seq')), may hold values from -3 to 3
- content_bias: bfloat16 [1024], P(('dp', 'seq')), may hold values from -3 to 3
- position_bias: bfloat16 [1024], P(('dp', 'seq')), may hold values from -3 to 3
- position_proj: bfloat16 [1024, 64], P(('dp', 'seq')), may hold values from -0.75 to 0.75
- out_bias: bfloat16 [1024], P(('dp', 'seq')), may hold values from -3 to 3
- attn_gain: bfloat16 [1024], P(('dp', 'seq')), may hold values from 0.5 to 1.5
- attn_shift: bfloat16 [1024], P(('dp', 'seq')), may hold values from -2 to 2
- inner_proj: bfloat16 [1024, 4096], P(('dp', 'seq')), may hold values from -0.1875 to 0.1875
- inner_bias: bfloat16 [4096], P(('dp', 'seq')), may hold values from -3 to 3
- outer_proj: bfloat16 [4096, 1024], P(('dp', 'seq')), may hold values from -0.1875 to 0.1875
- outer_bias: bfloat16 [1024], P(('dp', 'seq')), may hold values from -2 to 2
- final_gain: bfloat16 [1024], P(('dp', 'seq')), may hold values from 0.5 to 1.5
- final_shift: bfloat16 [1024], P(('dp', 'seq')), may hold values from -2 to 2
Outputs:
- output: bfloat16 [2, 8, 1024, 1024], P(None, 'dp', 'seq')
- input_grad: float32 [2, 8, 1024, 1024], P(None, 'dp', 'seq')
- query_proj_grad: float32 [1024, 1024], P(('dp', 'seq'))
- key_proj_grad: float32 [1024, 1024], P(('dp', 'seq'))
- value_proj_grad: float32 [1024, 1024], P(('dp', 'seq'))
- out_proj_grad: float32 [1024, 1024], P(('dp', 'seq'))
- value_bias_grad: float32 [1024], P(('dp', 'seq'))
- content_bias_grad: float32 [1024], P(('dp', 'seq'))
- position_bias_grad: float32 [1024], P(('dp', 'seq'))
- position_proj_grad: float32 [1024, 64], P(('dp', 'seq'))
- out_bias_grad: float32 [1024], P(('dp', 'seq'))
- attn_gain_grad: float32 [1024], P(('dp', 'seq'))
- attn_shift_grad: float32 [1024], P(('dp', 'seq'))
- inner_proj_grad: float32 [1024, 4096], P(('dp', 'seq'))
- inner_bias_grad: float32 [4096], P(('dp', 'seq'))
- outer_proj_grad: float32 [4096, 1024], P(('dp', 'seq'))
- outer_bias_grad: float32 [1024], P(('dp', 'seq'))
- final_gain_grad: float32 [1024], P(('dp', 'seq'))
- final_shift_grad: float32 [1024], P(('dp', 'seq'))
Inputs may be any that keep to these rules, and one draw needn't show every extreme that they name: `segment_ids`: ids never fall along a sequence; a token attends to the tokens of its own sequence with the same id.
All inputs are finite; a program needn't handle non-finite values.
Results may differ from a plain program's by a relative error of at most 0.024.
Values may be sent and summed in bfloat16 or wider, within the bound.
No kernel may reach another device: no remote copies, remote signals or barrier semaphores. Data moves between devices by JAX's collectives and lax.ppermute only.
A program may use at most 256 MiB of HBM per device.

v0:
```python
import math

import jax
import jax.numpy as jnp
from jax import lax
from jax.sharding import PartitionSpec as P

H = 16
DH = 64


highest = lax.Precision.HIGHEST


def rotations(length, half_size):
    position = jnp.arange(length, dtype=jnp.int32).astype(jnp.float32)
    steps = jnp.arange(half_size, dtype=jnp.int32).astype(jnp.float32)
    frequency = jnp.exp(steps * (-math.log(10000.0) / half_size))
    angle = position[:, None] * frequency[None, :]
    return (jnp.cos(angle), jnp.sin(angle))


def layer_norm(values, gain, shift):
    average = jnp.mean(values, axis=-1, keepdims=True)
    centred = values - average
    variance = jnp.mean(centred * centred, axis=-1, keepdims=True)
    return centred * lax.rsqrt(variance + 1e-06) * gain + shift


def norm_residual(inputs, branch, gain, shift):
    return layer_norm(inputs + branch, gain, shift)


def gelu_tanh(values):
    return jax.nn.gelu(values, approximate=True)


def product(left, right):
    return jnp.dot(left, right, preferred_element_type=jnp.float32)


def left_product(left, right):
    return jnp.einsum("ti,tj->ij", left, right, preferred_element_type=jnp.float32)


def right_product(left, right):
    return jnp.einsum("ti,ji->tj", left, right, preferred_element_type=jnp.float32)


def per_device(
    tokens,
    segment_ids,
    cotangent,
    query_proj,
    key_proj,
    value_proj,
    out_proj,
    value_bias,
    content_bias,
    position_bias,
    position_proj,
    out_bias,
    attn_gain,
    attn_shift,
    inner_proj,
    inner_bias,
    outer_proj,
    outer_bias,
    final_gain,
    final_shift,
):
    micro_count = tokens.shape[0]
    tok_rows = tokens.shape[2]
    groups = lax.axis_size("seq")
    head_local = H // groups
    local_width = head_local * DH
    half_size = DH // 2
    seq_len = tok_rows * groups
    score_scale = DH ** (-0.5)
    row_block = 512
    block_count = seq_len // row_block
    first_head = lax.axis_index("seq") * head_local
    all_docs = lax.all_gather(segment_ids, "seq", axis=2, tiled=True)
    cos_table, sin_table = rotations(seq_len, half_size)
    cos_rows = cos_table[:, None, :]
    sin_rows = sin_table[:, None, :]
    key_rel = jnp.concatenate([cos_table, sin_table], -1).astype(jnp.bfloat16)
    key_rel = jnp.broadcast_to(key_rel[:, None, :], (seq_len, head_local, DH))
    totals = []
    head_content = jnp.zeros((head_local, DH), jnp.float32)
    head_posbias = jnp.zeros((head_local, DH), jnp.float32)
    head_posproj = jnp.zeros((head_local, DH, DH), jnp.float32)
    out_list = []
    grad_list = []
    for micro_step in range(micro_count):
        gathered = (
            lax.all_gather(query_proj, ("dp", "seq"), axis=0, tiled=True),
            lax.all_gather(key_proj, ("dp", "seq"), axis=0, tiled=True),
            lax.all_gather(value_proj, ("dp", "seq"), axis=0, tiled=True),
            lax.all_gather(out_proj, ("dp", "seq"), axis=0, tiled=True),
            lax.all_gather(value_bias, ("dp", "seq"), axis=0, tiled=True),
            lax.all_gather(content_bias, ("dp", "seq"), axis=0, tiled=True),
            lax.all_gather(position_bias, ("dp", "seq"), axis=0, tiled=True),
            lax.all_gather(position_proj, ("dp", "seq"), axis=0, tiled=True),
            lax.all_gather(out_bias, ("dp", "seq"), axis=0, tiled=True),
            lax.all_gather(attn_gain, ("dp", "seq"), axis=0, tiled=True),
            lax.all_gather(attn_shift, ("dp", "seq"), axis=0, tiled=True),
            lax.all_gather(inner_proj, ("dp", "seq"), axis=0, tiled=True),
            lax.all_gather(inner_bias, ("dp", "seq"), axis=0, tiled=True),
            lax.all_gather(outer_proj, ("dp", "seq"), axis=0, tiled=True),
            lax.all_gather(outer_bias, ("dp", "seq"), axis=0, tiled=True),
            lax.all_gather(final_gain, ("dp", "seq"), axis=0, tiled=True),
            lax.all_gather(final_shift, ("dp", "seq"), axis=0, tiled=True),
        )
        if micro_step == 0:
            totals = [jnp.zeros(weight_part.shape, jnp.float32) for weight_part in gathered]
        (
            full_query,
            full_key,
            full_value,
            full_out,
            full_vbias,
            full_content,
            full_posbias,
            full_posproj,
            full_obias,
            full_attngain,
            full_attnshift,
            full_inner,
            full_ibias,
            full_outer,
            full_fbias,
            full_fgain,
            full_fshift,
        ) = gathered
        x_rows = tokens[micro_step, 0]
        x_float = x_rows.astype(jnp.float32)
        doc_ids = all_docs[micro_step, 0]
        q_tok = (
            product(x_rows, full_query).astype(jnp.bfloat16).reshape(tok_rows, groups, local_width)
        )
        k_tok = (
            product(x_rows, full_key).astype(jnp.bfloat16).reshape(tok_rows, groups, local_width)
        )
        v_tok = (
            product(x_rows, full_value).astype(jnp.bfloat16).reshape(tok_rows, groups, local_width)
        )
        q_heads, k_heads, v_heads = (
            lax.all_to_all(q_tok, "seq", split_axis=1, concat_axis=0, tiled=True),
            lax.all_to_all(k_tok, "seq", split_axis=1, concat_axis=0, tiled=True),
            lax.all_to_all(v_tok, "seq", split_axis=1, concat_axis=0, tiled=True),
        )
        q_heads = q_heads.reshape(seq_len, head_local, DH)
        k_heads = k_heads.reshape(seq_len, head_local, DH)
        v_heads = v_heads.reshape(seq_len, head_local, DH)
        content_rows = lax.dynamic_slice_in_dim(
            full_content.reshape(H, DH), first_head, head_local, 0
        ).astype(jnp.float32)
        posbias_rows = lax.dynamic_slice_in_dim(
            full_posbias.reshape(H, DH), first_head, head_local, 0
        ).astype(jnp.float32)
        vbias_rows = lax.dynamic_slice_in_dim(
            full_vbias.reshape(H, DH), first_head, head_local, 0
        ).astype(jnp.float32)
        posproj_rows = lax.dynamic_slice_in_dim(
            full_posproj.reshape(H, DH, DH), first_head, head_local, 0
        )
        q_float = q_heads.astype(jnp.float32)
        q_content = (q_float + content_rows).astype(jnp.bfloat16)
        q_pos = (q_float + posbias_rows).astype(jnp.bfloat16)
        turned = jnp.einsum("thd,hdf->thf", q_pos, posproj_rows, preferred_element_type=jnp.float32)
        turn_cos = turned[..., :half_size]
        turn_sin = turned[..., half_size:]
        q_rel = jnp.concatenate(
            [turn_cos * cos_rows + turn_sin * sin_rows, turn_cos * sin_rows - turn_sin * cos_rows],
            -1,
        ).astype(jnp.bfloat16)
        q_full = jnp.concatenate([q_content, q_rel], -1)
        k_full = jnp.concatenate([k_heads, key_rel], -1)
        q_blocks = q_full.reshape(block_count, row_block, head_local, 2 * DH)
        doc_blocks = doc_ids.reshape(block_count, row_block)

        def kept_scores(q_block, doc_block, k_full=k_full, doc_ids=doc_ids):
            raw_scores = (
                jnp.einsum("qhd,khd->hqk", q_block, k_full, preferred_element_type=jnp.float32)
                * score_scale
            )
            same_doc = doc_block[:, None] == doc_ids[None, :]
            return jnp.where(same_doc[None], raw_scores, -1e30)

        def attend_block(block_items, v_heads=v_heads, kept_scores=kept_scores):
            q_block, doc_block = block_items
            scores = kept_scores(q_block, doc_block)
            row_max = jnp.max(scores, axis=-1, keepdims=True)
            weights_exp = jnp.exp(scores - row_max)
            row_total = jnp.sum(weights_exp, axis=-1, keepdims=True)
            prob_low = (weights_exp / row_total).astype(jnp.bfloat16)
            mixed_rows = jnp.einsum(
                "hqk,khd->qhd", prob_low, v_heads, preferred_element_type=jnp.float32
            )
            return (mixed_rows, row_max + jnp.log(row_total))

        mixed_rows, log_sums = lax.map(attend_block, (q_blocks, doc_blocks))
        context = (mixed_rows.reshape(seq_len, head_local, DH) + vbias_rows).astype(jnp.bfloat16)
        ctx_tok = lax.all_to_all(
            context.reshape(seq_len, 1, local_width), "seq", split_axis=0, concat_axis=1, tiled=True
        )
        ctx_tok = ctx_tok.reshape(tok_rows, H * DH)
        attn_val = product(ctx_tok, full_out) + full_obias.astype(jnp.float32)
        hidden, first_back = jax.vjp(
            norm_residual,
            x_float,
            attn_val,
            full_attngain.astype(jnp.float32),
            full_attnshift.astype(jnp.float32),
        )
        hidden_low = hidden.astype(jnp.bfloat16)
        inner_val = product(hidden_low, full_inner) + full_ibias.astype(jnp.float32)
        active, gelu_back = jax.vjp(gelu_tanh, inner_val)
        active_low = active.astype(jnp.bfloat16)
        outer_val = product(active_low, full_outer) + full_fbias.astype(jnp.float32)
        result, second_back = jax.vjp(
            norm_residual,
            hidden,
            outer_val,
            full_fgain.astype(jnp.float32),
            full_fshift.astype(jnp.float32),
        )
        out_list.append(result.astype(jnp.bfloat16))
        g_result = cotangent[micro_step, 0].astype(jnp.float32)
        g_hidden, g_outer, g_fgain, g_fshift = second_back(g_result)
        g_outer = g_outer.astype(jnp.bfloat16)
        g_active = right_product(g_outer, full_outer)
        (g_inner,) = gelu_back(g_active)
        g_inner = g_inner.astype(jnp.bfloat16)
        g_hidden = g_hidden + right_product(g_inner, full_inner)
        g_sum, g_attn, g_attngain, g_attnshift = first_back(g_hidden)
        g_attn = g_attn.astype(jnp.bfloat16)
        g_context = right_product(g_attn, full_out).astype(jnp.bfloat16)
        g_heads = lax.all_to_all(
            g_context.reshape(tok_rows, groups, local_width),
            "seq",
            split_axis=1,
            concat_axis=0,
            tiled=True,
        )
        g_heads = g_heads.reshape(block_count, row_block, head_local, DH)

        def grad_block(
            sums_kv, block_items, v_heads=v_heads, k_full=k_full, kept_scores=kept_scores
        ):
            q_block, doc_block, log_block, g_block = block_items
            scores = kept_scores(q_block, doc_block)
            prob_full = jnp.exp(scores - log_block)
            g_prob = jnp.einsum(
                "qhd,khd->hqk", g_block, v_heads, preferred_element_type=jnp.float32
            )
            row_delta = jnp.sum(prob_full * g_prob, axis=-1, keepdims=True)
            g_score = (prob_full * (g_prob - row_delta)).astype(jnp.bfloat16)
            g_qblock = (
                jnp.einsum("hqk,khd->qhd", g_score, k_full, preferred_element_type=jnp.float32)
                * score_scale
            )
            g_keys = (
                sums_kv[0]
                + jnp.einsum(
                    "hqk,qhd->khd", g_score, q_block[..., :DH], preferred_element_type=jnp.float32
                )
                * score_scale
            )
            g_values = sums_kv[1] + jnp.einsum(
                "hqk,qhd->khd",
                prob_full.astype(jnp.bfloat16),
                g_block,
                preferred_element_type=jnp.float32,
            )
            return ((g_keys, g_values), g_qblock)

        empty_kv = jnp.zeros((seq_len, head_local, DH), jnp.float32)
        (g_keys, g_values), g_qblocks = lax.scan(
            grad_block, (empty_kv, empty_kv), (q_blocks, doc_blocks, log_sums, g_heads)
        )
        g_qfull = g_qblocks.reshape(seq_len, head_local, 2 * DH)
        g_content = g_qfull[..., :DH]
        g_rel_cos = g_qfull[..., DH : DH + half_size]
        g_rel_sin = g_qfull[..., DH + half_size :]
        g_turned = jnp.concatenate(
            [
                g_rel_cos * cos_rows + g_rel_sin * sin_rows,
                g_rel_cos * sin_rows - g_rel_sin * cos_rows,
            ],
            -1,
        )
        g_qpos = jnp.einsum(
            "thf,hdf->thd", g_turned, posproj_rows.astype(jnp.float32), precision=highest
        )
        head_posproj = head_posproj + jnp.einsum(
            "thd,thf->hdf", q_pos.astype(jnp.float32), g_turned, precision=highest
        )
        head_content = head_content + jnp.sum(g_content, axis=0)
        head_posbias = head_posbias + jnp.sum(g_qpos, axis=0)
        g_queries = (g_content + g_qpos).astype(jnp.bfloat16).reshape(seq_len, 1, local_width)
        g_keys_low = g_keys.astype(jnp.bfloat16).reshape(seq_len, 1, local_width)
        g_values_low = g_values.astype(jnp.bfloat16).reshape(seq_len, 1, local_width)
        g_q_tok, g_k_tok, g_v_tok = (
            lax.all_to_all(g_queries, "seq", split_axis=0, concat_axis=1, tiled=True),
            lax.all_to_all(g_keys_low, "seq", split_axis=0, concat_axis=1, tiled=True),
            lax.all_to_all(g_values_low, "seq", split_axis=0, concat_axis=1, tiled=True),
        )
        g_q_tok = g_q_tok.reshape(tok_rows, H * DH)
        g_k_tok = g_k_tok.reshape(tok_rows, H * DH)
        g_v_tok = g_v_tok.reshape(tok_rows, H * DH)
        g_input = (
            g_sum
            + right_product(g_q_tok, full_query)
            + right_product(g_k_tok, full_key)
            + right_product(g_v_tok, full_value)
        )
        grad_list.append(g_input)
        step_grads = (
            (0, left_product(x_rows, g_q_tok)),
            (1, left_product(x_rows, g_k_tok)),
            (2, left_product(x_rows, g_v_tok)),
            (3, left_product(ctx_tok, g_attn)),
            (4, jnp.sum(g_context.astype(jnp.float32), axis=0)),
            (8, jnp.sum(g_attn.astype(jnp.float32), axis=0)),
            (9, g_attngain),
            (10, g_attnshift),
            (11, left_product(hidden_low, g_inner)),
            (12, jnp.sum(g_inner.astype(jnp.float32), axis=0)),
            (13, left_product(active_low, g_outer)),
            (14, jnp.sum(g_outer.astype(jnp.float32), axis=0)),
            (15, g_fgain),
            (16, g_fshift),
        )
        for grad_slot, grad_value in step_grads:
            totals[grad_slot] = totals[grad_slot] + grad_value
    zero_index = first_head * 0
    content_full = lax.dynamic_update_slice(
        jnp.zeros((H, DH), jnp.float32), head_content, (first_head, zero_index)
    )
    posbias_full = lax.dynamic_update_slice(
        jnp.zeros((H, DH), jnp.float32), head_posbias, (first_head, zero_index)
    )
    posproj_full = lax.dynamic_update_slice(
        jnp.zeros((H, DH, DH), jnp.float32), head_posproj, (first_head, zero_index, zero_index)
    )
    totals[5] = content_full.reshape(H * DH)
    totals[6] = posbias_full.reshape(H * DH)
    totals[7] = posproj_full.reshape(H * DH, DH)
    reduced = (
        lax.psum_scatter(totals[0], ("dp", "seq"), scatter_dimension=0, tiled=True),
        lax.psum_scatter(totals[1], ("dp", "seq"), scatter_dimension=0, tiled=True),
        lax.psum_scatter(totals[2], ("dp", "seq"), scatter_dimension=0, tiled=True),
        lax.psum_scatter(totals[3], ("dp", "seq"), scatter_dimension=0, tiled=True),
        lax.psum_scatter(totals[4], ("dp", "seq"), scatter_dimension=0, tiled=True),
        lax.psum_scatter(totals[5], ("dp", "seq"), scatter_dimension=0, tiled=True),
        lax.psum_scatter(totals[6], ("dp", "seq"), scatter_dimension=0, tiled=True),
        lax.psum_scatter(totals[7], ("dp", "seq"), scatter_dimension=0, tiled=True),
        lax.psum_scatter(totals[8], ("dp", "seq"), scatter_dimension=0, tiled=True),
        lax.psum_scatter(totals[9], ("dp", "seq"), scatter_dimension=0, tiled=True),
        lax.psum_scatter(totals[10], ("dp", "seq"), scatter_dimension=0, tiled=True),
        lax.psum_scatter(totals[11], ("dp", "seq"), scatter_dimension=0, tiled=True),
        lax.psum_scatter(totals[12], ("dp", "seq"), scatter_dimension=0, tiled=True),
        lax.psum_scatter(totals[13], ("dp", "seq"), scatter_dimension=0, tiled=True),
        lax.psum_scatter(totals[14], ("dp", "seq"), scatter_dimension=0, tiled=True),
        lax.psum_scatter(totals[15], ("dp", "seq"), scatter_dimension=0, tiled=True),
        lax.psum_scatter(totals[16], ("dp", "seq"), scatter_dimension=0, tiled=True),
    )
    output = jnp.stack(out_list)[:, None]
    input_grad = jnp.stack(grad_list)[:, None]
    return (output, input_grad) + tuple(reduced)


def solution(mesh):
    in_specs = (
        P(None, "dp", "seq", None),
        P(None, "dp", "seq"),
        P(None, "dp", "seq", None),
        P(("dp", "seq"), None),
        P(("dp", "seq"), None),
        P(("dp", "seq"), None),
        P(("dp", "seq"), None),
        P(("dp", "seq")),
        P(("dp", "seq")),
        P(("dp", "seq")),
        P(("dp", "seq"), None),
        P(("dp", "seq")),
        P(("dp", "seq")),
        P(("dp", "seq")),
        P(("dp", "seq"), None),
        P(("dp", "seq")),
        P(("dp", "seq"), None),
        P(("dp", "seq")),
        P(("dp", "seq")),
        P(("dp", "seq")),
    )
    out_specs = (
        P(None, "dp", "seq", None),
        P(None, "dp", "seq", None),
        P(("dp", "seq"), None),
        P(("dp", "seq"), None),
        P(("dp", "seq"), None),
        P(("dp", "seq"), None),
        P(("dp", "seq")),
        P(("dp", "seq")),
        P(("dp", "seq")),
        P(("dp", "seq"), None),
        P(("dp", "seq")),
        P(("dp", "seq")),
        P(("dp", "seq")),
        P(("dp", "seq"), None),
        P(("dp", "seq")),
        P(("dp", "seq"), None),
        P(("dp", "seq")),
        P(("dp", "seq")),
        P(("dp", "seq")),
    )
    return jax.shard_map(
        per_device, mesh=mesh, in_specs=in_specs, out_specs=out_specs, check_vma=False
    )
```

profile of v0, /device:TPU:0, one launch (start us, length us, event | category | flops | bytes accessed | tf_op | source)
XLA Modules:
  0.0 1788.3 jit_solution(4598235839548858821)
XLA Ops:
  14.0 6.3 all_gather.71
  20.3 46.1 %all_gather.74 = bf16[1024,64]{1,0:T(8,128)(2,1)} all-gather(bf16[32,64]{1,0:T(8,128)(2,1)} %param.38), channel_id=1, replica_groups=mesh['dp'=8,'seq'=4] {'dp','seq'}, dimensions={0}, use_global_device_ids=true | all-gather | bytes 135168 | tf_op jit(solution)/shard_map/all_gather | solution.py:104
  71.4 37.6 %all-reduce.23 = (bf16[16,64]{1,0:T(8,128)(2,1)S(1)}, bf16[16,64]{1,0:T(8,128)(2,1)S(1)}, bf16[16,64]{1,0:T(8,128)(2,1)S(1)}, bf16[1024]{0:T(1024)(128)(2,1)}, b...) all-reduce(bf16[16,64]{1,0:T(8,128)(2,1)S(1)} %reshape.686, ...), channel_id=1, replica_groups=mesh['dp'=8,'seq'=4] {'dp','seq'}, use_global_device_ids=true, to_apply=%add.1 | all-reduce | flops 9216 | bytes 36864
  122.6 6.0 all-gather.10.cloned.1.call-done
  134.7 52.0 %all-gather.12.cloned.1.call-done = bf16[1024,1024]{1,0:T(8,128)(2,1)} async-done(((bf16[32,1024]{1,0:T(8,128)(2,1)}), bf16[1024,1024]{1,0:T(8,128)(2,1)}) %all-gather.12.cloned.1.call-update) | async-done | bytes 2097168 | tf_op jit(solution)/shard_map/all_gather | solution.py:99
  212.6 4.6 all-to-all-start.1
  255.2 4.3 all-to-all-start.6
  262.5 35.9 %while.54 = (s32[]{:T(128)}, f32[2,512,4,64]{1,0,3,2:T(2,128)}, f32[2,4,512,1]{2,1,3,0:T(4,128)S(1)}, s32[2,512]{1,0:T(2,128)S(1)}, s32[1,1,1024]{2,1,0:T(1,128)...) while((s32[]{:T(128)}, f32[2,512,4,64]{1,0,3,2:T(2,128)}, ...), condition=%wide.region_3.4_spmd, body=%wide.region_0.3_spmd.sunk | while | flops 830994432 | bytes 32057468 | solution.py:203
  270.0 10.4 dynamic_update_slice.47
  288.0 10.4 dynamic_update_slice.47
  315.4 38.2 %while.55 = (s32[]{:T(128)}, f32[2,512,4,64]{1,0,3,2:T(2,128)}, f32[2,4,512,1]{2,1,3,0:T(4,128)S(1)}, s32[2,512]{1,0:T(2,128)S(1)}, s32[1,1,1024]{2,1,0:T(1,128)...) while((s32[]{:T(128)}, f32[2,512,4,64]{1,0,3,2:T(2,128)}, ...), condition=%wide.region_11.12_spmd, body=%wide.region_8.11_spmd.sunk | while | flops 830994432 | bytes 32057468 | solution.py:203
  324.1 10.4 dynamic_update_slice.49
  343.1 10.4 dynamic_update_slice.49
  368.8 6.6 all-to-all-done.3
  379.6 46.9 %all-gather = bf16[32,1,128]{2,1,0:T(2,128)(2,1)S(1)} all-gather(bf16[1,1,128]{2,1,0:T(2,128)(2,1)S(1)} %bitcast.499), channel_id=1, replica_groups=mesh['dp'=8,'seq'=4] {'dp','seq'}, dimensions={0}, use_global_device_ids=true | all-gather | bytes 8448 | tf_op jit(solution)/shard_map/all_gather | solution.py:109
  447.3 8.2 convolution_add_fusion.3
  455.6 8.0 fusion.165
  475.1 7.9 convert_reduce_fusion
  486.0 7.7 convert_reduce_fusion.1
  527.9 85.6 %while.57 = (s32[]{:T(128)}, f32[1024,4,64]{0,2,1:T(8,128)S(1)}, f32[1024,4,64]{0,2,1:T(8,128)}, f32[2,512,4,128]{1,0,3,2:T(2,128)}, bf16[2,512,4,128]{3,1,2,0:T...) while((s32[]{:T(128)}, f32[1024,4,64]{0,2,1:T(8,128)S(1)}, ...), condition=%wide.region_29.30_spmd.clone, body=%wide.region_27.29_spmd.clone.sunk | while | flops 1912600576 | bytes 178325904 | solution.py:280
  551.3 19.6 %dynamic_update_slice.51 = f32[2,512,4,128]{1,0,3,2:T(2,128)} dynamic-update-slice(f32[2,512,4,128]{1,0,3,2:T(2,128)} %get-tuple-element.1129, f32[1,512,4,128]{1,0,3,2:T(1,128)S(1)} %copy.404, s32[]{:T(128)S(6)} %copy.442, s32[]{:T(128)} %constant.117.clone.1..sunk.3, s32[]{:T(128)} %constant.117.clone.1..sunk.3, s32[]{:T(128)} %constant.117.clone.1..sunk.3) | dynamic-update-slice | bytes 2097156 | tf_op jit(solution)/shard_map/while/body/jit(dynamic_update_index_in_dim)/dynamic_update_slice | solution.py:280
  593.9 19.6 %dynamic_update_slice.51 = f32[2,512,4,128]{1,0,3,2:T(2,128)} dynamic-update-slice(f32[2,512,4,128]{1,0,3,2:T(2,128)} %get-tuple-element.1129, f32[1,512,4,128]{1,0,3,2:T(1,128)S(1)} %copy.404, s32[]{:T(128)S(6)} %copy.442, s32[]{:T(128)} %constant.117.clone.1..sunk.3, s32[]{:T(128)} %constant.117.clone.1..sunk.3, s32[]{:T(128)} %constant.117.clone.1..sunk.3) | dynamic-update-slice | bytes 2097156 | tf_op jit(solution)/shard_map/while/body/jit(dynamic_update_index_in_dim)/dynamic_update_slice | solution.py:280
  613.6 4.4 reshape.712
  626.8 84.1 %while.56 = (s32[]{:T(128)}, f32[1024,4,64]{0,2,1:T(8,128)}, f32[1024,4,64]{0,2,1:T(8,128)}, f32[2,512,4,128]{1,0,3,2:T(2,128)}, bf16[2,512,4,128]{3,1,2,0:T(8,1...) while((s32[]{:T(128)}, f32[1024,4,64]{0,2,1:T(8,128)}, ...), condition=%wide.region_22.23_spmd.clone, body=%wide.region_20.22_spmd.clone.sunk | while | flops 1912600576 | bytes 178325904 | solution.py:280
  635.5 4.2 fusion.295
  649.1 19.6 %dynamic_update_slice.50 = f32[2,512,4,128]{1,0,3,2:T(2,128)} dynamic-update-slice(f32[2,512,4,128]{1,0,3,2:T(2,128)} %get-tuple-element.1168, f32[1,512,4,128]{1,0,3,2:T(1,128)S(1)} %copy.403, s32[]{:T(128)S(6)} %copy.454, s32[]{:T(128)} %constant.117.clone.1..sunk.2, s32[]{:T(128)} %constant.117.clone.1..sunk.2, s32[]{:T(128)} %constant.117.clone.1..sunk.2) | dynamic-update-slice | bytes 2097156 | tf_op jit(solution)/shard_map/while/body/jit(dynamic_update_index_in_dim)/dynamic_update_slice | solution.py:280
  677.4 4.5 fusion.295
  691.3 19.6 %dynamic_update_slice.50 = f32[2,512,4,128]{1,0,3,2:T(2,128)} dynamic-update-slice(f32[2,512,4,128]{1,0,3,2:T(2,128)} %get-tuple-element.1168, f32[1,512,4,128]{1,0,3,2:T(1,128)S(1)} %copy.403, s32[]{:T(128)S(6)} %copy.454, s32[]{:T(128)} %constant.117.clone.1..sunk.2, s32[]{:T(128)} %constant.117.clone.1..sunk.2, s32[]{:T(128)} %constant.117.clone.1..sunk.2) | dynamic-update-slice | bytes 2097156 | tf_op jit(solution)/shard_map/while/body/jit(dynamic_update_index_in_dim)/dynamic_update_slice | solution.py:280
  710.9 4.4 reshape.703
  742.9 4.5 all-to-all-done.13
  754.2 6.4 all-to-all-done.9
  768.5 5.4 copy.324
  784.4 5.6 all-to-all-done.14
  795.4 7.9 all-to-all-done.10
  811.2 5.4 copy.326
  827.0 5.5 all-to-all-done.15
  837.6 8.3 all-to-all-done.11
  853.8 5.4 copy.328
  864.6 10.0 convolution_add_fusion.1
  875.7 10.9 fusion.157
  886.6 11.0 convolution_add_fusion
  901.9 38.4 %all-reduce.22 = (f32[1024]{0:T(1024)S(1)}, f32[1024]{0:T(1024)S(1)}, f32[1024]{0:T(1024)S(1)}, f32[1024]{0:T(1024)S(1)}, f32[1024]{0:T(1024)S(1)}, /*index=5*/f...) all-reduce(f32[1024]{0:T(1024)S(1)} %add.461, ...), channel_id=6, replica_groups=mesh['dp'=8,'seq'=4] {'dp','seq'}, use_global_device_ids=true, to_apply=%region_36.37.clone | all-reduce | flops 13312 | bytes 106496
  954.7 37.7 %reduce-scatter.14.cloned.1.call-done = f32[32,1024]{1,0:T(8,128)} async-done(((f32[1024,1024]{1,0:T(8,128)}), f32[32,1024]{1,0:T(8,128)}) %reduce-scatter.14.cloned.1.call-update) | async-done | bytes 131088 | tf_op jit(solution)/shard_map/reduce_scatter | solution.py:355
  992.4 140.1 %reduce-scatter.22.cloned.1.call-done = f32[32,1024]{1,0:T(8,128)} async-done(((f32[1024,1024]{1,0:T(8,128)}), f32[32,1024]{1,0:T(8,128)}) %reduce-scatter.22.cloned.1.call-update) | async-done | bytes 131088
  1132.4 139.8 %reduce-scatter.24.cloned.1.call-done = f32[32,1024]{1,0:T(8,128)} async-done(((f32[1024,1024]{1,0:T(8,128)}), f32[32,1024]{1,0:T(8,128)}) %reduce-scatter.24.cloned.1.call-update) | async-done | bytes 131088
  1272.3 140.0 %reduce-scatter.26.cloned.1.call-done = f32[32,1024]{1,0:T(8,128)} async-done(((f32[1024,1024]{1,0:T(8,128)}), f32[32,1024]{1,0:T(8,128)}) %reduce-scatter.26.cloned.1.call-update) | async-done | bytes 131088
  1412.3 181.8 %reduce-scatter.18.cloned.1.call-done = f32[32,4096]{1,0:T(8,128)} async-done(((f32[1024,4096]{1,0:T(8,128)}), f32[32,4096]{1,0:T(8,128)}) %reduce-scatter.18.cloned.1.call-update) | async-done | bytes 524304 | tf_op jit(solution)/shard_map/reduce_scatter | solution.py:363
  1594.0 187.6 %reduce-scatter.20.cloned.1.call-done = f32[128,1024]{1,0:T(8,128)} async-done(((f32[4096,1024]{1,0:T(8,128)}), f32[128,1024]{1,0:T(8,128)}) %reduce-scatter.20.cloned.1.call-update) | async-done | bytes 524304 | tf_op jit(solution)/shard_map/reduce_scatter | solution.py:365
  (692 shorter events, 439.3 us)
Async XLA Ops:
  7.2 113.9 %copy-start.21 = (bf16[2,1,256,1024]{3,2,1,0:T(8,128)(2,1)S(1)}, bf16[2,1,256,1024]{3,2,1,0:T(8,128)(2,1)}, u32[]{:S(2)}) copy-start(bf16[2,1,256,1024]{3,2,1,0:T(8,128)(2,1)} %param.28) | copy-start | bytes 3145732
  7.2 104.2 %all-gather.8.cloned.1.call-start = ((), (), s32[]{:S(2)}) async-start(), calls=%async_computation.23 | async-start | bytes 2162688 | tf_op jit(solution)/shard_map/all_gather | solution.py:97
  7.9 120.6 %all-gather.10.cloned.1.call-start = ((), (), s32[]{:S(2)}) async-start(), calls=%async_computation.24 | async-start | bytes 2162688 | tf_op jit(solution)/shard_map/all_gather | solution.py:98
  8.7 178.0 %all-gather.12.cloned.1.call-start = ((), (), s32[]{:S(2)}) async-start(), calls=%async_computation.25 | async-start | bytes 2162688 | tf_op jit(solution)/shard_map/all_gather | solution.py:99
  9.4 433.0 %all-gather.14.cloned.1.call-start = ((), (), s32[]{:S(2)}) async-start(), calls=%async_computation.26 | async-start | bytes 2162688 | tf_op jit(solution)/shard_map/all_gather | solution.py:100
  10.0 437.3 %all-gather.16.cloned.1.call-start = ((), (), s32[]{:S(2)}) async-start(), calls=%async_computation.27 | async-start | bytes 8650752 | tf_op jit(solution)/shard_map/all_gather | solution.py:108
  10.6 445.0 %all-gather.18.cloned.1.call-start = ((), (), s32[]{:S(2)}) async-start(), calls=%async_computation.28 | async-start | bytes 8650752 | tf_op jit(solution)/shard_map/all_gather | solution.py:110
  111.4 118.9 %copy-start.87 = (f32[1024,32]{0,1:T(8,128)}, f32[1024,32]{0,1:T(8,128)S(1)}, u32[]{:S(2)}) copy-start(f32[1024,32]{0,1:T(8,128)S(1)} %get-tuple-element.777) | copy-start | bytes 393220
  111.4 118.9 %copy-start.89 = (f32[1024,32]{0,1:T(8,128)}, f32[1024,32]{0,1:T(8,128)S(1)}, u32[]{:S(2)}) copy-start(f32[1024,32]{0,1:T(8,128)S(1)} %get-tuple-element.778) | copy-start | bytes 393220
  116.9 82.7 %all-to-all-start = ((bf16[256,4,256]{0,2,1:T(8,128)(2,1)}), bf16[256,4,256]{0,2,1:T(8,128)(2,1)}, u32[]{:S(2)}, u32[]{:S(2)}) async-start(bf16[256,4,256]{0,2,1:T(8,128)(2,1)} %bitcast.477), calls=%async_computation | async-start | bytes 1048576 | tf_op jit(solution)/shard_map/all_to_all | solution.py:149
  199.6 12.3 all-to-all-start.4
  212.6 13.5 all-to-all-start.1
  226.1 15.0 all-to-all-start.5
  241.2 14.1 all-to-all-start.2
  255.2 57.2 %all-to-all-start.6 = ((bf16[256,4,256]{2,0,1:T(8,128)(2,1)}), bf16[256,4,256]{2,0,1:T(8,128)(2,1)}, u32[]{:S(2)}, u32[]{:S(2)}) async-start(bf16[256,4,256]{2,0,1:T(8,128)(2,1)} %bitcast.475), calls=%async_computation.6 | async-start | bytes 1048576 | tf_op jit(solution)/shard_map/all_to_all | solution.py:151
  315.4 41.7 %copy-start.73 = (f32[1024,1,256]{0,2,1:T(8,128)S(1)}, f32[1024,1,256]{0,2,1:T(8,128)}, u32[]{:S(2)}) copy-start(f32[1024,1,256]{0,2,1:T(8,128)} %reshape.691) | copy-start | bytes 3145732
  315.4 41.7 %copy-start.131 = (f32[256]{0:T(256)S(1)}, f32[256]{0:T(256)}, u32[]{:S(2)}) copy-start(f32[256]{0:T(256)} %reshape.724) | copy-start | bytes 3076
  359.9 66.6 %copy-start.142 = (bf16[1024]{0:T(1024)(128)(2,1)S(1)}, bf16[1024]{0:T(1024)(128)(2,1)}, u32[]{:S(2)}) copy-start(bf16[1024]{0:T(1024)(128)(2,1)} %get-tuple-element.714) | copy-start | bytes 6148
  359.9 66.6 %copy-start.141 = (bf16[1024]{0:T(1024)(128)(2,1)S(1)}, bf16[1024]{0:T(1024)(128)(2,1)}, u32[]{:S(2)}) copy-start(bf16[1024]{0:T(1024)(128)(2,1)} %get-tuple-element.716) | copy-start | bytes 6148
  359.9 66.6 %copy-start.140 = (bf16[1024]{0:T(1024)(128)(2,1)S(1)}, bf16[1024]{0:T(1024)(128)(2,1)}, u32[]{:S(2)}) copy-start(bf16[1024]{0:T(1024)(128)(2,1)} %get-tuple-element.717) | copy-start | bytes 6148
  359.9 66.7 %copy-start.139 = (bf16[1024]{0:T(1024)(128)(2,1)S(1)}, bf16[1024]{0:T(1024)(128)(2,1)}, u32[]{:S(2)}) copy-start(bf16[1024]{0:T(1024)(128)(2,1)} %get-tuple-element.719) | copy-start | bytes 6148
  359.9 66.7 %copy-start.138 = (bf16[1024]{0:T(1024)(128)(2,1)S(1)}, bf16[1024]{0:T(1024)(128)(2,1)}, u32[]{:S(2)}) copy-start(bf16[1024]{0:T(1024)(128)(2,1)} %get-tuple-element.718) | copy-start | bytes 6148
  363.1 12.3 all-to-all-start.3
  375.4 58.9 %all-to-all-start.7 = ((bf16[4,2,32768]{2,1,0:T(2,128)(2,1)}), bf16[4,2,32768]{2,1,0:T(2,128)(2,1)}, u32[]{:S(2)}, u32[]{:S(2)}) async-start(bf16[4,2,32768]{2,1,0:T(2,128)(2,1)} %reshape.770), calls=%async_computation.7 | async-start | bytes 1048576 | tf_op jit(solution)/shard_map/all_to_all | solution.py:205
  426.6 72.1 %copy-start.99 = (f32[1024]{0:T(1024)}, f32[1024]{0:T(1024)S(1)}, u32[]{:S(2)}) copy-start(f32[1024]{0:T(1024)S(1)} %convert_element_type.363) | copy-start | bytes 12292
  445.2 53.4 %copy-start.111 = (f32[256]{0:T(256)}, f32[256]{0:T(256)S(1)}, u32[]{:S(2)}) copy-start(f32[256]{0:T(256)S(1)} %broadcast_multiply_fusion.3) | copy-start | bytes 3076
  447.0 51.7 %copy-start.12 = (f32[256,1024]{1,0:T(8,128)}, f32[256,1024]{1,0:T(8,128)S(1)}, u32[]{:S(2)}) copy-start(f32[256,1024]{1,0:T(8,128)S(1)} %get-tuple-element.793) | copy-start | bytes 3145732
  447.0 51.7 %copy-start.113 = (f32[256]{0:T(256)}, f32[256]{0:T(256)S(1)}, u32[]{:S(2)}) copy-start(f32[256]{0:T(256)S(1)} %broadcast_multiply_fusion.1) | copy-start | bytes 3076
  447.3 51.4 %copy-start.115 = (f32[256]{0:T(256)}, f32[256]{0:T(256)S(1)}, u32[]{:S(2)}) copy-start(f32[256]{0:T(256)S(1)} %fusion.144) | copy-start | bytes 3076
  447.3 51.4 %copy-start.125 = (f32[256]{0:T(256)}, f32[256]{0:T(256)S(1)}, u32[]{:S(2)}) copy-start(f32[256]{0:T(256)S(1)} %fusion.146) | copy-start | bytes 3076
  506.2 13.1 all-to-all-start.12
  519.2 98.8 %all-to-all-start.8 = ((bf16[256,4,256]{0,2,1:T(8,128)(2,1)}), bf16[256,4,256]{0,2,1:T(8,128)(2,1)}, u32[]{:S(2)}, u32[]{:S(2)}) async-start(bf16[256,4,256]{0,2,1:T(8,128)(2,1)} %bitcast.46), calls=%async_computation.8 | async-start | bytes 1048576 | tf_op jit(solution)/shard_map/all_to_all | solution.py:240
  523.4 431.3 %reduce-scatter.16.cloned.1.call-start = ((), (), s32[]{:S(2)}) async-start(), calls=%async_computation.30 | async-start | bytes 540672 | tf_op jit(solution)/shard_map/reduce_scatter | solution.py:359
  719.3 273.0 %reduce-scatter.14.cloned.1.call-start = ((), (), s32[]{:S(2)}) async-start(), calls=%async_computation.29 | async-start | bytes 4325376 | tf_op jit(solution)/shard_map/reduce_scatter | solution.py:355
  734.0 13.4 all-to-all-start.13
  747.4 13.2 all-to-all-start.9
  751.6 380.9 %reduce-scatter.22.cloned.1.call-start = ((), (), s32[]{:S(2)}) async-start(), calls=%async_computation.33 | async-start | bytes 4325376
  777.4 12.6 all-to-all-start.14
  790.0 13.3 all-to-all-start.10
  794.1 478.1 %reduce-scatter.24.cloned.1.call-start = ((), (), s32[]{:S(2)}) async-start(), calls=%async_computation.34 | async-start | bytes 4325376
  820.1 12.4 all-to-all-start.15
  832.5 13.4 all-to-all-start.11
  836.7 575.6 %reduce-scatter.26.cloned.1.call-start = ((), (), s32[]{:S(2)}) async-start(), calls=%async_computation.35 | async-start | bytes 4325376
  859.3 734.7 %reduce-scatter.18.cloned.1.call-start = ((), (), s32[]{:S(2)}) async-start(), calls=%async_computation.31 | async-start | bytes 17301504 | tf_op jit(solution)/shard_map/reduce_scatter | solution.py:363
  874.7 906.9 %reduce-scatter.20.cloned.1.call-start = ((), (), s32[]{:S(2)}) async-start(), calls=%async_computation.32 | async-start | bytes 17301504 | tf_op jit(solution)/shard_map/reduce_scatter | solution.py:365
  897.7 48.4 %copy-start.34 = (f32[256,1024]{1,0:T(8,128)S(1)}, f32[256,1024]{1,0:T(8,128)}, u32[]{:S(2)}) copy-start(f32[256,1024]{1,0:T(8,128)} %copy-done.33) | copy-start | bytes 3145732
  897.7 48.4 %copy-start.128 = (f32[256]{0:T(256)S(1)}, f32[256]{0:T(256)}, u32[]{:S(2)}) copy-start(f32[256]{0:T(256)} %copy-done.127) | copy-start | bytes 3076
  899.1 49.8 %copy-start.44 = (bf16[1024,1024]{1,0:T(8,128)(2,1)S(1)}, bf16[1024,1024]{1,0:T(8,128)(2,1)}, u32[]{:S(2)}) copy-start(bf16[1024,1024]{1,0:T(8,128)(2,1)} %all-gather.10.cloned.1.call-done) | copy-start | bytes 6291460
  (145 other events, 840.8 us)
Sparse Core Ops, SparseCore 0:
  10.9 59.3 all-gather.7
  73.1 55.3 all-gather.9
  131.4 55.2 all-gather.11
  189.4 57.7 all-gather.13
  249.9 76.5 all-gather.15
  329.2 81.8 all-gather.17
  719.4 132.5 reduce-scatter.15
  854.9 137.3 reduce-scatter.13
  995.3 137.0 reduce-scatter.21
  1135.2 136.9 reduce-scatter.23
  1275.2 137.0 reduce-scatter.25
  1415.1 178.8 reduce-scatter.17
  1597.0 184.5 reduce-scatter.19
where the time goes:
time: 1810 us; the launch traced here: 1790 us
  waiting for transfers between devices  944 us (52%)
  local copies, waits for them, and re-layouts  305 us (17%)
  matrix products  205 us (11%)
  blocking collectives  175 us (10%)
  other arithmetic  75.9 us (4%)
  starting transfers between devices  64.9 us (4%)
    unnamed x16, waiting for transfers between devices  424 us
    reduce_scatter x1, waiting for transfers between devices, per_device(): lax.psum_scatter(totals[13], ('dp', 'seq'), scatter_dimension=0, tiled=True)  188 us
    reduce_scatter x1, waiting for transfers between devices, per_device(): lax.psum_scatter(totals[11], ('dp', 'seq'), scatter_dimension=0, tiled=True)  182 us
    dynamic_update_slice x8, local copies, waits for them, and re-layouts, per_device(): lax.scan(grad_block, (empty_kv, empty_kv), (q_blocks, doc_blocks, log_sum...  88 us
    unnamed x329, local copies, waits for them, and re-layouts  83.3 us
    unnamed x2, blocking collectives  76 us
    all_gather x1, waiting for transfers between devices, per_device(): lax.all_gather(value_proj, ('dp', 'seq'), axis=0, tiled=True)  52 us
    dot_general x12, matrix products, left_product(): jnp.einsum('ti,tj->ij', left, right, preferred_element_type=jnp.float32)  51.4 us
  transfers between devices with their start and end apart: 29, of which 19 were waited for; matrix products, arithmetic and copies ran while one was open for 23% of the time, Pallas kernels for 0%

commit v1 on v0

v1 whole, which is shorter than its diff:
```python
import math

import jax
import jax.numpy as jnp
from jax import lax
from jax.experimental import pallas as pl
from jax.experimental.pallas import tpu as pltpu
from jax.sharding import Mesh, PartitionSpec as P

H = 16
DH = 64
BLK = 256
NEG = -1e30
BF = jnp.bfloat16
F32 = jnp.float32
ALL = ("dp", "yy", "core")
SEQ = ("yy", "core")
CHIP = ("dp", "yy")


def dot(a, b, ca=1, cb=0):
    return lax.dot_general(a, b, (((ca,), (cb,)), ((), ())), preferred_element_type=F32)


def rotations(length, half_size):
    position = jnp.arange(length, dtype=jnp.int32).astype(F32)
    steps = jnp.arange(half_size, dtype=jnp.int32).astype(F32)
    frequency = jnp.exp(steps * (-math.log(10000.0) / half_size))
    angle = position[:, None] * frequency[None, :]
    return (jnp.cos(angle), jnp.sin(angle))


def layer_norm(values, gain, shift):
    average = jnp.mean(values, axis=-1, keepdims=True)
    centred = values - average
    variance = jnp.mean(centred * centred, axis=-1, keepdims=True)
    return centred * lax.rsqrt(variance + 1e-06) * gain + shift


def gelu_tanh(values):
    return jax.nn.gelu(values, approximate=True)


def swap(x, axis, bit):
    n = lax.axis_size(axis)
    return lax.ppermute(x, axis, [(i, i ^ bit) for i in range(n)])


def side(axis, bit):
    return jnp.where((lax.axis_index(axis) & bit) != 0, 1, 0)


def double(x, axis, bit, dim):
    other = swap(x, axis, bit)
    mine = side(axis, bit) == 0
    return jnp.stack([jnp.where(mine, x, other), jnp.where(mine, other, x)], dim)


def bits_of(axis):
    n = lax.axis_size(axis)
    return [1 << k for k in reversed(range(n.bit_length() - 1))]


def gather_bits(x, axis, dim=0):
    bits = bits_of(axis)
    for k, bit in enumerate(bits):
        x = double(x, axis, bit, dim + k)
    return x.reshape(x.shape[:dim] + (lax.axis_size(axis),) + x.shape[dim + len(bits) :])


def halve(terms, done, order, width):
    left = list(done)
    for axis, bit in order:
        dim = left.index((axis, bit))
        left.pop(dim)
        mine = side(axis, bit)
        send = sum(
            lax.dynamic_index_in_dim(t, 1 - mine, dim, keepdims=False).astype(F32) for t in terms
        ).astype(BF)
        got = swap(send, axis, bit)
        terms = [lax.dynamic_index_in_dim(t, mine, dim, keepdims=False) for t in terms] + [got]
    return sum(t.astype(F32) for t in terms)


def prep_head(e, q, qr, k, kr, first, bias, mat, cos, sin, pk):
    base = jnp.where(first, q, qr) if e == 0 else jnp.where(first, qr, q)
    both = (base + bias).astype(BF)
    turned = dot(both, mat)
    rel = turned[:, :128] * cos + turned[:, 128:] * sin
    qf = (jnp.where(first, both.astype(F32), rel) * (DH**-0.5)).astype(BF)
    kf = jnp.where(first, k if e == 0 else kr, pk).astype(BF)
    return both, qf, kf


def fwd_kernel(
    lohi, q_ref, k_ref, v_ref, segr_ref, segc_ref, cos_ref, sin_ref, pk_ref, bias_ref, mat_ref,
    vb_ref, ctx_ref, o_ref, lse_ref, qf_s, kf_s, sc_s,
):
    m = pl.program_id(0)
    nb = q_ref.shape[1] // BLK
    first = lax.broadcasted_iota(jnp.int32, (BLK, 128), 1) < DH

    def prep(i, c):
        rows = pl.ds(pl.multiple_of(i * BLK, BLK), BLK)
        q = q_ref[0, rows, :].astype(F32)
        k = k_ref[0, rows, :].astype(F32)
        qr, kr = pltpu.roll(q, DH, 1), pltpu.roll(k, DH, 1)
        for e in range(2):
            _, qf, kf = prep_head(
                e, q, qr, k, kr, first, bias_ref[0, e : e + 1, :], mat_ref[0, e],
                cos_ref[rows, :], sin_ref[rows, :], pk_ref[rows, :],
            )
            qf_s[e, rows, :] = qf
            kf_s[e, rows, :] = kf
        return c

    lax.fori_loop(0, nb, prep, 0)

    def q_block(i, c):
        rows = pl.ds(pl.multiple_of(i * BLK, BLK), BLK)
        at = (m * nb + i) * 2
        lo, hi = lohi[at], lohi[at + 1]
        segq = segc_ref[0, rows, :]
        segq = jnp.concatenate([segq] * (BLK // 128), 1)
        outs = []
        for e in range(2):
            qf = qf_s[e, rows, :]

            def scores(j, top, e=e, qf=qf):
                cols = pl.ds(pl.multiple_of(j * BLK, BLK), BLK)
                s = dot(qf, kf_s[e, cols, :], 1, 1)
                s = jnp.where(segq == segr_ref[0, j], s, NEG)
                sc_s[j] = s
                for g in range(BLK // 128):
                    top = jnp.maximum(top, s[:, g * 128 : g * 128 + 128])
                return top

            top = lax.fori_loop(lo, hi, scores, jnp.full((BLK, 128), NEG, F32))
            top = jnp.max(top, axis=1, keepdims=True)

            def mix(j, carry):
                total, acc = carry
                cols = pl.ds(pl.multiple_of(j * BLK, BLK), BLK)
                p = jnp.exp(sc_s[j] - top)
                for g in range(BLK // 128):
                    total = total + p[:, g * 128 : g * 128 + 128]
                acc = acc + dot(p.astype(BF), v_ref[0, cols, :])
                return total, acc

            zero = jnp.zeros((BLK, 128), F32)
            total, acc = lax.fori_loop(lo, hi, mix, (zero, zero))
            total = jnp.sum(total, axis=1, keepdims=True)
            outs.append((acc / total, top + jnp.log(total)))
        o = jnp.where(first, outs[0][0], outs[1][0])
        o_ref[0, rows, :] = o
        lse_ref[0, rows, :] = jnp.where(first, outs[0][1], outs[1][1])
        ctx_ref[0, rows, :] = (o + vb_ref[0]).astype(BF)
        return c

    lax.fori_loop(0, nb, q_block, 0)


def bwd_kernel(
    lohi, q_ref, k_ref, v_ref, g_ref, o_ref, lse_ref, segr_ref, segc_ref, cos_ref, sin_ref,
    pk_ref, bias_ref, mat_ref, matt_ref, gqkv_ref, gsm_ref, gpp_ref,
    both_s, qf_s, kf_s, lse_s, dl_s, gq_s, res_s,
):
    m, p = pl.program_id(0), pl.program_id(1)
    nb = q_ref.shape[1] // BLK
    width = gqkv_ref.shape[2] // 3
    first = lax.broadcasted_iota(jnp.int32, (BLK, 128), 1) < DH

    def prep(i, c):
        rows = pl.ds(pl.multiple_of(i * BLK, BLK), BLK)
        q = q_ref[0, rows, :].astype(F32)
        k = k_ref[0, rows, :].astype(F32)
        qr, kr = pltpu.roll(q, DH, 1), pltpu.roll(k, DH, 1)
        lse_t = lse_ref[0, rows, :].T
        dl_t = (g_ref[0, rows, :].astype(F32) * o_ref[0, rows, :]).T
        for e in range(2):
            both, qf, kf = prep_head(
                e, q, qr, k, kr, first, bias_ref[0, e : e + 1, :], mat_ref[0, e],
                cos_ref[rows, :], sin_ref[rows, :], pk_ref[rows, :],
            )
            both_s[e, rows, :] = both
            qf_s[e, rows, :] = qf
            kf_s[e, rows, :] = kf
            lse_s[e, i] = lse_t[e * DH : e * DH + 8, :]
            dl = jnp.sum(dl_t[e * DH : (e + 1) * DH, :], axis=0, keepdims=True)
            dl_s[e, i] = jnp.broadcast_to(dl, (8, BLK))
        return c

    lax.fori_loop(0, nb, prep, 0)

    for e in range(2):
        mine = first if e == 0 else jnp.logical_not(first)

        def clear(i, c):
            gq_s[pl.ds(pl.multiple_of(i * BLK, BLK), BLK), :] = jnp.zeros((BLK, 128), F32)
            return c

        lax.fori_loop(0, nb, clear, 0)

        def k_block(j, c, e=e, mine=mine):
            rows = pl.ds(pl.multiple_of(j * BLK, BLK), BLK)
            at = (m * nb + j) * 2
            lo, hi = lohi[at], lohi[at + 1]
            kf = kf_s[e, rows, :]
            vm = jnp.where(mine, v_ref[0, rows, :].astype(F32), 0.0).astype(BF)
            segk = jnp.concatenate([segc_ref[0, rows, :]] * (BLK // 128), 1)

            def q_step(i, carry):
                gk, gv = carry
                cols = pl.ds(pl.multiple_of(i * BLK, BLK), BLK)
                qf = qf_s[e, cols, :]
                g = g_ref[0, cols, :]
                s = dot(kf, qf, 1, 1) - lse_s[e, i, 0:1, :]
                prob = jnp.where(segk == segr_ref[0, i], jnp.exp(s), 0.0)
                gp = dot(vm, g, 1, 1) - dl_s[e, i, 0:1, :]
                ds = (prob * gp).astype(BF)
                gv = gv + dot(prob.astype(BF), g)
                gk = gk + dot(ds, qf)
                gq_s[cols, :] = gq_s[cols, :] + dot(ds, kf, 0, 0)
                return gk, gv

            zero = jnp.zeros((BLK, 128), F32)
            gk, gv = lax.fori_loop(lo, hi, q_step, (zero, zero))
            if e == 0:
                res_s[1, rows, :] = gk
                res_s[2, rows, :] = gv
            else:
                res_s[1, rows, :] = jnp.where(first, res_s[1, rows, :], pltpu.roll(gk, DH, 1))
                res_s[2, rows, :] = jnp.where(first, res_s[2, rows, :], gv)
            return c

        lax.fori_loop(0, nb, k_block, 0)

        def finish(i, carry, e=e):
            s_content, s_pos, s_proj = carry
            rows = pl.ds(pl.multiple_of(i * BLK, BLK), BLK)
            g = gq_s[rows, :] * (DH**-0.5)
            turned = jnp.concatenate(
                [(g * cos_ref[rows, :]).astype(BF), (g * sin_ref[rows, :]).astype(BF)], 1
            )
            gqp = dot(turned, matt_ref[0, e])
            gq = g + gqp
            if e == 0:
                res_s[0, rows, :] = gq
            else:
                res_s[0, rows, :] = jnp.where(first, res_s[0, rows, :], pltpu.roll(gq, DH, 1))
            s_content = s_content + jnp.sum(g, axis=0, keepdims=True)
            s_pos = s_pos + jnp.sum(gqp, axis=0, keepdims=True)
            s_proj = s_proj + dot(both_s[e, rows, :], turned, 0, 0)
            return s_content, s_pos, s_proj

        row = jnp.zeros((1, 128), F32)
        s_content, s_pos, s_proj = lax.fori_loop(
            0, nb, finish, (row, row, jnp.zeros((128, 256), F32))
        )
        gsm_ref[0, 0, e, 0:1, :] = s_content
        gsm_ref[0, 0, e, 1:2, :] = s_pos
        gpp_ref[0, 0, e] = s_proj

    for at in range(width // 128):

        @pl.when(p == at)
        def _(at=at):
            for part in range(3):
                off = part * width + at * 128
                gqkv_ref[0, :, off : off + 128] = res_s[part].astype(BF)


def attention_specs(L, width):
    pairs = width // 128
    pair = lambda k: pl.BlockSpec((1, L, 128), lambda m, p, *_: (m, 0, k * pairs + p))
    per_m = lambda *s: pl.BlockSpec((1,) + s, lambda m, p, *_: (m,) + (0,) * len(s))
    per_p = lambda *s: pl.BlockSpec((1,) + s, lambda m, p, *_: (p,) + (0,) * len(s))
    whole = lambda *s: pl.BlockSpec(s, lambda m, p, *_: (0,) * len(s))
    return pairs, pair, per_m, per_p, whole


def attention_forward(qkv, lohi, segr, segc, cos, sin, pk, bias, mat, vb):
    M, L, w3 = qkv.shape
    width = w3 // 3
    nb = L // BLK
    pairs, pair, per_m, per_p, whole = attention_specs(L, width)
    return pl.pallas_call(
        fwd_kernel,
        out_shape=(
            jax.ShapeDtypeStruct((M, L, width), BF),
            jax.ShapeDtypeStruct((M, L, width), F32),
            jax.ShapeDtypeStruct((M, L, width), F32),
        ),
        grid_spec=pltpu.PrefetchScalarGridSpec(
            num_scalar_prefetch=1,
            grid=(M, pairs),
            in_specs=[
                pair(0), pair(1), pair(2), per_m(nb, 1, BLK), per_m(L, 128), whole(L, 128),
                whole(L, 128), whole(L, 128), per_p(2, 128), per_p(2, 128, 256), per_p(1, 128),
            ],
            out_specs=[pair(0), pair(0), pair(0)],
            scratch_shapes=[
                pltpu.VMEM((2, L, 128), BF),
                pltpu.VMEM((2, L, 128), BF),
                pltpu.VMEM((nb, BLK, BLK), F32),
            ],
        ),
        compiler_params=pltpu.CompilerParams(
            dimension_semantics=("arbitrary", "arbitrary"), vmem_limit_bytes=32 << 20
        ),
        name="attend",
    )(lohi, qkv, qkv, qkv, segr, segc, cos, sin, pk, bias, mat, vb)


def attention_backward(qkv, g, o, lse, lohi, segr, segc, cos, sin, pk, bias, mat, matt):
    M, L, w3 = qkv.shape
    width = w3 // 3
    nb = L // BLK
    pairs, pair, per_m, per_p, whole = attention_specs(L, width)
    per_mp = lambda *s: pl.BlockSpec((1, 1) + s, lambda m, p, *_: (m, p) + (0,) * len(s))
    return pl.pallas_call(
        bwd_kernel,
        out_shape=(
            jax.ShapeDtypeStruct((M, L, w3), BF),
            jax.ShapeDtypeStruct((M, pairs, 2, 8, 128), F32),
            jax.ShapeDtypeStruct((M, pairs, 2, 128, 256), F32),
        ),
        grid_spec=pltpu.PrefetchScalarGridSpec(
            num_scalar_prefetch=1,
            grid=(M, pairs),
            in_specs=[
                pair(0), pair(1), pair(2), pair(0), pair(0), pair(0), per_m(nb, 1, BLK),
                per_m(L, 128), whole(L, 128), whole(L, 128), whole(L, 128), per_p(2, 128),
                per_p(2, 128, 256), per_p(2, 256, 128),
            ],
            out_specs=[per_m(L, w3), per_mp(2, 8, 128), per_mp(2, 128, 256)],
            scratch_shapes=[
                pltpu.VMEM((2, L, 128), BF),
                pltpu.VMEM((2, L, 128), BF),
                pltpu.VMEM((2, L, 128), BF),
                pltpu.VMEM((2, nb, 8, BLK), F32),
                pltpu.VMEM((2, nb, 8, BLK), F32),
                pltpu.VMEM((L, 128), F32),
                pltpu.VMEM((3, L, 128), F32),
            ],
        ),
        compiler_params=pltpu.CompilerParams(
            dimension_semantics=("arbitrary", "arbitrary"), vmem_limit_bytes=40 << 20
        ),
        name="attend_back",
    )(lohi, qkv, qkv, qkv, g, o, lse, segr, segc, cos, sin, pk, bias, mat, matt)


def per_device(
    tokens, segment_ids, cotangent, query_proj, key_proj, value_proj, out_proj, value_bias,
    content_bias, position_bias, position_proj, out_bias, attn_gain, attn_shift, inner_proj,
    inner_bias, outer_proj, outer_bias, final_gain, final_shift,
):
    M, _, T, D = tokens.shape
    n_dp, n_yy, n_core = (lax.axis_size(a) for a in ALL)
    S = n_yy * n_core
    chips = n_dp * n_yy
    devices = chips * n_core
    L = T * S
    R = query_proj.shape[0]
    U = outer_proj.shape[0]
    FF = U * devices
    hl = H // S
    width = hl * DH
    pairs = width // 128
    half = DH // 2
    N = M * T
    core = lax.axis_index("core")
    seq = lax.axis_index("yy") * n_core + core
    dp_bits = [("dp", b) for b in bits_of("dp")]
    yy_bits = [("yy", b) for b in bits_of("yy")]
    two = lambda bits: (2,) * len(bits)

    smalls = [
        content_bias, position_bias, position_proj.reshape(-1), value_bias, out_bias, attn_gain,
        attn_shift, outer_bias, final_gain, final_shift, inner_bias,
    ]
    sizes = [s.size for s in smalls]
    w3 = 3 * width
    extra = -(-sum(sizes) // w3)
    packed = jnp.concatenate(smalls + [jnp.zeros((extra * w3 - sum(sizes),), BF)])
    packed = jnp.broadcast_to(packed.reshape(1, extra, w3), (S, extra, w3))
    by_seq = jnp.stack([query_proj, key_proj, value_proj], 0).reshape(3, R, S, width)
    by_seq = by_seq.transpose(2, 1, 0, 3).reshape(S, R, w3)
    mixed = lax.all_to_all(
        jnp.concatenate([by_seq, packed], 1), SEQ, split_axis=0, concat_axis=0, tiled=True
    )
    mixed = gather_bits(mixed, "dp")
    w_qkv = mixed[:, :, :R].reshape(D, w3)
    flat = mixed[:, :, R:].reshape(devices, extra * w3)
    full, at = [], 0
    for size in sizes:
        full.append(flat[:, at : at + size])
        at += size
    heads = lambda v: lax.dynamic_slice_in_dim(v.reshape(S, -1), seq, 1, 0)
    full_content, full_posbias, full_posproj, full_vbias = full[:4]
    vec = lambda v: v.reshape(1, -1).astype(F32)
    full_obias, full_again, full_ashift, full_fbias, full_fgain, full_fshift = map(vec, full[4:10])
    ib = lax.dynamic_index_in_dim(full[10].reshape(chips, n_core, 2, U // 2), core, 1, False)
    full_ibias = ib.transpose(1, 0, 2).reshape(1, -1).astype(F32)

    inner_cols = inner_proj.reshape(R, chips, n_core, 2, U // 2).transpose(2, 0, 3, 1, 4)
    inner_cols = inner_cols.reshape(n_core, R, FF // n_core)
    inner_mine = lax.all_to_all(inner_cols, "core", split_axis=0, concat_axis=0, tiled=True)
    inner_mine = inner_mine.reshape(n_core * R, FF // n_core)
    out_mine = lax.all_gather(out_proj, "core", axis=0, tiled=True)
    outer_mine = jnp.concatenate([outer_proj[: U // 2], outer_proj[U // 2 :]], 1)
    big = jnp.concatenate([inner_mine, out_mine, outer_mine], 1)
    big = lax.all_gather(big, CHIP, axis=0, tiled=True)
    FH = FF // n_core
    w_inner = big[:, :FH]
    w_out = big[:, FH : FH + D]
    w_outer = [big[:, FH + D + k * D : FH + 2 * D + k * D] for k in range(2)]

    x = tokens[:, 0]
    x_all = x
    for k, (axis, bit) in enumerate(yy_bits):
        x_all = double(x_all, axis, bit, 1 + k)
    x_all = x_all.reshape(M, n_yy, T, D)
    x_all = double(x_all, "core", 1, 2).reshape(M * L, D)
    docs = lax.all_gather(segment_ids[:, 0], SEQ, axis=1, tiled=True)
    nb = L // BLK
    ends = docs.reshape(M, nb, BLK)
    lo = jnp.sum(docs[:, None, :] < ends[:, :, :1], -1) // BLK
    hi = (jnp.sum(docs[:, None, :] <= ends[:, :, -1:], -1) + BLK - 1) // BLK
    lohi = jnp.stack([lo, hi], -1).reshape(-1).astype(jnp.int32)
    segr = docs.reshape(M, nb, 1, BLK)
    segc = jnp.broadcast_to(docs[:, :, None], (M, L, 128))
    cos_t, sin_t = rotations(L, half)
    none = jnp.zeros((L, DH), F32)
    cos2 = jnp.concatenate([none, cos_t, cos_t], 1)
    sin2 = jnp.concatenate([none, sin_t, sin_t], 1)
    pk2 = jnp.concatenate([none, cos_t, sin_t], 1).astype(BF).astype(F32)
    bias = jnp.stack(
        [heads(full_content).reshape(hl, DH), heads(full_posbias).reshape(hl, DH)], 1
    )
    bias = bias.reshape(pairs, 2, 2 * DH).astype(F32)
    pp = heads(full_posproj).reshape(hl, DH, DH)
    pc, ps = pp[..., :half], pp[..., half:]
    z64 = jnp.zeros((hl, DH, DH), BF)
    mat = jnp.concatenate([z64, pc, -ps, z64, ps, pc], 2)
    mat = jnp.concatenate([jnp.zeros_like(mat), mat], 1).reshape(pairs, 2, 128, 256)
    matt = jnp.swapaxes(mat[:, :, DH:, :], 2, 3)
    matt = jnp.concatenate([matt, jnp.zeros_like(matt)], 3)
    vb = heads(full_vbias).reshape(pairs, 1, 128).astype(F32)

    qkv = dot(x_all, w_qkv).astype(BF).reshape(M, L, w3)
    ctx, o, lse = attention_forward(qkv, lohi, segr, segc, cos2, sin2, pk2, bias, mat, vb)
    ctx_tok = lax.all_to_all(
        ctx.reshape(M, S, T, width), SEQ, split_axis=1, concat_axis=1, tiled=True
    )
    ctx_tok = ctx_tok.transpose(0, 2, 1, 3).reshape(N, H * DH)
    x_float = x.reshape(N, D).astype(F32)
    attn = dot(ctx_tok, w_out) + full_obias
    hidden, first_back = jax.vjp(
        lambda a, g, b: layer_norm(a, g, b), x_float + attn, full_again, full_ashift
    )
    pair = lambda v: jnp.concatenate([v, swap(v, "core", 1)], 0)
    hid_pair = pair(hidden.astype(BF))
    inner = dot(hid_pair, w_inner) + full_ibias
    active, gelu_back = jax.vjp(gelu_tanh, inner)
    active = active.astype(BF)
    part = dot(active[:, :D], w_outer[0]) if FH == D else None
    FQ = FH // 2
    part = dot(active[:, :FQ], w_outer[0]) + dot(active[:, FQ:], w_outer[1])
    outer = part[:N] + swap(part[N:].astype(BF), "core", 1).astype(F32) + full_fbias
    result, second_back = jax.vjp(
        lambda a, g, b: layer_norm(a, g, b), hidden + outer, full_fgain, full_fshift
    )
    output = result.astype(BF).reshape(M, 1, T, D)

    g_hidden, g_fgain, g_fshift = second_back(cotangent[:, 0].reshape(N, D).astype(F32))
    go = g_hidden.astype(BF)
    go_pair = pair(go)
    g_outer_w = [dot(active[:, k * FQ : (k + 1) * FQ], go_pair, 0, 0).astype(BF) for k in range(2)]
    g_active = jnp.concatenate([dot(go_pair, w, 1, 1) for w in w_outer], 1)
    (g_inner,) = gelu_back(g_active)
    gi = g_inner.astype(BF)
    g_part = dot(gi, w_inner, 1, 1)
    g_inner_w = dot(hid_pair, gi, 0, 0).astype(BF)
    g_hidden = g_hidden + g_part[:N] + swap(g_part[N:].astype(BF), "core", 1).astype(F32)
    g_sum, g_again, g_ashift = first_back(g_hidden)
    ga = g_sum.astype(BF)
    gc = dot(ga, w_out, 1, 1).astype(BF)
    g_heads = lax.all_to_all(
        gc.reshape(M, T, S, width).transpose(0, 2, 1, 3), SEQ, split_axis=1, concat_axis=1, tiled=True
    ).reshape(M, L, width)
    g_out_w = dot(ctx_tok, ga, 0, 0).astype(BF)
    gqkv, gsm, gpp = attention_backward(
        qkv, g_heads, o, lse, lohi, segr, segc, cos2, sin2, pk2, bias, mat, matt
    )
    gqkv = gqkv.reshape(M * L, w3)

    dx = dot(gqkv, w_qkv, 1, 1).astype(BF)
    dx = halve(
        [dx.reshape((M,) + two(yy_bits) + (2, T, D)).transpose(
            tuple(range(1, len(yy_bits) + 2)) + (0, len(yy_bits) + 2, len(yy_bits) + 3)
        )],
        yy_bits + [("core", 1)],
        [("core", 1)] + yy_bits,
        D,
    )
    input_grad = (g_sum + dx.reshape(N, D)).reshape(M, 1, T, D)

    g_qkv_w = dot(x_all, gqkv, 0, 0).astype(BF)
    colsum = lambda v: jnp.sum(v.astype(F32), axis=0)
    spread = lambda v: lax.dynamic_update_slice(
        jnp.zeros((S, v.size), F32), v.reshape(1, -1), (seq, 0)
    ).reshape(devices, -1)
    gsm = jnp.sum(gsm, 0)[:, :, :2, :DH].reshape(hl, 2, DH)
    gpp = jnp.sum(gpp, 0).reshape(hl, 128, 256)[:, DH:]
    e1, e2 = gpp[:, :, DH : 2 * DH], gpp[:, :, 3 * DH :]
    g_posproj = jnp.concatenate(
        [e1[..., :half] + e2[..., half:], e2[..., :half] - e1[..., half:]], -1
    )
    own = lambda v: v.reshape(devices, -1)
    g_ibias = colsum(gi).reshape(2, chips, 1, U // 2).transpose(1, 2, 0, 3).reshape(chips, 1, U)
    on_core = (jnp.arange(n_core) == core).reshape(1, n_core, 1)
    g_ibias = jnp.where(on_core, g_ibias, 0.0).reshape(devices, U)
    g_smalls = jnp.concatenate(
        [
            spread(gsm[:, 0]), spread(gsm[:, 1]), spread(g_posproj), own(colsum(gc)),
            own(colsum(ga)), own(g_again), own(g_ashift), own(colsum(go)), own(g_fgain),
            own(g_fshift), g_ibias, jnp.zeros((devices, extra * w3 - sum(sizes)), F32),
        ],
        1,
    )
    g_smalls = g_smalls.astype(BF).reshape(two(dp_bits + yy_bits) + (2, extra, w3))
    g_smalls = halve(
        [g_smalls], dp_bits + yy_bits + [("core", 1)], [("core", 1)] + yy_bits, w3
    ).astype(BF)
    g_mixed = jnp.concatenate(
        [g_qkv_w.reshape(two(dp_bits) + (S * R, w3)), g_smalls], len(dp_bits)
    )
    g_mixed = halve([g_mixed], dp_bits, dp_bits[::-1], w3)
    g_small = g_mixed[S * R :].reshape(-1)
    g_rows = lax.all_to_all(
        g_mixed[: S * R].astype(BF).reshape(S, R, 3, width), SEQ, split_axis=0, concat_axis=0,
        tiled=True,
    )
    g_rows = g_rows.astype(F32).transpose(2, 1, 0, 3).reshape(3, R, D)
    small_grads, at = [], 0
    for size, like in zip(sizes, smalls):
        small_grads.append(g_small[at : at + size])
        at += size

    chip_bits = dp_bits + yy_bits
    orders = [yy_bits + dp_bits[::-1], dp_bits[::-1][:1] + yy_bits + dp_bits[::-1][1:]]
    rows = two(chip_bits) + (n_core * R,)
    red_outer = [
        halve([g.reshape(rows + (D,))], chip_bits, orders[k], D) for k, g in enumerate(g_outer_w)
    ]
    red_inner = [
        halve([g_inner_w[:, k * FQ : (k + 1) * FQ].reshape(rows + (FQ,))], chip_bits, orders[k], FQ)
        for k in range(2)
    ]
    go2 = g_out_w.reshape(D, n_core, D // n_core)
    mine = lax.dynamic_index_in_dim(go2, core, 1, False).astype(F32)
    theirs = lax.dynamic_index_in_dim(go2, 1 - core, 1, False)
    g_out_half = (mine + swap(theirs, "core", 1).astype(F32)).astype(BF)
    red_out = halve([g_out_half.reshape(rows + (D // n_core,))], chip_bits, orders[0], D)
    red_inner = jnp.concatenate(red_inner, 1).astype(BF).reshape(n_core, R, FH)
    red_inner = lax.all_to_all(red_inner, "core", split_axis=0, concat_axis=0, tiled=True)
    inner_grad = red_inner.reshape(n_core, R, 2, chips, U // 2).transpose(1, 3, 0, 2, 4)
    inner_grad = inner_grad.astype(F32).reshape(R, FF)
    red_out = lax.all_to_all(
        red_out.astype(BF).reshape(n_core, R, D // n_core), "core", split_axis=0, concat_axis=0,
        tiled=True,
    )
    out_grad = red_out.astype(F32).transpose(1, 0, 2).reshape(R, D)
    outer_grad = jnp.concatenate(red_outer, 0)

    s = small_grads
    return (
        output, input_grad, g_rows[0], g_rows[1], g_rows[2], out_grad, s[3], s[0], s[1],
        s[2].reshape(R, DH), s[4], s[5], s[6], inner_grad, s[10], outer_grad, s[7], s[8], s[9],
    )


def solution(mesh):
    n_dp, n_seq = mesh.devices.shape
    mesh = Mesh(mesh.devices.reshape(n_dp, n_seq // 2, 2), ALL)
    tok, ids = P(None, "dp", SEQ, None), P(None, "dp", SEQ)
    mat, vec = P(ALL, None), P(ALL)
    in_specs = (
        tok, ids, tok, mat, mat, mat, mat, vec, vec, vec, mat, vec, vec, vec, mat, vec, mat, vec,
        vec, vec,
    )
    out_specs = (
        tok, tok, mat, mat, mat, mat, vec, vec, vec, mat, vec, vec, vec, mat, vec, mat, vec, vec,
        vec,
    )
    return jax.shard_map(
        per_device, mesh=mesh, in_specs=in_specs, out_specs=out_specs, check_vma=False
    )
```

time: 1810 us -> 608 us (0.34)
  waiting for transfers between devices: 944 us -> 140 us
  local copies, waits for them, and re-layouts: 305 us -> 69.6 us
  blocking collectives: 175 us -> 34.2 us
  matrix products: 205 us -> 68.5 us
  Pallas kernels: 0 us -> 120 us
    unnamed x16 -> x1, waiting for transfers between devices: 424 us -> 0.02 us
    reduce_scatter x4 -> x0, waiting for transfers between devices: 407 us -> none  [the longest x1 188 us: per_device(): lax.psum_scatter(totals[13], ('dp', 'seq'), scatter_dimension=0, tiled=True)]
    dot_general x70 -> x15, matrix products: 205 us -> 68.5 us  [dot(): lax.dot_general(a, b, (((ca,), (cb,)), ((), ())), preferred_element_type=...]
    dynamic_update_slice x16 -> x3, local copies, waits for them, and re-layouts: 132 us -> 1.07 us  [per_device(): lax.dynamic_update_slice(jnp.zeros((S, v.size), F32), v.reshape(1, -1), (...]
    pallas_call x0 -> x2, Pallas kernels: none -> 120 us  [the longest x1 67.8 us: attention_backward(): pl.pallas_call(bwd_kernel, out_shape=(jax.ShapeDtypeStruct((M, L, w3), BF...]
    ppermute x0 -> x37, waiting for transfers between devices: none -> 113 us  [swap(): return lax.ppermute(x, axis, [(i, i ^ bit) for i in range(n)])]
    unnamed x2 -> x0, blocking collectives: 76 us -> none
    all_gather x3 -> x2, blocking collectives: 99.2 us -> 34.2 us  [the longest x1 32 us: per_device(): docs = lax.all_gather(segment_ids[:, 0], SEQ, axis=1, tiled=True)]
  transfers between devices with their start and end apart: 29 -> 45, of which waited for: 19 -> 17; matrix products, arithmetic and copies ran while one was open for 23% -> 27% of each run, Pallas kernels for 0% -> 20%
where the time goes in v1:
time: 608 us; the launch traced here: 597 us
  waiting for transfers between devices  140 us (23%)
  Pallas kernels  120 us (20%)
  other arithmetic  84.1 us (14%)
  local copies, waits for them, and re-layouts  69.6 us (11%)
  matrix products  68.5 us (11%)
  starting transfers between devices  65.2 us (11%)
  blocking collectives  34.2 us (6%)
  between operations  15.9 us (3%)
    ppermute x37, waiting for transfers between devices, swap(): return lax.ppermute(x, axis, [(i, i ^ bit) for i in range(n)])  113 us
    dot_general x15, matrix products, dot(): lax.dot_general(a, b, (((ca,), (cb,)), ((), ())), preferred_element_type=...  68.5 us
    pallas_call x1, Pallas kernels, attention_backward(): pl.pallas_call(bwd_kernel, out_shape=(jax.ShapeDtypeStruct((M, L, w3), BF...  67.8 us
    pallas_call x1, Pallas kernels, attention_forward(): pl.pallas_call(fwd_kernel, out_shape=(jax.ShapeDtypeStruct((M, L, width),...  52.1 us
    ppermute x37, starting transfers between devices, swap(): return lax.ppermute(x, axis, [(i, i ^ bit) for i in range(n)])  38.4 us
    all_gather x1, blocking collectives, per_device(): docs = lax.all_gather(segment_ids[:, 0], SEQ, axis=1, tiled=True)  32 us
    convert_element_type x19, other arithmetic, halve(): send = sum((lax.dynamic_index_in_dim(t, 1 - mine, dim, keepdims=False).as...  29.8 us
    unnamed x152, local copies, waits for them, and re-layouts  19.2 us
  transfers between devices with their start and end apart: 45, of which 17 were waited for; matrix products, arithmetic and copies ran while one was open for 27% of the time, Pallas kernels for 20%

profile of v1, /device:TPU:0, one launch (start us, length us, event | category | flops | bytes accessed | tf_op | source)
XLA Modules:
  0.0 597.5 jit_solution(17704513669906236605)
XLA Ops:
  10.0 3.6 all-to-all-start.2
  19.1 4.2 all-to-all-start
  25.5 32.0 %all-gather = s32[2,1,1024]{2,1,0:T(1,128)S(1)} all-gather(s32[2,1,256]{2,1,0:T(1,128)S(1)} %copy-done.51), channel_id=2, replica_groups=mesh['dp'=8,'yy'=2,'core'=2] {'yy','core'}, dimensions={2}, use_global_device_ids=true | all-gather | bytes 10240 | tf_op jit(solution)/shard_map/all_gather | solution.py:426
  58.2 3.1 collective-permute-start.2
  61.3 3.0 fusion.71
  64.3 23.7 %collective-permute-done.2 = bf16[4,36,768]{2,1,0:T(8,128)(2,1)S(1)} collective-permute-done((bf16[4,36,768]{2,1,0:T(8,128)(2,1)S(1)}, bf16[4,36,768]{2,1,0:T(8,128)(2,1)S(1)}, u32[]{:S(2)}, u32[]{:S(2)}) %collective-permute-start.2) | collective-permute-done | bytes 221216 | tf_op jit(solution)/shard_map/ppermute | solution.py:46
  89.3 16.6 %collective-permute-done.3 = bf16[2,4,36,768]{3,2,1,0:T(8,128)(2,1)S(1)} collective-permute-done((bf16[2,4,36,768]{3,2,1,0:T(8,128)(2,1)S(1)}, bf16[2,4,36,768]{3,2,1,0:T(8,128)(2,1)S(1)}, u32[]{:S(2)}, u32[]{:S(2)}) %collective-permute-start.3) | collective-permute-done | bytes 442400 | tf_op jit(solution)/shard_map/ppermute | solution.py:46
  112.1 3.2 pad_maximum_fusion.11
  115.3 33.3 %collective-permute-done.4 = bf16[2,2,4,36,768]{4,2,3,1,0:T(4,128)(2,1)} collective-permute-done((bf16[2,2,4,36,768]{4,2,3,1,0:T(4,128)(2,1)}, bf16[2,2,4,36,768]{4,2,3,1,0:T(4,128)(2,1)}, u32[]{:S(2)}, u32[]{:S(2)}) %collective-permute-start.4) | collective-permute-done | bytes 884768 | tf_op jit(solution)/shard_map/ppermute | solution.py:46
  154.7 2.8 copy.369
  161.0 3.6 convolution_convert_fusion.2
  165.0 52.1 %attend.1 = (bf16[2,1024,256]{2,1,0:T(8,128)(2,1)S(1)}, f32[2,1024,256]{2,1,0:T(8,128)S(1)}, f32[2,1024,256]{2,1,0:T(8,128)S(1)}) custom-call(s32[16]{0:T(128)S(1)} %reshape.825.lohi, bf16[2,1024,768]{2,1,0:T(8,128)(2,1)S(1)} %bitcast.461, bf16[2,1024,768]{2,1,0:T(8,128)(2,1)S(1)} %bitcast.462, bf16[2,1024,768]{2,1,0:T(8,128)(2,1)S(1)} %bitcast.463, ...), custom_call_target="tpu_custom_call" | custom-call | tf_op jit(solution)/shard_map/attend/pallas_call | solution.py:287
  220.9 3.7 all-to-all-start.1
  224.8 14.2 %all-to-all-done.1 = bf16[2,4,256,256]{3,2,0,1:T(8,128)(2,1)S(1)} async-done(((bf16[2,4,256,256]{3,2,0,1:T(8,128)(2,1)}), bf16[2,4,256,256]{3,2,0,1:T(8,128)(2,1)S(1)}, u32[]{:S(2)}, u32[]{:S(2)}) %all-to-all-start.1) | async-done | bytes 1048608 | tf_op jit(solution)/shard_map/all_to_all | solution.py:454
  241.1 3.3 fusion.102
  248.0 10.1 %multiply_convert_fusion = (bf16[1024,2048]{1,0:T(8,128)(2,1)S(1)}, f32[1024,2048]{1,0:T(8,128)}) fusion(f32[2048]{0:T(1024)S(1)} %reshape.887, bf16[1024,5120]{1,0:T(8,128)(2,1)} %all-gather.3.cloned.1.call-done, bf16[512,1024]{1,0:T(8,128)(2,1)} %collective-permute-done.5, bf16[512,1024]{1,0:T(8,128)(2,1)S(1)} %fusion.36), kind=kOutput, calls=%fused_computation.11 | convolution fusion | flops 4320133120 | bytes 18882560 | tf_op jit(solution)/shard_map/dot_general | solution.py:22
  258.1 5.4 fusion.28
  263.6 3.9 convolution_add_fusion
  272.6 2.7 fusion.94
  282.2 2.7 collective-permute-done.7
  284.9 4.7 convolution_convert_fusion.4
  291.8 4.2 convolution_convert_fusion.3
  298.7 4.3 fusion.26
  303.0 4.1 fusion.21
  307.2 6.2 %convert_reduce_fusion = (bf16[2048]{0:T(1024)(128)(2,1)S(1)}, bf16[1024,2048]{1,0:T(8,128)(2,1)S(1)}) fusion(f32[1024,2048]{1,0:T(8,128)S(1)} %bitcast.478, f32[2048]{0:T(1024)S(1)} %reshape.887, f32[1024,1024]{1,0:T(8,128)S(1)} %fusion.21, f32[1024,1024]{1,0:T(8,128)S(1)} %fusion.26), kind=kLoop, calls=%fused_computation.10 | loop fusion | flops 50329600 | bytes 20983808 | tf_op jit(solution)/shard_map/reduce_sum | solution.py:511
  313.4 6.6 %convolution_convert_fusion.1 = bf16[1024,2048]{1,0:T(8,128)(2,1)S(1)} fusion(bf16[1024,2048]{1,0:T(8,128)(2,1)S(1)} %get-tuple-element.174, bf16[512,1024]{1,0:T(8,128)(2,1)} %collective-permute-done.5, bf16[512,1024]{1,0:T(8,128)(2,1)S(1)} %copy-done.41), kind=kOutput, calls=%fused_computation.14 | convolution fusion | flops 4301258752 | bytes 10485760 | tf_op jit(solution)/shard_map/dot_general | solution.py:22
  324.8 4.5 fusion.7
  339.1 9.0 %collective-permute-done.21 = bf16[2,2,2,64,1024]{4,3,2,1,0:T(8,128)(2,1)} collective-permute-done((bf16[2,2,2,64,1024]{4,3,2,1,0:T(8,128)(2,1)}, bf16[2,2,2,64,1024]{4,3,2,1,0:T(8,128)(2,1)}, u32[]{:S(2)}, u32[]{:S(2)}) %collective-permute-start.21) | collective-permute-done | bytes 1048608 | tf_op jit(solution)/shard_map/ppermute | solution.py:46
  358.1 3.8 fusion.103
  363.8 4.5 all-to-all-start.3
  389.8 67.8 %attend_back.1 = (bf16[2,1024,768]{2,1,0:T(8,128)(2,1)S(1)}, f32[2,2,2,8,128]{4,3,2,1,0:T(8,128)S(1)}, f32[2,2,2,128,256]{4,3,2,1,0:T(8,128)S(1)}) custom-call(s32[16]{0:T(128)S(1)} %reshape.825.lohi, bf16[2,1024,768]{2,1,0:T(8,128)(2,1)} %bitcast.464, bf16[2,1024,768]{2,1,0:T(8,128)(2,1)} %bitcast.465, bf16[2,1024,768]{2,1,0:T(8,128)(2,1)} %bitcast.466, ...), custom_call_target="tpu_custom_call" | custom-call | tf_op jit(solution)/shard_map/attend_back/pallas_call | solution.py:321
  457.6 3.5 convolution_convert_fusion.6
  461.2 5.1 convolution_convert_fusion
  470.1 2.9 collective-permute-start.36
  475.1 3.1 copy_bitcast_fusion
  481.8 2.9 collective-permute-start.28
  484.7 6.2 %collective-permute-done.24 = bf16[64,1024]{1,0:T(8,128)(2,1)} collective-permute-done((bf16[64,1024]{1,0:T(8,128)(2,1)}, bf16[64,1024]{1,0:T(8,128)(2,1)}, u32[]{:S(2)}, u32[]{:S(2)}) %collective-permute-start.24) | collective-permute-done | bytes 131104 | tf_op jit(solution)/shard_map/ppermute | solution.py:46
  506.5 4.1 all-to-all-start.6
  521.6 2.9 copy.412
  524.4 3.0 reshape.951
  534.1 4.2 collective-permute-done.19
  541.0 4.2 collective-permute-done.20
  546.8 3.3 all-to-all-start.5
  553.3 2.9 fusion.19
  558.4 5.4 collective-permute-done.15
  565.8 3.4 all-to-all-start.4
  570.9 12.9 %all-to-all-done.4 = bf16[4,32,3,256]{3,1,2,0:T(8,128)(2,1)S(1)} async-done(((bf16[4,32,3,256]{3,1,2,0:T(8,128)(2,1)}), bf16[4,32,3,256]{3,1,2,0:T(8,128)(2,1)S(1)}, u32[]{:S(2)}, u32[]{:S(2)}) %all-to-all-start.4) | async-done | bytes 196640 | tf_op jit(solution)/shard_map/all_to_all | solution.py:542
  586.2 2.6 fusion.20
  (433 shorter events, 161.8 us)
Async XLA Ops:
  10.0 5.9 all-to-all-start.2
  13.6 227.5 %all-gather.3.cloned.1.call-start = ((), (), s32[]{:S(2)}) async-start(), calls=%async_computation.7 | async-start | bytes 11141120 | tf_op jit(solution)/shard_map/all_gather | solution.py:414
  19.1 39.1 %all-to-all-start = ((bf16[4,36,768]{2,1,0:T(8,128)(2,1)}), bf16[4,36,768]{2,1,0:T(8,128)(2,1)S(1)}, u32[]{:S(2)}, u32[]{:S(2)}) async-start(bf16[4,36,768]{2,1,0:T(8,128)(2,1)} %pad_maximum_fusion.15), calls=%async_computation | async-start | bytes 491520 | tf_op jit(solution)/shard_map/all_to_all | solution.py:390
  23.3 85.4 %collective-permute-start = (bf16[2,256,1024]{2,1,0:T(8,128)(2,1)S(1)}, bf16[2,256,1024]{2,1,0:T(8,128)(2,1)}, u32[]{:S(2)}, u32[]{:S(2)}) collective-permute-start(bf16[2,256,1024]{2,1,0:T(8,128)(2,1)S(1)} %bitcast.522), channel_id=1, source_target_pairs={{0,2},{2,0},{1,3},{3,1},{4,6},{6,4},{5,7},{7,5},{8,10},{10,8},{9,1... | collective-permute-start | bytes 3145736 | tf_op jit(solution)/shard_map/ppermute | solution.py:46
  58.2 29.9 %collective-permute-start.2 = (bf16[4,36,768]{2,1,0:T(8,128)(2,1)S(1)}, bf16[4,36,768]{2,1,0:T(8,128)(2,1)S(1)}, u32[]{:S(2)}, u32[]{:S(2)}) collective-permute-start(bf16[4,36,768]{2,1,0:T(8,128)(2,1)S(1)} %all-to-all-done), channel_id=1, source_target_pairs={{0,16},{4,20},{8,24},{12,28},{16,0},{20,4},{24,8},{28,12},{1,17},{... | collective-permute-start | bytes 663560 | tf_op jit(solution)/shard_map/ppermute | solution.py:46
  88.2 17.7 %collective-permute-start.3 = (bf16[2,4,36,768]{3,2,1,0:T(8,128)(2,1)S(1)}, bf16[2,4,36,768]{3,2,1,0:T(8,128)(2,1)S(1)}, u32[]{:S(2)}, u32[]{:S(2)}) collective-permute-start(bf16[2,4,36,768]{3,2,1,0:T(8,128)(2,1)S(1)} %pad_maximum_fusion.13), channel_id=1, source_target_pairs={{0,8},{4,12},{8,0},{12,4},{16,24},{20,28},{24,16},{28,20},{1,9},{5... | collective-permute-start | bytes 1327112 | tf_op jit(solution)/shard_map/ppermute | solution.py:46
  107.3 41.3 %collective-permute-start.4 = (bf16[2,2,4,36,768]{4,2,3,1,0:T(4,128)(2,1)}, bf16[2,2,4,36,768]{4,2,3,1,0:T(4,128)(2,1)}, u32[]{:S(2)}, u32[]{:S(2)}) collective-permute-start(bf16[2,2,4,36,768]{4,2,3,1,0:T(4,128)(2,1)} %copy.365), channel_id=1, source_target_pairs={{0,4},{4,0},{8,12},{12,8},{16,20},{20,16},{24,28},{28,24},{1,5},{5... | collective-permute-start | bytes 2654216 | tf_op jit(solution)/shard_map/ppermute | solution.py:46
  111.9 45.7 %collective-permute-start.1 = (bf16[2,2,256,1024]{3,2,1,0:T(8,128)(2,1)}, bf16[2,2,256,1024]{3,2,1,0:T(8,128)(2,1)}, u32[]{:S(2)}, u32[]{:S(2)}) collective-permute-start(bf16[2,2,256,1024]{3,2,1,0:T(8,128)(2,1)} %pad_maximum_fusion.2), channel_id=1, source_target_pairs={{0,1},{1,0},{2,3},{3,2},{4,5},{5,4},{6,7},{7,6},{8,9},{9,8},{10,11... | collective-permute-start | bytes 6291464 | tf_op jit(solution)/shard_map/ppermute | solution.py:46
  164.6 52.5 %copy-start = (bf16[2048,768]{1,0:T(8,128)(2,1)}, bf16[2048,768]{1,0:T(8,128)(2,1)S(1)}, u32[]{:S(2)}) copy-start(bf16[2048,768]{1,0:T(8,128)(2,1)S(1)} %convolution_convert_fusion.2) | copy-start | bytes 9437188
  165.0 52.2 %copy-start.1 = (s32[2,1024,128]{2,1,0:T(8,128)}, s32[2,1024,128]{2,1,0:T(8,128)S(1)}, u32[]{:S(2)}) copy-start(s32[2,1024,128]{2,1,0:T(8,128)S(1)} %broadcast_in_dim.83.segc_ref) | copy-start | bytes 3145732
  220.9 18.1 %all-to-all-start.1 = ((bf16[2,4,256,256]{3,2,0,1:T(8,128)(2,1)}), bf16[2,4,256,256]{3,2,0,1:T(8,128)(2,1)S(1)}, u32[]{:S(2)}, u32[]{:S(2)}) async-start(bf16[2,4,256,256]{3,2,0,1:T(8,128)(2,1)} %copy.376), calls=%async_computation.1 | async-start | bytes 2097152 | tf_op jit(solution)/shard_map/all_to_all | solution.py:454
  245.1 2.9 collective-permute-start.5
  269.7 2.9 collective-permute-start.6
  281.9 3.0 collective-permute-start.7
  291.4 41.1 %collective-permute-start.29 = (bf16[2,2,2,64,1024]{4,3,2,1,0:T(8,128)(2,1)}, bf16[2,2,2,64,1024]{4,3,2,1,0:T(8,128)(2,1)}, u32[]{:S(2)}, u32[]{:S(2)}) collective-permute-start(bf16[2,2,2,64,1024]{4,3,2,1,0:T(8,128)(2,1)} %dynamic-slice_bitcast_fusion.1), channel_id=1, source_target_pairs={{0,2},{2,0},{1,3},{3,1},{4,6},{6,4},{5,7},{7,5},{8,10},{10,8},{9,1... | collective-permute-start | bytes 3145736 | tf_op jit(solution)/shard_map/ppermute | solution.py:46
  297.2 39.1 %collective-permute-start.33 = (bf16[2,2,2,64,1024]{4,3,2,1,0:T(8,128)(2,1)}, bf16[2,2,2,64,1024]{4,3,2,1,0:T(8,128)(2,1)}, u32[]{:S(2)}, u32[]{:S(2)}) collective-permute-start(bf16[2,2,2,64,1024]{4,3,2,1,0:T(8,128)(2,1)} %dynamic-slice_bitcast_fusion), channel_id=1, source_target_pairs={{0,4},{4,0},{8,12},{12,8},{16,20},{20,16},{24,28},{28,24},{1,5},{5... | collective-permute-start | bytes 3145736 | tf_op jit(solution)/shard_map/ppermute | solution.py:46
  321.7 26.4 %collective-permute-start.21 = (bf16[2,2,2,64,1024]{4,3,2,1,0:T(8,128)(2,1)}, bf16[2,2,2,64,1024]{4,3,2,1,0:T(8,128)(2,1)}, u32[]{:S(2)}, u32[]{:S(2)}) collective-permute-start(bf16[2,2,2,64,1024]{4,3,2,1,0:T(8,128)(2,1)} %dynamic-slice_bitcast_fusion.3), channel_id=1, source_target_pairs={{0,2},{2,0},{1,3},{3,1},{4,6},{6,4},{5,7},{7,5},{8,10},{10,8},{9,1... | collective-permute-start | bytes 3145736 | tf_op jit(solution)/shard_map/ppermute | solution.py:46
  324.2 26.6 %collective-permute-start.25 = (bf16[2,2,2,64,1024]{4,3,2,1,0:T(8,128)(2,1)}, bf16[2,2,2,64,1024]{4,3,2,1,0:T(8,128)(2,1)}, u32[]{:S(2)}, u32[]{:S(2)}) collective-permute-start(bf16[2,2,2,64,1024]{4,3,2,1,0:T(8,128)(2,1)} %dynamic-slice_bitcast_fusion.2), channel_id=1, source_target_pairs={{0,4},{4,0},{8,12},{12,8},{16,20},{20,16},{24,28},{28,24},{1,5},{5... | collective-permute-start | bytes 3145736 | tf_op jit(solution)/shard_map/ppermute | solution.py:46
  331.7 22.9 %collective-permute-start.8 = (bf16[512,1024]{1,0:T(8,128)(2,1)}, bf16[512,1024]{1,0:T(8,128)(2,1)}, u32[]{:S(2)}, u32[]{:S(2)}) collective-permute-start(bf16[512,1024]{1,0:T(8,128)(2,1)} %slice.346), channel_id=1, source_target_pairs={{0,1},{1,0},{2,3},{3,2},{4,5},{5,4},{6,7},{7,6},{8,9},{9,8},{10,11... | collective-permute-start | bytes 3145736 | tf_op jit(solution)/shard_map/ppermute | solution.py:46
  334.7 38.6 %collective-permute-start.30 = (bf16[2,2,64,1024]{3,2,1,0:T(8,128)(2,1)}, bf16[2,2,64,1024]{3,2,1,0:T(8,128)(2,1)}, u32[]{:S(2)}, u32[]{:S(2)}) collective-permute-start(bf16[2,2,64,1024]{3,2,1,0:T(8,128)(2,1)} %fusion.43), channel_id=1, source_target_pairs={{0,4},{4,0},{8,12},{12,8},{16,20},{20,16},{24,28},{28,24},{1,5},{5... | collective-permute-start | bytes 1572872 | tf_op jit(solution)/shard_map/ppermute | solution.py:46
  338.6 36.9 %collective-permute-start.34 = (bf16[2,2,64,1024]{3,2,1,0:T(8,128)(2,1)}, bf16[2,2,64,1024]{3,2,1,0:T(8,128)(2,1)}, u32[]{:S(2)}, u32[]{:S(2)}) collective-permute-start(bf16[2,2,64,1024]{3,2,1,0:T(8,128)(2,1)} %fusion.42), channel_id=1, source_target_pairs={{0,2},{2,0},{1,3},{3,1},{4,6},{6,4},{5,7},{7,5},{8,10},{10,8},{9,1... | collective-permute-start | bytes 1572872 | tf_op jit(solution)/shard_map/ppermute | solution.py:46
  350.4 29.0 %collective-permute-start.22 = (bf16[2,2,64,1024]{3,2,0,1:T(8,128)(2,1)}, bf16[2,2,64,1024]{3,2,0,1:T(8,128)(2,1)}, u32[]{:S(2)}, u32[]{:S(2)}) collective-permute-start(bf16[2,2,64,1024]{3,2,0,1:T(8,128)(2,1)} %copy.407), channel_id=1, source_target_pairs={{0,4},{4,0},{8,12},{12,8},{16,20},{20,16},{24,28},{28,24},{1,5},{5... | collective-permute-start | bytes 1572872 | tf_op jit(solution)/shard_map/ppermute | solution.py:46
  353.1 28.5 %collective-permute-start.26 = (bf16[2,2,64,1024]{3,2,0,1:T(8,128)(2,1)}, bf16[2,2,64,1024]{3,2,0,1:T(8,128)(2,1)}, u32[]{:S(2)}, u32[]{:S(2)}) collective-permute-start(bf16[2,2,64,1024]{3,2,0,1:T(8,128)(2,1)} %copy.410), channel_id=1, source_target_pairs={{0,2},{2,0},{1,3},{3,1},{4,6},{6,4},{5,7},{7,5},{8,10},{10,8},{9,1... | collective-permute-start | bytes 1572872 | tf_op jit(solution)/shard_map/ppermute | solution.py:46
  363.8 21.5 %all-to-all-start.3 = ((bf16[2,4,256,256]{3,2,0,1:T(8,128)(2,1)}), bf16[2,4,256,256]{3,2,0,1:T(8,128)(2,1)}, u32[]{:S(2)}, u32[]{:S(2)}) async-start(bf16[2,4,256,256]{3,2,0,1:T(8,128)(2,1)} %bitcast.457), calls=%async_computation.3 | async-start | bytes 2097152 | tf_op jit(solution)/shard_map/all_to_all | solution.py:490
  371.2 126.1 %collective-permute-start.16 = (bf16[1024,512]{1,0:T(8,128)(2,1)}, bf16[1024,512]{1,0:T(8,128)(2,1)}, u32[]{:S(2)}, u32[]{:S(2)}) collective-permute-start(bf16[1024,512]{1,0:T(8,128)(2,1)} %bitcast.527), channel_id=1, source_target_pairs={{0,1},{1,0},{2,3},{3,2},{4,5},{5,4},{6,7},{7,6},{8,9},{9,8},{10,11... | collective-permute-start | bytes 3145736 | tf_op jit(solution)/shard_map/ppermute | solution.py:46
  375.3 91.0 %collective-permute-start.31 = (bf16[2,64,1024]{2,1,0:T(8,128)(2,1)}, bf16[2,64,1024]{2,1,0:T(8,128)(2,1)}, u32[]{:S(2)}, u32[]{:S(2)}) collective-permute-start(bf16[2,64,1024]{2,1,0:T(8,128)(2,1)} %fusion.49), channel_id=1, source_target_pairs={{0,8},{4,12},{8,0},{12,4},{16,24},{20,28},{24,16},{28,20},{1,9},{5... | collective-permute-start | bytes 786440 | tf_op jit(solution)/shard_map/ppermute | solution.py:46
  377.4 90.8 %collective-permute-start.35 = (bf16[2,64,1024]{2,1,0:T(8,128)(2,1)}, bf16[2,64,1024]{2,1,0:T(8,128)(2,1)}, u32[]{:S(2)}, u32[]{:S(2)}) collective-permute-start(bf16[2,64,1024]{2,1,0:T(8,128)(2,1)} %fusion.48), channel_id=1, source_target_pairs={{0,8},{4,12},{8,0},{12,4},{16,24},{20,28},{24,16},{28,20},{1,9},{5... | collective-permute-start | bytes 786440 | tf_op jit(solution)/shard_map/ppermute | solution.py:46
  381.3 91.7 %collective-permute-start.23 = (bf16[2,64,1024]{2,1,0:T(8,128)(2,1)}, bf16[2,64,1024]{2,1,0:T(8,128)(2,1)}, u32[]{:S(2)}, u32[]{:S(2)}) collective-permute-start(bf16[2,64,1024]{2,1,0:T(8,128)(2,1)} %fusion.51), channel_id=1, source_target_pairs={{0,8},{4,12},{8,0},{12,4},{16,24},{20,28},{24,16},{28,20},{1,9},{5... | collective-permute-start | bytes 786440 | tf_op jit(solution)/shard_map/ppermute | solution.py:46
  383.5 96.9 %collective-permute-start.27 = (bf16[2,64,1024]{2,1,0:T(8,128)(2,1)}, bf16[2,64,1024]{2,1,0:T(8,128)(2,1)}, u32[]{:S(2)}, u32[]{:S(2)}) collective-permute-start(bf16[2,64,1024]{2,1,0:T(8,128)(2,1)} %fusion.50), channel_id=1, source_target_pairs={{0,8},{4,12},{8,0},{12,4},{16,24},{20,28},{24,16},{28,20},{1,9},{5... | collective-permute-start | bytes 786440 | tf_op jit(solution)/shard_map/ppermute | solution.py:46
  389.8 67.8 %copy-start.26 = (bf16[2,2,2,256,1024]{4,3,2,1,0:T(8,128)(2,1)S(1)}, bf16[2,2,2,256,1024]{4,3,2,1,0:T(8,128)(2,1)}, u32[]{:S(2)}) copy-start(bf16[2,2,2,256,1024]{4,3,2,1,0:T(8,128)(2,1)} %copy-done.25) | copy-start | bytes 12582916
  468.2 42.4 %collective-permute-start.32 = (bf16[64,1024]{1,0:T(8,128)(2,1)}, bf16[64,1024]{1,0:T(8,128)(2,1)}, u32[]{:S(2)}, u32[]{:S(2)}) collective-permute-start(bf16[64,1024]{1,0:T(8,128)(2,1)} %fusion.60), channel_id=1, source_target_pairs={{0,16},{4,20},{8,24},{12,28},{16,0},{20,4},{24,8},{28,12},{1,17},{... | collective-permute-start | bytes 393224 | tf_op jit(solution)/shard_map/ppermute | solution.py:46
  470.1 47.2 %collective-permute-start.36 = (bf16[64,1024]{1,0:T(8,128)(2,1)}, bf16[64,1024]{1,0:T(8,128)(2,1)}, u32[]{:S(2)}, u32[]{:S(2)}) collective-permute-start(bf16[64,1024]{1,0:T(8,128)(2,1)} %fusion.58), channel_id=1, source_target_pairs={{0,16},{4,20},{8,24},{12,28},{16,0},{20,4},{24,8},{28,12},{1,17},{... | collective-permute-start | bytes 393224 | tf_op jit(solution)/shard_map/ppermute | solution.py:46
  474.8 16.2 %collective-permute-start.24 = (bf16[64,1024]{1,0:T(8,128)(2,1)}, bf16[64,1024]{1,0:T(8,128)(2,1)}, u32[]{:S(2)}, u32[]{:S(2)}) collective-permute-start(bf16[64,1024]{1,0:T(8,128)(2,1)} %fusion.65), channel_id=1, source_target_pairs={{0,16},{4,20},{8,24},{12,28},{16,0},{20,4},{24,8},{28,12},{1,17},{... | collective-permute-start | bytes 393224 | tf_op jit(solution)/shard_map/ppermute | solution.py:46
  480.4 1.4 collective-permute-start.11
  481.8 11.4 %collective-permute-start.28 = (bf16[64,1024]{1,0:T(8,128)(2,1)S(1)}, bf16[64,1024]{1,0:T(8,128)(2,1)S(1)}, u32[]{:S(2)}, u32[]{:S(2)}) collective-permute-start(bf16[64,1024]{1,0:T(8,128)(2,1)S(1)} %fusion.62), channel_id=1, source_target_pairs={{0,16},{4,20},{8,24},{12,28},{16,0},{20,4},{24,8},{28,12},{1,17},{... | collective-permute-start | bytes 393224 | tf_op jit(solution)/shard_map/ppermute | solution.py:46
  491.0 62.3 %collective-permute-start.9 = (bf16[2,2,256,1024]{3,2,1,0:T(8,128)(2,1)}, bf16[2,2,256,1024]{3,2,1,0:T(8,128)(2,1)}, u32[]{:S(2)}, u32[]{:S(2)}) collective-permute-start(bf16[2,2,256,1024]{3,2,1,0:T(8,128)(2,1)} %copy_bitcast_fusion), channel_id=1, source_target_pairs={{0,1},{1,0},{2,3},{3,2},{4,5},{5,4},{6,7},{7,6},{8,9},{9,8},{10,11... | collective-permute-start | bytes 6291464 | tf_op jit(solution)/shard_map/ppermute | solution.py:46
  493.2 4.1 collective-permute-start.12
  500.7 13.2 %collective-permute-start.17 = (bf16[2,2,2,64,512]{4,3,2,1,0:T(8,128)(2,1)}, bf16[2,2,2,64,512]{4,3,2,1,0:T(8,128)(2,1)}, u32[]{:S(2)}, u32[]{:S(2)}) collective-permute-start(bf16[2,2,2,64,512]{4,3,2,1,0:T(8,128)(2,1)} %dynamic-slice_bitcast_fusion.4), channel_id=1, source_target_pairs={{0,2},{2,0},{1,3},{3,1},{4,6},{6,4},{5,7},{7,5},{8,10},{10,8},{9,1... | collective-permute-start | bytes 1572872 | tf_op jit(solution)/shard_map/ppermute | solution.py:46
  504.3 25.0 %collective-permute-start.13 = (bf16[2,2,132,768]{3,1,2,0:T(2,128)(2,1)}, bf16[2,2,132,768]{3,1,2,0:T(2,128)(2,1)S(1)}, u32[]{:S(2)}, u32[]{:S(2)}) collective-permute-start(bf16[2,2,132,768]{3,1,2,0:T(2,128)(2,1)} %bitcast.458), channel_id=1, source_target_pairs={{0,4},{4,0},{8,12},{12,8},{16,20},{20,16},{24,28},{28,24},{1,5},{5... | collective-permute-start | bytes 2433032 | tf_op jit(solution)/shard_map/ppermute | solution.py:46
  506.5 12.7 %all-to-all-start.6 = ((bf16[2,32,2048]{2,1,0:T(8,128)(2,1)}), bf16[2,32,2048]{2,1,0:T(8,128)(2,1)}, u32[]{:S(2)}, u32[]{:S(2)}) async-start(bf16[2,32,2048]{2,1,0:T(8,128)(2,1)} %pad_maximum_fusion.14), calls=%async_computation.6 | async-start | bytes 524288 | tf_op jit(solution)/shard_map/all_to_all | solution.py:568
  515.6 14.5 %collective-permute-start.18 = (bf16[2,2,64,512]{3,2,0,1:T(8,128)(2,1)}, bf16[2,2,64,512]{3,2,0,1:T(8,128)(2,1)}, u32[]{:S(2)}, u32[]{:S(2)}) collective-permute-start(bf16[2,2,64,512]{3,2,0,1:T(8,128)(2,1)} %copy.403), channel_id=1, source_target_pairs={{0,4},{4,0},{8,12},{12,8},{16,20},{20,16},{24,28},{28,24},{1,5},{5... | collective-permute-start | bytes 786440 | tf_op jit(solution)/shard_map/ppermute | solution.py:46
  531.2 7.2 %collective-permute-start.19 = (bf16[2,64,512]{2,1,0:T(8,128)(2,1)S(1)}, bf16[2,64,512]{2,1,0:T(8,128)(2,1)S(1)}, u32[]{:S(2)}, u32[]{:S(2)}) collective-permute-start(bf16[2,64,512]{2,1,0:T(8,128)(2,1)S(1)} %fusion.68), channel_id=1, source_target_pairs={{0,8},{4,12},{8,0},{12,4},{16,24},{20,28},{24,16},{28,20},{1,9},{5... | collective-permute-start | bytes 393224 | tf_op jit(solution)/shard_map/ppermute | solution.py:46
  532.1 17.9 %collective-permute-start.14 = (bf16[2,132,768]{2,1,0:T(8,128)(2,1)}, bf16[2,132,768]{2,1,0:T(8,128)(2,1)}, u32[]{:S(2)}, u32[]{:S(2)}) collective-permute-start(bf16[2,132,768]{2,1,0:T(8,128)(2,1)} %fusion.47), channel_id=1, source_target_pairs={{0,8},{4,12},{8,0},{12,4},{16,24},{20,28},{24,16},{28,20},{1,9},{5... | collective-permute-start | bytes 1216520 | tf_op jit(solution)/shard_map/ppermute | solution.py:46
  539.3 5.9 collective-permute-start.20
  546.8 11.0 %all-to-all-start.5 = ((bf16[2,32,512]{2,1,0:T(8,128)(2,1)}), bf16[2,32,512]{2,1,0:T(8,128)(2,1)S(1)}, u32[]{:S(2)}, u32[]{:S(2)}) async-start(bf16[2,32,512]{2,1,0:T(8,128)(2,1)} %bitcast.87), calls=%async_computation.5 | async-start | bytes 131072 | tf_op jit(solution)/shard_map/all_to_all | solution.py:571
  551.2 12.6 %collective-permute-start.15 = (bf16[132,768]{1,0:T(8,128)(2,1)S(1)}, bf16[132,768]{1,0:T(8,128)(2,1)S(1)}, u32[]{:S(2)}, u32[]{:S(2)}) collective-permute-start(bf16[132,768]{1,0:T(8,128)(2,1)S(1)} %fusion.56), channel_id=1, source_target_pairs={{0,16},{4,20},{8,24},{12,28},{16,0},{20,4},{24,8},{28,12},{1,17},{... | collective-permute-start | bytes 608264 | tf_op jit(solution)/shard_map/ppermute | solution.py:46
  556.2 30.0 %collective-permute-start.10 = (bf16[2,256,1024]{2,1,0:T(8,128)(2,1)}, bf16[2,256,1024]{2,1,0:T(8,128)(2,1)}, u32[]{:S(2)}, u32[]{:S(2)}) collective-permute-start(bf16[2,256,1024]{2,1,0:T(8,128)(2,1)} %fusion.19), channel_id=1, source_target_pairs={{0,2},{2,0},{1,3},{3,1},{4,6},{6,4},{5,7},{7,5},{8,10},{10,8},{9,1... | collective-permute-start | bytes 3145736 | tf_op jit(solution)/shard_map/ppermute | solution.py:46
  565.8 18.1 %all-to-all-start.4 = ((bf16[4,32,3,256]{3,1,2,0:T(8,128)(2,1)}), bf16[4,32,3,256]{3,1,2,0:T(8,128)(2,1)S(1)}, u32[]{:S(2)}, u32[]{:S(2)}) async-start(bf16[4,32,3,256]{3,1,2,0:T(8,128)(2,1)} %copy.396), calls=%async_computation.4 | async-start | bytes 393216 | tf_op jit(solution)/shard_map/all_to_all | solution.py:542
  (66 other events, 392.1 us)
Sparse Core Ops, SparseCore 0:
  17.3 168.1 all-gather.2

commit v2 on v1

v2 whole, which is shorter than its diff:
```python
import functools
import math

import jax
import jax.numpy as jnp
from jax import lax
from jax.experimental import pallas as pl
from jax.experimental.pallas import tpu as pltpu
from jax.sharding import Mesh, PartitionSpec as P

H = 16
DH = 64
BLK = 256
GRP = 2
NEG = -1e30
BF = jnp.bfloat16
F32 = jnp.float32
DP = ("dz", "dx")
SEQ = ("yy", "core")
CHIP = DP + ("yy",)
ALL = DP + SEQ


def dot(a, b, ca=1, cb=0):
    return lax.dot_general(a, b, (((ca,), (cb,)), ((), ())), preferred_element_type=F32)


def rotations(length, half_size):
    position = jnp.arange(length, dtype=jnp.int32).astype(F32)
    steps = jnp.arange(half_size, dtype=jnp.int32).astype(F32)
    frequency = jnp.exp(steps * (-math.log(10000.0) / half_size))
    angle = position[:, None] * frequency[None, :]
    return (jnp.cos(angle), jnp.sin(angle))


def layer_norm(values, gain, shift):
    average = jnp.mean(values, axis=-1, keepdims=True)
    centred = values - average
    variance = jnp.mean(centred * centred, axis=-1, keepdims=True)
    return centred * lax.rsqrt(variance + 1e-06) * gain + shift


def gelu_tanh(values):
    return jax.nn.gelu(values, approximate=True)


def swap(x, axis, bit):
    n = lax.axis_size(axis)
    return lax.ppermute(x, axis, [(i, i ^ bit) for i in range(n)])


def side(axis, bit):
    return jnp.where((lax.axis_index(axis) & bit) != 0, 1, 0)


def double(x, axis, bit, dim, other=None):
    other = swap(x, axis, bit) if other is None else other
    mine = side(axis, bit) == 0
    return jnp.stack([jnp.where(mine, x, other), jnp.where(mine, other, x)], dim)


def bits_of(axis):
    n = lax.axis_size(axis)
    return [1 << k for k in reversed(range(n.bit_length() - 1))]


def gather_bits(x, axis, dim=0, wait=None):
    bits = bits_of(axis)
    for k, bit in enumerate(bits):
        x = double(x, axis, bit, dim + k)
        if wait is not None and k == 0:
            behind = tuple(wait)
            wait.append(x)
            x = after(x, *behind)
    return x.reshape(x.shape[:dim] + (lax.axis_size(axis),) + x.shape[dim + len(bits) :])


def total(terms):
    return sum(t.astype(F32) for t in terms)


class Chain:
    def __init__(self, terms, left):
        self.terms, self.left, self.sends = terms, list(left), []

    def send(self, step):
        axis, bit = step
        dim = self.left.index(step)
        self.left.pop(dim)
        mine = side(axis, bit)
        take = lambda t, k: lax.dynamic_index_in_dim(t, k, dim, keepdims=False)
        out = total([take(t, 1 - mine) for t in self.terms]).astype(BF)
        self.terms = [take(t, mine) for t in self.terms]
        self.sends.append(out)
        return out

    def run(self, steps):
        for step in steps:
            got = swap(self.send(step), *step)
            self.terms.append(got)
        return self

    def result(self):
        return total(self.terms)


def run_together(chains, steps):
    sends = []
    for step in steps:
        parts = [c.send(step) for c in chains]
        sends.append(jnp.concatenate(parts, -1))
        got, at = swap(sends[-1], *step), 0
        for c, part in zip(chains, parts):
            c.terms.append(got[..., at : at + part.shape[-1]])
            at += part.shape[-1]
    return sends


def after(x, *others):
    return lax.optimization_barrier((x,) + others)[0]


def meet(x, *chains):
    x, last = lax.optimization_barrier((x, [c.terms[-1] for c in chains]))
    for c, t in zip(chains, last):
        c.terms[-1] = t
    return x


def tables(tab):
    lane = lax.broadcasted_iota(jnp.int32, tab.shape, 1)
    turned = pltpu.roll(tab, DH, 1)
    cos = jnp.where(lane < DH, 0.0, tab)
    sin = jnp.where(lane < DH, 0.0, turned)
    return cos, sin, jnp.where(lane < DH + DH // 2, tab, turned)


def prep_head(e, q, qr, k, kr, first, bias, mat, cos, sin, pk):
    base = jnp.where(first, q, qr) if e == 0 else jnp.where(first, qr, q)
    both = (base + bias).astype(BF)
    turned = dot(both, mat)
    rel = turned[:, :128] * cos + turned[:, 128:] * sin
    qf = (jnp.where(first, both.astype(F32), rel) * (DH**-0.5)).astype(BF)
    kf = jnp.where(first, k if e == 0 else kr, pk).astype(BF)
    return both, qf, kf


def row_of(ref, start, width):
    return jnp.concatenate([ref[0, start + t] for t in range(width // 128)], 1)


def seg_columns(segr_ref, seg_s, i):
    for t in range(i * (BLK // 128), (i + 1) * (BLK // 128)):
        tile = jnp.broadcast_to(segr_ref[0, t], (128, 128)).T
        seg_s[t * 128 : (t + 1) * 128, :] = tile


def by_width(n, most, body):
    for k in range(1, most + 1):

        @pl.when(n == k)
        def _(k=k):
            body(k * BLK)


def fwd_kernel(
    lohi, q_ref, k_ref, v_ref, segr_ref, tab_ref, bias_ref, mat_ref, vb_ref,
    ctx_ref, o_ref, lse_ref, qf_s, kf_s, seg_s,
):
    m = pl.program_id(0)
    nb = q_ref.shape[1] // BLK
    first = lax.broadcasted_iota(jnp.int32, (BLK, 128), 1) < DH

    def prep(i):
        rows = slice(i * BLK, (i + 1) * BLK)
        seg_columns(segr_ref, seg_s, i)
        q = q_ref[0, rows, :].astype(F32)
        k = k_ref[0, rows, :].astype(F32)
        qr, kr = pltpu.roll(q, DH, 1), pltpu.roll(k, DH, 1)
        cos, sin, pk = tables(tab_ref[rows, :])
        for e in range(2):
            _, qf, kf = prep_head(
                e, q, qr, k, kr, first, bias_ref[0, e : e + 1, :], mat_ref[0, e],
                cos, sin, pk,
            )
            qf_s[e, rows, :] = qf
            kf_s[e, rows, :] = kf

    for i in range(nb):
        prep(i)

    def q_group(i, c):
        at = (m * nb + i * GRP) * 2
        starts = [lohi[at + 2 * u] for u in range(GRP)]
        n = lohi[at + 1]
        for u in range(1, GRP):
            n = jnp.maximum(n, lohi[at + 2 * u + 1])

        def body(width):
            for u in range(GRP):
                rows = pl.ds(pl.multiple_of((i * GRP + u) * BLK, BLK), BLK)
                start = jnp.minimum(starts[u], (nb * BLK - width) // 128)
                cols = pl.ds(pl.multiple_of(start * 128, 128), width)
                segq = jnp.concatenate([seg_s[rows, :]] * (width // 128), 1)
                same = segq == row_of(segr_ref, start, width)
                outs = []
                for e in range(2):
                    s = dot(qf_s[e, rows, :], kf_s[e, cols, :], 1, 1)
                    s = jnp.where(same, s, NEG)
                    top = jnp.max(s, axis=1, keepdims=True)
                    p = jnp.exp(s - top)
                    total = jnp.sum(p, axis=1, keepdims=True)
                    acc = dot(p.astype(BF), v_ref[0, cols, :])
                    outs.append((acc / total, top + jnp.log(total)))
                o = jnp.where(first, outs[0][0], outs[1][0])
                o_ref[0, rows, :] = o.astype(BF)
                lse_t = jnp.where(first, outs[0][1], outs[1][1]).T
                for e in range(2):
                    for t in range(BLK // 128):
                        lse_ref[0, 0, e, (i * GRP + u) * (BLK // 128) + t] = lse_t[
                            e * DH : e * DH + 1, t * 128 : t * 128 + 128
                        ]
                ctx_ref[0, rows, :] = (o + vb_ref[0]).astype(BF)

        by_width(n, nb, body)
        return c

    lax.fori_loop(0, nb // GRP, q_group, 0)


def bwd_kernel(
    m, lohi, q_ref, k_ref, v_ref, g_ref, o_ref, lse_ref, segr_ref, tab_ref, bias_ref,
    mat_ref, *refs,
):
    gqkv_ref, gsm_ref, gpp_ref, both_s, qf_s, kf_s, seg_s, dl_s, gq_s, res_s = refs[-10:]
    p = pl.program_id(0)
    nb = q_ref.shape[1] // BLK
    width3 = gqkv_ref.shape[2] // 3
    first = lax.broadcasted_iota(jnp.int32, (BLK, 128), 1) < DH

    def prep(i):
        rows = slice(i * BLK, (i + 1) * BLK)
        seg_columns(segr_ref, seg_s, i)
        q = q_ref[0, rows, :].astype(F32)
        k = k_ref[0, rows, :].astype(F32)
        qr, kr = pltpu.roll(q, DH, 1), pltpu.roll(k, DH, 1)
        cos, sin, pk = tables(tab_ref[rows, :])
        dl_t = (g_ref[0, rows, :].astype(F32) * o_ref[0, rows, :].astype(F32)).T
        for e in range(2):
            both, qf, kf = prep_head(
                e, q, qr, k, kr, first, bias_ref[0, e : e + 1, :], mat_ref[0, e],
                cos, sin, pk,
            )
            both_s[e, rows, :] = both
            qf_s[e, rows, :] = qf
            kf_s[e, rows, :] = kf
            gq_s[e, rows, :] = jnp.zeros((BLK, 128), F32)
            dl = jnp.sum(dl_t[e * DH : (e + 1) * DH, :], axis=0, keepdims=True)
            for t in range(BLK // 128):
                dl_s[e, i * (BLK // 128) + t] = dl[:, t * 128 : t * 128 + 128]

    for i in range(nb):
        prep(i)

    def k_group(j, c):
        at = (m * nb + j * GRP) * 2
        starts = [lohi[at + 2 * u] for u in range(GRP)]
        n = lohi[at + 1]
        for u in range(1, GRP):
            n = jnp.maximum(n, lohi[at + 2 * u + 1])

        def body(width):
            for u in range(GRP):
                rows = pl.ds(pl.multiple_of((j * GRP + u) * BLK, BLK), BLK)
                start = jnp.minimum(starts[u], (nb * BLK - width) // 128)
                cols = pl.ds(pl.multiple_of(start * 128, 128), width)
                segk = jnp.concatenate([seg_s[rows, :]] * (width // 128), 1)
                same = segk == row_of(segr_ref, start, width)
                g = g_ref[0, cols, :]
                v = v_ref[0, rows, :].astype(F32)
                outs = []
                for e in range(2):
                    row = lambda ref: jnp.concatenate(
                        [ref[e, start + t] for t in range(width // 128)], 1
                    )
                    mine = first if e == 0 else jnp.logical_not(first)
                    vm = jnp.where(mine, v, 0.0).astype(BF)
                    kf, qf = kf_s[e, rows, :], qf_s[e, cols, :]
                    prob = jnp.where(same, jnp.exp(dot(kf, qf, 1, 1) - row(lse_ref.at[0, 0])), 0.0)
                    ds = (prob * (dot(vm, g, 1, 1) - row(dl_s))).astype(BF)
                    gv = dot(prob.astype(BF), g)
                    gk = dot(ds, qf)
                    gq_s[e, cols, :] = gq_s[e, cols, :] + dot(ds, kf, 0, 0)
                    outs.append((gk, gv))
                res_s[1, rows, :] = jnp.where(first, outs[0][0], pltpu.roll(outs[1][0], DH, 1))
                res_s[2, rows, :] = jnp.where(first, outs[0][1], outs[1][1])

        by_width(n, nb, body)
        return c

    lax.fori_loop(0, nb // GRP, k_group, 0)

    def finish(i, carry):
        rows = pl.ds(pl.multiple_of(i * BLK, BLK), BLK)
        new, gqs = [], []
        cos, sin, _ = tables(tab_ref[rows, :])
        for e in range(2):
            s_content, s_pos, s_proj = carry[e]
            g = gq_s[e, rows, :] * (DH**-0.5)
            turned = jnp.concatenate(
                [(g * cos).astype(BF), (g * sin).astype(BF)], 1
            )
            swapped = jnp.concatenate([mat_ref[0, e, DH:, :], mat_ref[0, e, :DH, :]], 0)
            gqp = dot(turned, swapped, 1, 1)
            gqs.append(g + gqp)
            s_content = s_content + jnp.sum(g, axis=0, keepdims=True)
            s_pos = s_pos + jnp.sum(gqp, axis=0, keepdims=True)
            s_proj = s_proj + dot(both_s[e, rows, :], turned, 0, 0)
            new.append((s_content, s_pos, s_proj))
        res_s[0, rows, :] = jnp.where(first, gqs[0], pltpu.roll(gqs[1], DH, 1))
        return tuple(new)

    row0 = jnp.zeros((1, 128), F32)
    zero = (row0, row0, jnp.zeros((128, 256), F32))
    sums = lax.fori_loop(0, nb, finish, (zero, zero), unroll=True)
    for e in range(2):
        gsm_ref[0, e, 0:1, :] = sums[e][0]
        gsm_ref[0, e, 1:2, :] = sums[e][1]
        gpp_ref[0, e] = sums[e][2]

    for at in range(width3 // 128):

        @pl.when(p == at)
        def _(at=at):
            for part in range(3):
                off = part * width3 + at * 128
                gqkv_ref[0, :, off : off + 128] = res_s[part].astype(BF)


def attention_specs(L, width):
    pairs = width // 128
    pair = lambda k: pl.BlockSpec((1, L, 128), lambda m, p, *_: (m, 0, k * pairs + p))
    per_m = lambda *s: pl.BlockSpec((1,) + s, lambda m, p, *_: (m,) + (0,) * len(s))
    per_p = lambda *s: pl.BlockSpec((1,) + s, lambda m, p, *_: (p,) + (0,) * len(s))
    whole = lambda *s: pl.BlockSpec(s, lambda m, p, *_: (0,) * len(s))
    return pairs, pair, per_m, per_p, whole


def attention_forward(qkv, lohi, segr, tab, bias, mat, vb):
    M, L, w3 = qkv.shape
    width = w3 // 3
    nb = L // BLK
    pairs, pair, per_m, per_p, whole = attention_specs(L, width)
    return pl.pallas_call(
        fwd_kernel,
        out_shape=(
            jax.ShapeDtypeStruct((M, L, width), BF),
            jax.ShapeDtypeStruct((M, L, width), BF),
            jax.ShapeDtypeStruct((M, pairs, 2, L // 128, 1, 128), F32),
        ),
        grid_spec=pltpu.PrefetchScalarGridSpec(
            num_scalar_prefetch=1,
            grid=(M, pairs),
            in_specs=[
                pair(0), pair(1), pair(2), per_m(L // 128, 1, 128), whole(L, 128), per_p(2, 128),
                per_p(2, 128, 256), per_p(1, 128),
            ],
            out_specs=[
                pair(0), pair(0),
                pl.BlockSpec((1, 1, 2, L // 128, 1, 128), lambda m, p, *_: (m, p, 0, 0, 0, 0)),
            ],
            scratch_shapes=[
                pltpu.VMEM((2, L, 128), BF),
                pltpu.VMEM((2, L, 128), BF),
                pltpu.VMEM((L, 128), F32),
            ],
        ),
        compiler_params=pltpu.CompilerParams(
            dimension_semantics=("arbitrary", "arbitrary"), vmem_limit_bytes=32 << 20
        ),
        name="attend",
    )(lohi, qkv, qkv, qkv, segr, tab, bias, mat, vb)


def attention_backward(m, into, qkv, g, o, lse, lohi, segr, tab, bias, mat):
    M, L, w3 = qkv.shape
    more = [] if into is None else [into]
    width = w3 // 3
    pairs = width // 128
    pair = lambda k: pl.BlockSpec((1, L, 128), lambda p, *_: (m, 0, k * pairs + p))
    per_m = lambda *s: pl.BlockSpec((1,) + s, lambda p, *_: (m,) + (0,) * len(s))
    per_p = lambda *s: pl.BlockSpec((1,) + s, lambda p, *_: (p,) + (0,) * len(s))
    whole = lambda *s: pl.BlockSpec(s, lambda p, *_: (0,) * len(s))
    return pl.pallas_call(
        functools.partial(bwd_kernel, m),
        out_shape=(
            jax.ShapeDtypeStruct((M, L, w3), BF),
            jax.ShapeDtypeStruct((pairs, 2, 8, 128), F32),
            jax.ShapeDtypeStruct((pairs, 2, 128, 256), F32),
        ),
        grid_spec=pltpu.PrefetchScalarGridSpec(
            num_scalar_prefetch=1,
            grid=(pairs,),
            in_specs=[
                pair(0), pair(1), pair(2), pair(0), pair(0),
                pl.BlockSpec((1, 1, 2, L // 128, 1, 128), lambda p, *_: (m, p, 0, 0, 0, 0)),
                per_m(L // 128, 1, 128),
                whole(L, 128), per_p(2, 128), per_p(2, 128, 256),
            ] + [pl.BlockSpec(memory_space=pl.ANY) for _ in more],
            out_specs=[per_m(L, w3), per_p(2, 8, 128), per_p(2, 128, 256)],
            scratch_shapes=[
                pltpu.VMEM((2, L, 128), BF),
                pltpu.VMEM((2, L, 128), BF),
                pltpu.VMEM((2, L, 128), BF),
                pltpu.VMEM((L, 128), F32),
                pltpu.VMEM((2, L // 128, 1, 128), F32),
                pltpu.VMEM((2, L, 128), F32),
                pltpu.VMEM((3, L, 128), F32),
            ],
        ),
        compiler_params=pltpu.CompilerParams(
            dimension_semantics=("arbitrary",), vmem_limit_bytes=32 << 20
        ),
        input_output_aliases={11: 0} if more else {},
        name="attend_back",
    )(lohi, qkv, qkv, qkv, g, o, lse, segr, tab, bias, mat, *more)


UB = 512


def ff_forward_kernel(
    hid_ref, hid2_ref, wi_ref, wo_ref, ib_ref, act_ref, dg_ref, own_ref, send_ref, acc
):
    u = pl.program_id(0)
    n2 = 2 * hid_ref.shape[0]
    RB = n2 // 2
    for r in range(n2 // RB):
        rows = slice(r * RB, (r + 1) * RB)
        v = dot((hid_ref if r == 0 else hid2_ref)[...], wi_ref[...]) + ib_ref[...]
        c = math.sqrt(2.0 / math.pi)
        v2 = v * v
        t = jnp.tanh(c * v * (1.0 + 0.044715 * v2))
        h = 0.5 * (1.0 + t)
        act = (v * h).astype(BF)
        dg = h + (0.5 * c) * v * (1.0 - t * t) * (1.0 + (3 * 0.044715) * v2)
        act_ref[rows, :] = act
        dg_ref[rows, :] = dg.astype(BF)
        new = dot(act, wo_ref[...])

        @pl.when(u == 0)
        def _(rows=rows, new=new):
            acc[rows, :] = new

        @pl.when(u > 0)
        def _(rows=rows, new=new):
            acc[rows, :] = acc[rows, :] + new

    @pl.when(u == pl.num_programs(0) - 1)
    def _():
        own_ref[...] = acc[: n2 // 2, :]
        send_ref[...] = acc[n2 // 2 :, :].astype(BF)


def ff_backward_kernel(
    go_ref, hid_ref, hid2_ref, wi_ref, wo_ref, dg_ref, ga_ref, gb_ref, gib_ref, own_ref,
    send_ref, acc, hid_t, gi_s,
):
    u = pl.program_id(0)
    n2 = go_ref.shape[0]
    RB = n2 // 2

    @pl.when(u == 0)
    def _():
        hid_t[:, : n2 // 2] = hid_ref[...].T
        hid_t[:, n2 // 2 :] = hid2_ref[...].T

    total = jnp.zeros((1, UB), F32)
    for r in range(n2 // RB):
        rows = slice(r * RB, (r + 1) * RB)
        gi = (dot(go_ref[rows, :], wo_ref[...], 1, 1) * dg_ref[rows, :].astype(F32)).astype(BF)
        gi_s[rows, :] = gi
        total = total + jnp.sum(gi.astype(F32), axis=0, keepdims=True)
        new = dot(gi, wi_ref[...], 1, 1)

        @pl.when(u == 0)
        def _(rows=rows, new=new):
            acc[rows, :] = new

        @pl.when(u > 0)
        def _(rows=rows, new=new):
            acc[rows, :] = acc[rows, :] + new

    gib_ref[...] = total
    g = dot(hid_t[...], gi_s[...]).astype(BF)

    @pl.when(u < pl.num_programs(0) // 2)
    def _():
        ga_ref[...] = g

    @pl.when(u >= pl.num_programs(0) // 2)
    def _():
        gb_ref[...] = g

    @pl.when(u == pl.num_programs(0) - 1)
    def _():
        own_ref[...] = acc[: n2 // 2, :]
        send_ref[...] = acc[n2 // 2 :, :].astype(BF)


def ff_specs(n2, d, fh):
    nq = fh // 2 // UB
    fixed = lambda *shape: pl.BlockSpec(shape, lambda u: (0,) * len(shape))
    units = lambda rows: pl.BlockSpec((rows, UB), lambda u: (0, u))
    outer = pl.BlockSpec((UB, d), lambda u: (lax.rem(u, nq), fh // d + u // nq))
    return fixed, units, outer


def ff_forward(hid, hid2, big, ib, fh):
    n2, d = 2 * hid.shape[0], hid.shape[1]
    fixed, units, outer = ff_specs(n2, d, fh)
    return pl.pallas_call(
        ff_forward_kernel,
        out_shape=(
            jax.ShapeDtypeStruct((n2, fh), BF),
            jax.ShapeDtypeStruct((n2, fh), BF),
            jax.ShapeDtypeStruct((n2 // 2, d), F32),
            jax.ShapeDtypeStruct((n2 // 2, d), BF),
        ),
        grid=(fh // UB,),
        in_specs=[fixed(n2 // 2, d), fixed(n2 // 2, d), units(d), outer, units(1)],
        out_specs=[units(n2), units(n2), fixed(n2 // 2, d), fixed(n2 // 2, d)],
        scratch_shapes=[pltpu.VMEM((n2, d), F32)],
        compiler_params=pltpu.CompilerParams(
            dimension_semantics=("arbitrary",), vmem_limit_bytes=56 << 20
        ),
        name="feed",
    )(hid, hid2, big, big, ib)


def ff_backward(go, hid, hid2, big, dg, fh):
    n2, d = go.shape
    fixed, units, outer = ff_specs(n2, d, fh)
    nq = fh // 2 // UB
    return pl.pallas_call(
        ff_backward_kernel,
        out_shape=(
            jax.ShapeDtypeStruct((d, fh // 2), BF),
            jax.ShapeDtypeStruct((d, fh // 2), BF),
            jax.ShapeDtypeStruct((1, fh), F32),
            jax.ShapeDtypeStruct((n2 // 2, d), F32),
            jax.ShapeDtypeStruct((n2 // 2, d), BF),
        ),
        grid=(fh // UB,),
        in_specs=[
            fixed(n2, d), fixed(n2 // 2, d), fixed(n2 // 2, d), units(d), outer, units(n2),
        ],
        out_specs=[
            pl.BlockSpec((d, UB), lambda u: (0, jnp.minimum(u, nq - 1))),
            pl.BlockSpec((d, UB), lambda u: (0, jnp.maximum(u - nq, 0))),
            units(1), fixed(n2 // 2, d), fixed(n2 // 2, d),
        ],
        scratch_shapes=[
            pltpu.VMEM((n2, d), F32),
            pltpu.VMEM((d, n2), BF),
            pltpu.VMEM((n2, UB), BF),
        ],
        compiler_params=pltpu.CompilerParams(
            dimension_semantics=("arbitrary",), vmem_limit_bytes=44 << 20
        ),
        name="feed_back",
    )(go, hid, hid2, big, big, dg)


def per_device(
    tokens, segment_ids, cotangent, query_proj, key_proj, value_proj, out_proj, value_bias,
    content_bias, position_bias, position_proj, out_bias, attn_gain, attn_shift, inner_proj,
    inner_bias, outer_proj, outer_bias, final_gain, final_shift,
):
    M, _, T, D = tokens.shape
    n_dz, n_dx, n_yy, n_core = (lax.axis_size(a) for a in ALL)
    S = n_yy * n_core
    chips = n_dz * n_dx * n_yy
    devices = chips * n_core
    L = T * S
    R = query_proj.shape[0]
    U = outer_proj.shape[0]
    FF = U * devices
    hl = H // S
    width = hl * DH
    pairs = width // 128
    half = DH // 2
    N = M * T
    core = lax.axis_index("core")
    seq = lax.axis_index("yy") * n_core + core
    x_bit = [("dx", 1)]
    yy_bits = [("yy", b) for b in bits_of("yy")]
    two = lambda bits: (2,) * len(bits)

    x = tokens[:, 0]
    x_other = swap(x, "yy", yy_bits[0][1])
    docs = lax.all_gather(segment_ids[:, 0], SEQ, axis=1, tiled=True)
    gate = [x_other]
    by_seq = jnp.stack([query_proj, key_proj, value_proj], 0).reshape(3, R, S, width)
    w3 = 3 * width
    by_seq = by_seq.transpose(2, 1, 0, 3).reshape(S, R, w3)
    mixed = lax.all_to_all(by_seq, SEQ, split_axis=0, concat_axis=0, tiled=True)
    mixed = gather_bits(mixed, "dz", 0, gate)
    w_qkv = gather_bits(mixed, "dx", 1).reshape(D, w3)

    row = lambda v: jnp.pad(v, (0, 128 - v.size))
    vectors = [
        content_bias, position_bias, value_bias, out_bias, attn_gain, attn_shift, outer_bias,
        final_gain, final_shift, inner_bias,
    ]
    n_vec = len(vectors)
    packed = jnp.concatenate([jnp.stack([row(v) for v in vectors]), position_proj.reshape(-1, 128)])
    n_pack = packed.shape[0]
    for axis in reversed(ALL):
        packed = gather_bits(packed, axis)
    packed = packed.reshape(devices, n_pack, 128)
    heads = lambda v: lax.dynamic_slice_in_dim(v.reshape(S, -1), seq, 1, 0)
    full = [packed[:, k, :R] for k in range(n_vec - 1)]
    full_content, full_posbias, full_vbias = full[:3]
    full_posproj = packed[:, n_vec:].reshape(devices, -1)
    vec = lambda v: v.reshape(1, -1).astype(F32)
    full_obias, full_again, full_ashift, full_fbias, full_fgain, full_fshift = map(vec, full[3:9])
    ib = packed[:, n_vec - 1, :U].reshape(chips, n_core, 2, U // 2)
    ib = lax.dynamic_index_in_dim(ib, core, 1, False)
    full_ibias = ib.transpose(1, 0, 2).reshape(1, -1).astype(F32)

    x_all = x
    for k, (axis, bit) in enumerate(yy_bits):
        x_all = double(x_all, axis, bit, 1 + k, x_other if k == 0 else None)
    x_all = x_all.reshape(M, n_yy, T, D)
    x_all = double(x_all, "core", 1, 2).reshape(M * L, D)

    FH, DC = FF // n_core, D // n_core
    inner_cols = inner_proj.reshape(R, chips, n_core, 2, U // 2).transpose(2, 0, 3, 1, 4)
    out_cols = out_proj.reshape(R, n_core, DC).transpose(1, 0, 2)
    cols = jnp.concatenate([inner_cols.reshape(n_core, R, FH), out_cols], 2)
    cols = lax.all_to_all(cols, "core", split_axis=0, concat_axis=0, tiled=True)
    cols = cols.reshape(n_core * R, FH + DC)
    big = [cols[:, :FH], outer_proj[: U // 2], outer_proj[U // 2 :], cols[:, FH:]]
    big = after(jnp.concatenate(big, 1), gate[1], docs)
    big = lax.all_gather(big, CHIP, axis=0, tiled=True)
    w_out_half = big[:, FH + 2 * D :]
    w_out_other = swap(w_out_half, "core", 1)
    by_core = lambda mine, other: jnp.where(
        core == 0, jnp.concatenate([mine, other], 1), jnp.concatenate([other, mine], 1)
    )

    nb = L // BLK
    ends = docs.reshape(M, nb, BLK)
    lo = jnp.sum(docs[:, None, :] < ends[:, :, :1], -1) // 128
    count = (jnp.sum(docs[:, None, :] <= ends[:, :, -1:], -1) - lo * 128 + BLK - 1) // BLK
    lo = jnp.minimum(lo, (L - count * BLK) // 128)
    lohi = jnp.stack([lo, count], -1).reshape(-1).astype(jnp.int32)
    segr = docs.reshape(M, L // 128, 1, 128).astype(F32)
    cos_t, sin_t = rotations(L, half)
    tab = jnp.concatenate([sin_t, sin_t, cos_t, cos_t], 1)
    bias = jnp.stack(
        [heads(full_content).reshape(hl, DH), heads(full_posbias).reshape(hl, DH)], 1
    )
    bias = bias.reshape(pairs, 2, 2 * DH).astype(F32)
    pp = heads(full_posproj).reshape(hl, DH, DH)
    pc, ps = pp[..., :half], pp[..., half:]
    z64 = jnp.zeros((hl, DH, DH), BF)
    mat = jnp.concatenate([z64, pc, -ps, z64, ps, pc], 2)
    mat = jnp.concatenate([jnp.zeros_like(mat), mat], 1).reshape(pairs, 2, 128, 256)
    vb = heads(full_vbias).reshape(pairs, 1, 128).astype(F32)

    qkv = dot(x_all, w_qkv).astype(BF).reshape(M, L, w3)
    ctx, o, lse = attention_forward(qkv, lohi, segr, tab, bias, mat, vb)
    ctx_tok = lax.all_to_all(
        ctx.reshape(M, S, T, width), SEQ, split_axis=1, concat_axis=1, tiled=True
    )
    ctx_tok = ctx_tok.transpose(0, 2, 1, 3).reshape(N, H * DH)
    x_float = x.reshape(N, D).astype(F32)
    attn = by_core(dot(ctx_tok, w_out_half), dot(ctx_tok, w_out_other)) + full_obias
    hidden, first_back = jax.vjp(
        lambda a, g, b: layer_norm(a, g, b), x_float + attn, full_again, full_ashift
    )
    hid = hidden.astype(BF)
    hid2 = swap(hid, "core", 1)
    active, dgelu, part, part_send = ff_forward(hid, hid2, big, full_ibias, FH)
    outer = part + swap(part_send, "core", 1).astype(F32) + full_fbias
    result, second_back = jax.vjp(
        lambda a, g, b: layer_norm(a, g, b), hidden + outer, full_fgain, full_fshift
    )
    output = result.astype(BF).reshape(M, 1, T, D)

    g_hidden, g_fgain, g_fshift = second_back(cotangent[:, 0].reshape(N, D).astype(F32))
    go = g_hidden.astype(BF)
    w_out = by_core(w_out_half, w_out_other)
    go_pair = jnp.concatenate([go, after(swap(go, "core", 1), w_out)], 0)
    FQ = FH // 2
    z_dims = [("dz", b) for b in bits_of("dz")]
    z_bits = z_dims[::-1]
    chip_bits = z_dims + x_bit + yy_bits
    rows = two(chip_bits) + (n_core * R,)
    g_outer_w = [dot(active[:, k * FQ : (k + 1) * FQ], go_pair, 0, 0).astype(BF) for k in range(2)]
    outer_y, outer_x = [Chain([g.reshape(rows + (D,))], chip_bits) for g in g_outer_w]
    outer_y.run(yy_bits[:1])
    outer_x.run(x_bit)
    *g_inner_w, g_ib, g_part, g_send = ff_backward(
        after(go_pair, outer_y.sends[0], outer_x.sends[0]), hid, hid2, big, dgelu, FH
    )
    g_send = meet(g_send, outer_y, outer_x)
    inner_y, inner_x = [
        Chain([g.reshape(rows + (FQ,))], chip_bits) for g in g_inner_w
    ]
    inner_x.run(x_bit)
    inner_y.run(yy_bits[:1])
    g_send = after(g_send, inner_x.sends[0], inner_y.sends[0])
    g_hidden = g_hidden + g_part + swap(g_send, "core", 1).astype(F32)
    g_sum, g_again, g_ashift = first_back(g_hidden)
    ga = g_sum.astype(BF)
    gc = jnp.stack(
        [dot(ga, w_out[k * width : (k + 1) * width], 1, 1).astype(BF) for k in range(S)]
    )
    g_heads = lax.all_to_all(gc, SEQ, split_axis=0, concat_axis=0, tiled=True)
    g_heads = g_heads.reshape(S, M, T, width).transpose(1, 0, 2, 3).reshape(M, L, width)

    ga_cols = after(ga, gc)
    cols = lambda k: lax.dynamic_slice_in_dim(ga_cols, k * DC, DC, 1)
    theirs = swap(dot(ctx_tok, cols(1 - core), 0, 0).astype(BF), "core", 1)
    g_out_half = (dot(ctx_tok, cols(core), 0, 0) + theirs.astype(F32)).astype(BF)
    out_y = Chain([g_out_half.reshape(rows + (DC,))], chip_bits)
    outer_y.terms, outer_x.terms, _ = lax.optimization_barrier((outer_y.terms, outer_x.terms, gc))
    outer_y.run(yy_bits[1:] + x_bit)
    outer_x.run(yy_bits)
    g_heads = meet(after(g_heads, outer_y.sends[-1], outer_x.sends[1]), inner_x, inner_y)
    inner_y.run(yy_bits[1:] + x_bit)
    inner_x.run(yy_bits)
    g_heads = after(g_heads, inner_y.sends[-1], inner_x.sends[1])
    out_y.run(yy_bits)

    gqkv, small = None, []
    for m in range(M):
        gqkv, sm, pp_m = attention_backward(
            m, gqkv, qkv, g_heads, o, lse, lohi, segr, tab, bias, mat
        )
        small.append((sm, pp_m))
        if m == 0:
            gqkv, g_heads = lax.optimization_barrier((gqkv, g_heads))
            g_heads = meet(g_heads, outer_y, outer_x, inner_y, inner_x)
            ff = [outer_y, outer_x, inner_y, inner_x]
            g_heads = after(g_heads, *run_together(ff, z_bits[:1]))
    gqkv = meet(gqkv, out_y, *ff).reshape(M * L, w3)
    gqkv = after(gqkv, *run_together(ff, z_bits[1:]))

    g_qkv_w = dot(x_all, gqkv, 0, 0).astype(BF).reshape(two(z_dims + x_bit) + (S * R, w3))
    mixed = Chain([g_qkv_w], z_dims + x_bit)
    mixed.run(x_bit)
    out_y.run(x_bit)
    dx = after(gqkv, mixed.sends[0], out_y.sends[-1])
    dx = dot(dx, w_qkv, 1, 1).astype(BF).reshape((M,) + two(yy_bits) + (2, T, D))
    dx = jnp.moveaxis(dx, 0, len(yy_bits) + 1)
    dx = Chain([dx], yy_bits + [("core", 1)]).run([("core", 1)] + yy_bits)
    colsums = (gc, ga, go, g_again, g_ashift, g_fgain, g_fshift, g_ib)
    (small, colsums, _) = meet((small, colsums, dx.sends[-1]), mixed, out_y, *ff)
    mixed.run(z_bits)
    out_y.terms = after(out_y.terms, mixed.sends[-1])
    out_y.run(z_bits)
    gc, ga, go, g_again, g_ashift, g_fgain, g_fshift, g_ib = colsums
    gsm, gpp = sum(k[0] for k in small), sum(k[1] for k in small)
    g_mixed = meet(mixed.result().astype(BF), dx)
    g_rows = lax.all_to_all(
        g_mixed.reshape(S, R, 3, width), SEQ, split_axis=0, concat_axis=0, tiled=True
    )
    g_rows = g_rows.astype(F32).transpose(2, 1, 0, 3).reshape(3, R, D)
    input_grad = (g_sum.reshape(M, T, D) + dx.result()).reshape(M, 1, T, D)

    colsum = lambda v: jnp.sum(v.astype(F32), axis=0).reshape(-1)
    gsm = gsm[:, :, :2, :DH].reshape(hl, 2, DH).transpose(1, 0, 2).reshape(2, 1, width)
    here = (jnp.arange(S) == seq).reshape(1, S, 1)
    g_heads_sm = jnp.where(here, gsm, 0.0).reshape(2, D)
    g_rest = [jnp.sum(gc.astype(F32), 1).reshape(-1), colsum(ga)] + [v.reshape(-1) for v in (g_again, g_ashift)]
    g_rest += [colsum(go), g_fgain.reshape(-1), g_fshift.reshape(-1)]
    g_vectors = jnp.concatenate([g_heads_sm, jnp.stack(g_rest)]).astype(BF)
    g_vectors = g_vectors.reshape(n_vec - 1, devices, R).transpose(1, 0, 2)
    g_vectors = jnp.pad(g_vectors, ((0, 0), (0, 0), (0, 128 - R)))
    g_ibias = g_ib.reshape(2, chips, 1, U // 2).transpose(1, 2, 0, 3).reshape(chips, 1, U)
    on_core = (jnp.arange(n_core) == core).reshape(1, n_core, 1)
    g_ibias = jnp.where(on_core, g_ibias, 0.0).reshape(devices, 1, U).astype(BF)
    g_ibias = jnp.pad(g_ibias, ((0, 0), (0, 0), (0, 128 - U)))
    gpp = gpp.reshape(hl, 128, 256)[:, DH:]
    e1, e2 = gpp[:, :, DH : 2 * DH], gpp[:, :, 3 * DH :]
    g_posproj = jnp.concatenate(
        [e1[..., :half] + e2[..., half:], e2[..., :half] - e1[..., half:]], -1
    ).astype(BF)
    g_posproj = jnp.where(here, g_posproj.reshape(1, 1, -1), jnp.zeros((), BF))
    g_posproj = g_posproj.reshape(devices, -1, 128)
    g_packed = jnp.concatenate([g_vectors, g_ibias, g_posproj], 1)
    g_packed = lax.all_to_all(g_packed, ALL, split_axis=0, concat_axis=0, tiled=True)
    g_packed = jnp.sum(g_packed.astype(F32), 0)
    s = [g_packed[k, : v.size] for k, v in enumerate(vectors)]
    g_pp = g_packed[n_vec:].reshape(R, DH)

    outer_grad = jnp.concatenate([outer_y.result(), outer_x.result()], 0)

    def by_rows(v):
        v = v.astype(BF).reshape(n_core, R, -1)
        mine = lax.dynamic_index_in_dim(v, core, 0, False)
        other = swap(lax.dynamic_index_in_dim(v, 1 - core, 0, False), "core", 1)
        return jnp.where(core == 0, mine, other), jnp.where(core == 0, other, mine)

    inner_grad = jnp.stack(by_rows(jnp.concatenate([inner_y.result(), inner_x.result()], 1)), 1)
    inner_grad = inner_grad.reshape(R, n_core, 2, chips, U // 2).transpose(0, 3, 1, 2, 4)
    inner_grad = inner_grad.astype(F32).reshape(R, FF)
    out_grad = jnp.concatenate(by_rows(out_y.result()), 1).astype(F32)

    return (
        output, input_grad, g_rows[0], g_rows[1], g_rows[2], out_grad, s[2], s[0], s[1], g_pp,
        s[3], s[4], s[5], inner_grad, s[9], outer_grad, s[6], s[7], s[8],
    )


def solution(mesh):
    n_dp, n_seq = mesh.devices.shape
    mesh = Mesh(mesh.devices.reshape(n_dp // 2, 2, n_seq // 2, 2), ALL)
    tok, ids = P(None, DP, SEQ, None), P(None, DP, SEQ)
    mat, vec = P(ALL, None), P(ALL)
    in_specs = (
        tok, ids, tok, mat, mat, mat, mat, vec, vec, vec, mat, vec, vec, vec, mat, vec, mat, vec,
        vec, vec,
    )
    out_specs = (
        tok, tok, mat, mat, mat, mat, vec, vec, vec, mat, vec, vec, vec, mat, vec, mat, vec, vec,
        vec,
    )
    return jax.shard_map(
        per_device, mesh=mesh, in_specs=in_specs, out_specs=out_specs, check_vma=False
    )
```

time: 608 us -> 515 us (0.85)
  matrix products: 68.5 us -> 30.7 us
  Pallas kernels: 120 us -> 90.1 us
  blocking collectives: 34.2 us -> 5.56 us
  waiting for transfers between devices: 140 us -> 165 us
  local copies, waits for them, and re-layouts: 69.6 us -> 55.7 us
  starting transfers between devices: 65.2 us -> 58.9 us
    dot_general x15 -> x13, matrix products: 68.5 us -> 30.7 us  [dot(): lax.dot_general(a, b, (((ca,), (cb,)), ((), ())), preferred_element_type=...]
    pallas_call x1, Pallas kernels: 52.1 us -> 19.1 us  [attention_forward(): pl.pallas_call(fwd_kernel, out_shape=(jax.ShapeDtypeStruct((M, L, width),...]
    all_gather x1, blocking collectives: 32 us -> 5.56 us  [per_device(): docs = lax.all_gather(segment_ids[:, 0], SEQ, axis=1, tiled=True)]
    ppermute x37, waiting for transfers between devices: 113 us -> 135 us  [swap(): return lax.ppermute(x, axis, [(i, i ^ bit) for i in range(n)])]
    add x6 -> x4, other arithmetic: 9.34 us -> 2.32 us  [the longest x2 2.24 us: total(): return sum((t.astype(F32) for t in terms))]
    all_to_all x1, waiting for transfers between devices: 14.2 us -> 7.23 us  [per_device(): lax.all_to_all(ctx.reshape(M, S, T, width), SEQ, split_axis=1, concat_axi...]
    all_to_all x6 -> x5, waiting for transfers between devices: 12.9 us -> 18 us  [the longest x1 16.6 us: per_device(): g_heads = lax.all_to_all(gc, SEQ, split_axis=0, concat_axis=0, tiled=True)]
    squeeze x7 -> x12, local copies, waits for them, and re-layouts: 8.44 us -> 12.4 us  [the longest x9 11.4 us: send(): take = lambda t, k: lax.dynamic_index_in_dim(t, k, dim, keepdims=False)]
  transfers between devices with their start and end apart: 45 -> 44, of which waited for: 17 -> 17; matrix products, arithmetic and copies ran while one was open for 27% -> 22% of each run, Pallas kernels for 20% -> 14%
where the time goes in v2:
time: 515 us; the launch traced here: 505 us
  waiting for transfers between devices  165 us (32%)
  Pallas kernels  90.1 us (17%)
  other arithmetic  83.2 us (16%)
  starting transfers between devices  58.9 us (11%)
  local copies, waits for them, and re-layouts  55.7 us (11%)
  matrix products  30.7 us (6%)
  between operations  16.2 us (3%)
  blocking collectives  5.56 us (1%)
    ppermute x37, waiting for transfers between devices, swap(): return lax.ppermute(x, axis, [(i, i ^ bit) for i in range(n)])  135 us
    ppermute x37, starting transfers between devices, swap(): return lax.ppermute(x, axis, [(i, i ^ bit) for i in range(n)])  34.1 us
    dot_general x13, matrix products, dot(): lax.dot_general(a, b, (((ca,), (cb,)), ((), ())), preferred_element_type=...  30.7 us
    pallas_call x2, Pallas kernels, attention_backward(): pl.pallas_call(functools.partial(bwd_kernel, m), out_shape=(jax.ShapeDtyp...  28.6 us
    convert_element_type x18, other arithmetic, send(): out = total([take(t, 1 - mine) for t in self.terms]).astype(BF)  28.4 us
    pallas_call x1, Pallas kernels, ff_backward(): pl.pallas_call(ff_backward_kernel, out_shape=(jax.ShapeDtypeStruct((d, fh...  22.1 us
    pallas_call x1, Pallas kernels, ff_forward(): pl.pallas_call(ff_forward_kernel, out_shape=(jax.ShapeDtypeStruct((n2, fh...  20.3 us
    pallas_call x1, Pallas kernels, attention_forward(): pl.pallas_call(fwd_kernel, out_shape=(jax.ShapeDtypeStruct((M, L, width),...  19.1 us
  transfers between devices with their start and end apart: 44, of which 17 were waited for; matrix products, arithmetic and copies ran while one was open for 22% of the time, Pallas kernels for 14%

profile of v2, /device:TPU:0, one launch (start us, length us, event | category | flops | bytes accessed | tf_op | source)
XLA Modules:
  0.0 505.2 jit_solution(943379510878455881)
XLA Ops:
  10.9 3.5 all-to-all-start.2
  16.2 4.3 all-to-all-start
  21.6 5.6 %all-gather = s32[2,1,1024]{2,1,0:T(1,128)S(1)} all-gather(s32[2,1,256]{2,1,0:T(1,128)S(1)} %copy-done.60), channel_id=2, replica_groups=mesh['dz'=4,'dx'=2,'yy'=2,'core'=2] {'yy','core'}, dimensions={2}, use_global_device_ids=true | all-gather | bytes 10240 | tf_op jit(solution)/shard_map/all_gather | solution.py:602
  27.2 2.7 collective-permute-start.2
  29.9 9.6 %collective-permute-done.2 = bf16[4,32,768]{2,1,0:T(8,128)(2,1)S(1)} collective-permute-done((bf16[4,32,768]{2,1,0:T(8,128)(2,1)S(1)}, bf16[4,32,768]{2,1,0:T(8,128)(2,1)S(1)}, u32[]{:S(2)}, u32[]{:S(2)}) %collective-permute-start.2) | collective-permute-done | bytes 196640 | tf_op jit(solution)/shard_map/ppermute | solution.py:49
  42.2 3.1 multiply_sine_fusion
  45.9 24.5 %collective-permute-done.6 = bf16[2,26,128]{2,1,0:T(8,128)(2,1)S(1)} collective-permute-done((bf16[2,26,128]{2,1,0:T(8,128)(2,1)S(1)}, bf16[2,26,128]{2,1,0:T(8,128)(2,1)S(1)}, u32[]{:S(2)}, u32[]{:S(2)}) %collective-permute-start.6) | collective-permute-done | bytes 13344 | tf_op jit(solution)/shard_map/ppermute | solution.py:49
  72.1 2.3 collective-permute-done.7
  74.8 8.6 %collective-permute-done.8 = bf16[2,2,2,26,128]{4,3,2,1,0:T(8,128)(2,1)S(1)} collective-permute-done((bf16[2,2,2,26,128]{4,3,2,1,0:T(8,128)(2,1)S(1)}, bf16[2,2,2,26,128]{4,3,2,1,0:T(8,128)(2,1)S(1)}, u32[]{:S(2)}, u32[]{:S(2)}) %collective-permute-start.8) | collective-permute-done | bytes 53280 | tf_op jit(solution)/shard_map/ppermute | solution.py:49
  89.8 24.8 %collective-permute-done.9 = bf16[2,2,2,2,26,128]{5,4,3,2,1,0:T(8,128)(2,1)S(1)} collective-permute-done((bf16[2,2,2,2,26,128]{5,4,3,2,1,0:T(8,128)(2,1)S(1)}, bf16[2,2,2,2,26,128]{5,4,3,2,1,0:T(8,128)(2,1)S(1)}, u32[]{:S(2)}, u32[]{:S(2)}) %collective-permute-start.9) | collective-permute-done | bytes 106528 | tf_op jit(solution)/shard_map/ppermute | solution.py:49
  119.5 30.7 %collective-permute-done.4 = bf16[4,4,32,768]{3,2,1,0:T(8,128)(2,1)} collective-permute-done((bf16[4,4,32,768]{3,2,1,0:T(8,128)(2,1)}, bf16[4,4,32,768]{3,2,1,0:T(8,128)(2,1)}, u32[]{:S(2)}, u32[]{:S(2)}) %collective-permute-start.4) | collective-permute-done | bytes 786464 | tf_op jit(solution)/shard_map/ppermute | solution.py:49
  152.0 2.7 select_bitcast_fusion.1
  155.1 3.6 convolution_convert_fusion.1
  158.8 19.1 %attend.1 = (bf16[2,1024,256]{2,1,0:T(8,128)(2,1)S(1)}, bf16[2,1024,256]{2,1,0:T(8,128)(2,1)S(1)}, f32[2,2,2,8,1,128]{5,4,3,2,1,0:T(1,128)S(1)}) custom-call(s32[16]{0:T(128)S(1)} %reshape.999.lohi, bf16[2,1024,768]{2,1,0:T(8,128)(2,1)S(1)} %bitcast.511, bf16[2,1024,768]{2,1,0:T(8,128)(2,1)S(1)} %bitcast.512, bf16[2,1024,768]{2,1,0:T(8,128)(2,1)S(1)} %bitcast.513, ...), custom_call_target="tpu_custom_call" | custom-call | tf_op jit(solution)/shard_map/attend/pallas_call | solution.py:354
  179.8 4.8 all-to-all-start.1
  184.6 4.1 all-gather.3.cloned.1.call-done.wi_ref.wo_ref
  188.7 2.3 slice.234
  191.9 7.2 %all-to-all-done.1 = bf16[2,4,256,256]{3,2,0,1:T(8,128)(2,1)} async-done(((bf16[2,4,256,256]{3,2,0,1:T(8,128)(2,1)}), bf16[2,4,256,256]{3,2,0,1:T(8,128)(2,1)}, u32[]{:S(2)}, u32[]{:S(2)}) %all-to-all-start.1) | async-done | bytes 1048608 | tf_op jit(solution)/shard_map/all_to_all | solution.py:675
  201.4 2.3 fusion.88
  206.8 2.3 fusion.23
  212.1 20.3 %feed.1 = (bf16[1024,2048]{1,0:T(8,128)(2,1)}, bf16[1024,2048]{1,0:T(8,128)(2,1)}, f32[512,1024]{1,0:T(8,128)}, bf16[512,1024]{1,0:T(8,128)(2,1)}) custom-call(bf16[512,1024]{1,0:T(8,128)(2,1)} %get-tuple-element.298.hid_ref, bf16[512,1024]{1,0:T(8,128)(2,1)} %collective-permute-done.11.hid2_ref, ...), custom_call_target="tpu_custom_call" | custom-call | tf_op jit(solution)/shard_map/feed/pallas_call | solution.py:522
  232.8 2.6 collective-permute-done.12
  235.5 3.3 fusion.94
  245.4 3.1 maximum_select_fusion.2
  248.8 3.9 fusion.17
  252.7 3.9 fusion.20
  259.5 4.5 collective-permute-start.15
  263.9 3.0 pad_maximum_fusion.2.go_ref
  267.0 22.1 %feed_back.1 = (bf16[1024,1024]{1,0:T(8,128)(2,1)S(1)}, bf16[1024,1024]{1,0:T(8,128)(2,1)S(1)}, f32[1,2048]{1,0:T(1,128)S(1)}, f32[512,1024]{1,0:T(8,128)S(1)}, bf16[512,1024]{1,0:T(8,128)(2,1)S(1)}) custom-call(bf16[1024,1024]{1,0:T(8,128)(2,1)} %pad_maximum_fusion.2.go_ref, bf16[512,1024]{1,0:T(8,128)(2,1)} %get-tuple-element.298.hid_ref, ...), custom_call_target="tpu_custom_call" | custom-call | tf_op jit(solution)/shard_map/feed_back/pallas_call | solution.py:545
  301.6 4.2 all-to-all-start.3
  305.9 2.2 fusion.31
  309.2 2.2 fusion.32
  313.4 16.6 %all-to-all-done.3 = bf16[4,512,256]{2,1,0:T(8,128)(2,1)} async-done(((bf16[4,512,256]{2,1,0:T(8,128)(2,1)}), bf16[4,512,256]{2,1,0:T(8,128)(2,1)}, u32[]{:S(2)}, u32[]{:S(2)}) %all-to-all-start.3) | async-done | bytes 1048608 | tf_op jit(solution)/shard_map/all_to_all | solution.py:722
  330.0 2.3 copy.298
  340.3 3.2 convolution_convert_fusion.3
  343.6 16.5 %attend_back.2 = (bf16[2,1024,768]{2,1,0:T(8,128)(2,1)S(1)}, f32[2,2,8,128]{3,2,1,0:T(8,128)S(1)}, f32[2,2,128,256]{3,2,1,0:T(8,128)S(1)}) custom-call(s32[16]{0:T(128)S(1)} %reshape.999.lohi, bf16[2,1024,768]{2,1,0:T(8,128)(2,1)S(1)} %bitcast.514, bf16[2,1024,768]{2,1,0:T(8,128)(2,1)S(1)} %bitcast.515, bf16[2,1024,768]{2,1,0:T(8,128)(2,1)S(1)} %bitcast.516, ...), custom_call_target="tpu_custom_call" | custom-call | tf_op jit(solution)/shard_map/attend_back/pallas_call | solution.py:394
  366.8 2.5 add_convert_fusion
  378.7 12.2 %attend_back.3 = (bf16[2,1024,768]{2,1,0:T(8,128)(2,1)S(1)}, f32[2,2,8,128]{3,2,1,0:T(8,128)S(1)}, f32[2,2,128,256]{3,2,1,0:T(8,128)S(1)}) custom-call(s32[16]{0:T(128)S(1)} %reshape.999.lohi, bf16[2,1024,768]{2,1,0:T(8,128)(2,1)S(1)} %bitcast.517, bf16[2,1024,768]{2,1,0:T(8,128)(2,1)S(1)} %bitcast.518, ...), custom_call_target="tpu_custom_call", output_to_operand_aliasing={{0}: (11, {})} | custom-call | tf_op jit(solution)/shard_map/attend_back/pallas_call | solution.py:394
  399.1 3.6 convolution_convert_fusion.2
  405.8 3.7 convolution_convert_fusion
  417.3 21.1 %collective-permute-done.29 = bf16[64,4096]{1,0:T(8,128)(2,1)S(1)} collective-permute-done((bf16[64,4096]{1,0:T(8,128)(2,1)S(1)}, bf16[64,4096]{1,0:T(8,128)(2,1)S(1)}, u32[]{:S(2)}, u32[]{:S(2)}) %collective-permute-start.29) | collective-permute-done | bytes 524320 | tf_op jit(solution)/shard_map/ppermute | solution.py:49
  439.3 3.1 fusion.5
  451.5 4.7 all-to-all-start.5
  466.2 2.7 collective-permute-start.31
  471.7 4.8 collective-permute-done.33
  477.4 2.5 collective-permute-start.34
  487.1 3.4 all-to-all-start.4
  490.4 3.9 fusion.8
  (444 shorter events, 139.1 us)
Async XLA Ops:
  10.9 5.3 %all-to-all-start.2 = ((bf16[2,32,2560]{2,1,0:T(8,128)(2,1)}), bf16[2,32,2560]{2,1,0:T(8,128)(2,1)S(1)}, u32[]{:S(2)}, u32[]{:S(2)}) async-start(bf16[2,32,2560]{2,1,0:T(8,128)(2,1)} %pad_maximum_fusion.12), calls=%async_computation.2 | async-start | bytes 655360 | tf_op jit(solution)/shard_map/all_to_all | solution.py:642
  16.2 11.0 %all-to-all-start = ((bf16[4,32,768]{2,1,0:T(8,128)(2,1)}), bf16[4,32,768]{2,1,0:T(8,128)(2,1)S(1)}, u32[]{:S(2)}, u32[]{:S(2)}) async-start(bf16[4,32,768]{2,1,0:T(8,128)(2,1)} %reshape.1001), calls=%async_computation | async-start | bytes 393216 | tf_op jit(solution)/shard_map/all_to_all | solution.py:607
  20.5 168.2 %all-gather.3.cloned.1.call-start = ((), (), s32[]{:S(2)}) async-start(), calls=%async_computation.6 | async-start | bytes 10027008 | tf_op jit(solution)/shard_map/all_gather | solution.py:646
  20.7 19.1 %copy-start.68 = (bf16[32]{0:T(256)(128)(2,1)S(1)}, bf16[32]{0:T(256)(128)(2,1)}, u32[]{:S(2)}) copy-start(bf16[32]{0:T(256)(128)(2,1)} %param.39) | copy-start | bytes 196
  20.7 19.1 %copy-start.61 = (bf16[128]{0:T(256)(128)(2,1)S(1)}, bf16[128]{0:T(256)(128)(2,1)}, u32[]{:S(2)}) copy-start(bf16[128]{0:T(256)(128)(2,1)} %param.35) | copy-start | bytes 772
  20.7 19.4 %copy-start.19 = (bf16[2,1,256,1024]{3,2,1,0:T(8,128)(2,1)S(1)}, bf16[2,1,256,1024]{3,2,1,0:T(8,128)(2,1)}, u32[]{:S(2)}) copy-start(bf16[2,1,256,1024]{3,2,1,0:T(8,128)(2,1)} %param.20) | copy-start | bytes 3145732
  27.2 12.3 %collective-permute-start.2 = (bf16[4,32,768]{2,1,0:T(8,128)(2,1)S(1)}, bf16[4,32,768]{2,1,0:T(8,128)(2,1)S(1)}, u32[]{:S(2)}, u32[]{:S(2)}) collective-permute-start(bf16[4,32,768]{2,1,0:T(8,128)(2,1)S(1)} %all-to-all-done), channel_id=1, source_target_pairs={{0,16},{8,24},{16,0},{24,8},{1,17},{9,25},{17,1},{25,9},{2,18},{10... | collective-permute-start | bytes 589832 | tf_op jit(solution)/shard_map/ppermute | solution.py:49
  40.0 5.5 %collective-permute-start.5 = (bf16[26,128]{1,0:T(8,128)(2,1)S(1)}, bf16[26,128]{1,0:T(8,128)(2,1)S(1)}, u32[]{:S(2)}, u32[]{:S(2)}) collective-permute-start(bf16[26,128]{1,0:T(8,128)(2,1)S(1)} %concatenate.107), channel_id=1, source_target_pairs={{0,1},{1,0},{2,3},{3,2},{4,5},{5,4},{6,7},{7,6},{8,9},{9,8},{10,11... | collective-permute-start | bytes 19976 | tf_op jit(solution)/shard_map/ppermute | solution.py:49
  40.1 43.2 %collective-permute-start = (bf16[2,256,1024]{2,1,0:T(8,128)(2,1)S(1)}, bf16[2,256,1024]{2,1,0:T(8,128)(2,1)}, u32[]{:S(2)}, u32[]{:S(2)}) collective-permute-start(bf16[2,256,1024]{2,1,0:T(8,128)(2,1)S(1)} %bitcast.538), channel_id=1, source_target_pairs={{0,2},{2,0},{1,3},{3,1},{4,6},{6,4},{5,7},{7,5},{8,10},{10,8},{9,1... | collective-permute-start | bytes 3145736 | tf_op jit(solution)/shard_map/ppermute | solution.py:49
  45.5 24.9 %collective-permute-start.6 = (bf16[2,26,128]{2,1,0:T(8,128)(2,1)S(1)}, bf16[2,26,128]{2,1,0:T(8,128)(2,1)S(1)}, u32[]{:S(2)}, u32[]{:S(2)}) collective-permute-start(bf16[2,26,128]{2,1,0:T(8,128)(2,1)S(1)} %pad_maximum_fusion.18), channel_id=1, source_target_pairs={{0,2},{2,0},{1,3},{3,1},{4,6},{6,4},{5,7},{7,5},{8,10},{10,8},{9,1... | collective-permute-start | bytes 39944 | tf_op jit(solution)/shard_map/ppermute | solution.py:49
  70.4 4.0 collective-permute-start.7
  74.5 8.9 %collective-permute-start.8 = (bf16[2,2,2,26,128]{4,3,2,1,0:T(8,128)(2,1)S(1)}, bf16[2,2,2,26,128]{4,3,2,1,0:T(8,128)(2,1)S(1)}, u32[]{:S(2)}, u32[]{:S(2)}) collective-permute-start(bf16[2,2,2,26,128]{4,3,2,1,0:T(8,128)(2,1)S(1)} %pad_maximum_fusion.15), channel_id=1, source_target_pairs={{0,16},{8,24},{16,0},{24,8},{1,17},{9,25},{17,1},{25,9},{2,18},{10... | collective-permute-start | bytes 159752 | tf_op jit(solution)/shard_map/ppermute | solution.py:49
  86.4 65.5 %collective-permute-start.1 = (bf16[2,2,256,1024]{3,2,1,0:T(8,128)(2,1)}, bf16[2,2,256,1024]{3,2,1,0:T(8,128)(2,1)}, u32[]{:S(2)}, u32[]{:S(2)}) collective-permute-start(bf16[2,2,256,1024]{3,2,1,0:T(8,128)(2,1)} %pad_maximum_fusion.1), channel_id=1, source_target_pairs={{0,1},{1,0},{2,3},{3,2},{4,5},{5,4},{6,7},{7,6},{8,9},{9,8},{10,11... | collective-permute-start | bytes 6291464 | tf_op jit(solution)/shard_map/ppermute | solution.py:49
  86.4 28.2 %collective-permute-start.3 = (bf16[2,4,32,768]{3,2,1,0:T(8,128)(2,1)S(1)}, bf16[2,4,32,768]{3,2,1,0:T(8,128)(2,1)S(1)}, u32[]{:S(2)}, u32[]{:S(2)}) collective-permute-start(bf16[2,4,32,768]{3,2,1,0:T(8,128)(2,1)S(1)} %pad_maximum_fusion.11), channel_id=1, source_target_pairs={{0,8},{8,0},{16,24},{24,16},{1,9},{9,1},{17,25},{25,17},{2,10},{10... | collective-permute-start | bytes 1179656 | tf_op jit(solution)/shard_map/ppermute | solution.py:49
  87.5 27.1 %collective-permute-start.9 = (bf16[2,2,2,2,26,128]{5,4,3,2,1,0:T(8,128)(2,1)S(1)}, bf16[2,2,2,2,26,128]{5,4,3,2,1,0:T(8,128)(2,1)S(1)}, u32[]{:S(2)}, u32[]{:S(2)}) collective-permute-start(bf16[2,2,2,2,26,128]{5,4,3,2,1,0:T(8,128)(2,1)S(1)} %pad_maximum_fusion.14), channel_id=1, source_target_pairs={{0,8},{8,0},{16,24},{24,16},{1,9},{9,1},{17,25},{25,17},{2,10},{10... | collective-permute-start | bytes 319496 | tf_op jit(solution)/shard_map/ppermute | solution.py:49
  115.8 34.4 %collective-permute-start.4 = (bf16[4,4,32,768]{3,2,1,0:T(8,128)(2,1)}, bf16[4,4,32,768]{3,2,1,0:T(8,128)(2,1)}, u32[]{:S(2)}, u32[]{:S(2)}) collective-permute-start(bf16[4,4,32,768]{3,2,1,0:T(8,128)(2,1)} %bitcast.18), channel_id=1, source_target_pairs={{0,4},{4,0},{1,5},{5,1},{2,6},{6,2},{3,7},{7,3},{8,12},{12,8},{9,1... | collective-permute-start | bytes 2359304 | tf_op jit(solution)/shard_map/ppermute | solution.py:49
  179.8 19.3 %all-to-all-start.1 = ((bf16[2,4,256,256]{3,2,0,1:T(8,128)(2,1)}), bf16[2,4,256,256]{3,2,0,1:T(8,128)(2,1)}, u32[]{:S(2)}, u32[]{:S(2)}) async-start(bf16[2,4,256,256]{3,2,0,1:T(8,128)(2,1)} %copy.289), calls=%async_computation.1 | async-start | bytes 2097152 | tf_op jit(solution)/shard_map/all_to_all | solution.py:675
  191.0 12.8 %collective-permute-start.10 = (bf16[1024,512]{1,0:T(8,128)(2,1)}, bf16[1024,512]{1,0:T(8,128)(2,1)}, u32[]{:S(2)}, u32[]{:S(2)}) collective-permute-start(bf16[1024,512]{1,0:T(8,128)(2,1)} %slice.234), channel_id=1, source_target_pairs={{0,1},{1,0},{2,3},{3,2},{4,5},{5,4},{6,7},{7,6},{8,9},{9,8},{10,11... | collective-permute-start | bytes 3145736 | tf_op jit(solution)/shard_map/ppermute | solution.py:49
  209.1 3.0 collective-permute-start.11
  232.4 3.1 collective-permute-start.12
  245.2 3.3 collective-permute-start.13
  257.9 34.3 %collective-permute-start.14 = (bf16[2,2,2,64,1024]{4,3,2,1,0:T(8,128)(2,1)S(1)}, bf16[2,2,2,64,1024]{4,3,2,1,0:T(8,128)(2,1)S(1)}, u32[]{:S(2)}, u32[]{:S(2)}) collective-permute-start(bf16[2,2,2,64,1024]{4,3,2,1,0:T(8,128)(2,1)S(1)} %get-tuple-element.306), channel_id=1, source_target_pairs={{0,2},{2,0},{1,3},{3,1},{4,6},{6,4},{5,7},{7,5},{8,10},{10,8},{9,1... | collective-permute-start | bytes 3145736 | tf_op jit(solution)/shard_map/ppermute | solution.py:49
  259.5 32.7 %collective-permute-start.15 = (bf16[2,2,2,64,1024]{4,3,2,1,0:T(8,128)(2,1)S(1)}, bf16[2,2,2,64,1024]{4,3,2,1,0:T(8,128)(2,1)S(1)}, u32[]{:S(2)}, u32[]{:S(2)}) collective-permute-start(bf16[2,2,2,64,1024]{4,3,2,1,0:T(8,128)(2,1)S(1)} %get-tuple-element.304), channel_id=1, source_target_pairs={{0,4},{4,0},{1,5},{5,1},{2,6},{6,2},{3,7},{7,3},{8,12},{12,8},{9,1... | collective-permute-start | bytes 3145736 | tf_op jit(solution)/shard_map/ppermute | solution.py:49
  292.2 2.7 collective-permute-start.16
  292.3 40.0 %collective-permute-start.17 = (bf16[2,2,2,64,1024]{4,3,2,1,0:T(8,128)(2,1)}, bf16[2,2,2,64,1024]{4,3,2,1,0:T(8,128)(2,1)}, u32[]{:S(2)}, u32[]{:S(2)}) collective-permute-start(bf16[2,2,2,64,1024]{4,3,2,1,0:T(8,128)(2,1)} %dynamic-slice_bitcast_fusion.3), channel_id=1, source_target_pairs={{0,4},{4,0},{1,5},{5,1},{2,6},{6,2},{3,7},{7,3},{8,12},{12,8},{9,1... | collective-permute-start | bytes 3145736 | tf_op jit(solution)/shard_map/ppermute | solution.py:49
  292.4 39.9 %collective-permute-start.18 = (bf16[2,2,2,64,1024]{4,3,2,1,0:T(8,128)(2,1)}, bf16[2,2,2,64,1024]{4,3,2,1,0:T(8,128)(2,1)}, u32[]{:S(2)}, u32[]{:S(2)}) collective-permute-start(bf16[2,2,2,64,1024]{4,3,2,1,0:T(8,128)(2,1)} %dynamic-slice_bitcast_fusion.2), channel_id=1, source_target_pairs={{0,2},{2,0},{1,3},{3,1},{4,6},{6,4},{5,7},{7,5},{8,10},{10,8},{9,1... | collective-permute-start | bytes 3145736 | tf_op jit(solution)/shard_map/ppermute | solution.py:49
  301.6 28.3 %all-to-all-start.3 = ((bf16[4,512,256]{2,1,0:T(8,128)(2,1)}), bf16[4,512,256]{2,1,0:T(8,128)(2,1)}, u32[]{:S(2)}, u32[]{:S(2)}) async-start(bf16[4,512,256]{2,1,0:T(8,128)(2,1)} %pad_maximum_fusion.4), calls=%async_computation.3 | async-start | bytes 2097152 | tf_op jit(solution)/shard_map/all_to_all | solution.py:722
  308.1 52.0 %collective-permute-start.19 = (bf16[2,2,64,1024]{3,2,1,0:T(8,128)(2,1)}, bf16[2,2,64,1024]{3,2,1,0:T(8,128)(2,1)}, u32[]{:S(2)}, u32[]{:S(2)}) collective-permute-start(bf16[2,2,64,1024]{3,2,1,0:T(8,128)(2,1)} %fusion.31), channel_id=1, source_target_pairs={{0,4},{4,0},{1,5},{5,1},{2,6},{6,2},{3,7},{7,3},{8,12},{12,8},{9,1... | collective-permute-start | bytes 1572872 | tf_op jit(solution)/shard_map/ppermute | solution.py:49
  311.4 48.7 %collective-permute-start.20 = (bf16[2,2,64,1024]{3,2,1,0:T(8,128)(2,1)}, bf16[2,2,64,1024]{3,2,1,0:T(8,128)(2,1)}, u32[]{:S(2)}, u32[]{:S(2)}) collective-permute-start(bf16[2,2,64,1024]{3,2,1,0:T(8,128)(2,1)} %fusion.32), channel_id=1, source_target_pairs={{0,2},{2,0},{1,3},{3,1},{4,6},{6,4},{5,7},{7,5},{8,10},{10,8},{9,1... | collective-permute-start | bytes 1572872 | tf_op jit(solution)/shard_map/ppermute | solution.py:49
  334.5 25.6 %collective-permute-start.21 = (bf16[2,2,64,1024]{3,2,1,0:T(8,128)(2,1)}, bf16[2,2,64,1024]{3,2,1,0:T(8,128)(2,1)}, u32[]{:S(2)}, u32[]{:S(2)}) collective-permute-start(bf16[2,2,64,1024]{3,2,1,0:T(8,128)(2,1)} %fusion.29), channel_id=1, source_target_pairs={{0,4},{4,0},{1,5},{5,1},{2,6},{6,2},{3,7},{7,3},{8,12},{12,8},{9,1... | collective-permute-start | bytes 1572872 | tf_op jit(solution)/shard_map/ppermute | solution.py:49
  338.7 21.5 %collective-permute-start.22 = (bf16[2,2,64,1024]{3,2,0,1:T(8,128)(2,1)}, bf16[2,2,64,1024]{3,2,0,1:T(8,128)(2,1)}, u32[]{:S(2)}, u32[]{:S(2)}) collective-permute-start(bf16[2,2,64,1024]{3,2,0,1:T(8,128)(2,1)} %copy.301), channel_id=1, source_target_pairs={{0,2},{2,0},{1,3},{3,1},{4,6},{6,4},{5,7},{7,5},{8,10},{10,8},{9,1... | collective-permute-start | bytes 1572872 | tf_op jit(solution)/shard_map/ppermute | solution.py:49
  343.6 23.3 %collective-permute-start.23 = (bf16[1024,512]{1,0:T(8,128)(2,1)}, bf16[1024,512]{1,0:T(8,128)(2,1)}, u32[]{:S(2)}, u32[]{:S(2)}) collective-permute-start(bf16[1024,512]{1,0:T(8,128)(2,1)} %convolution_convert_fusion.3), channel_id=1, source_target_pairs={{0,1},{1,0},{2,3},{3,2},{4,5},{5,4},{6,7},{7,6},{8,9},{9,8},{10,11... | collective-permute-start | bytes 3145736 | tf_op jit(solution)/shard_map/ppermute | solution.py:49
  366.8 25.9 %collective-permute-start.25 = (bf16[2,64,4096]{2,1,0:T(8,128)(2,1)}, bf16[2,64,4096]{2,1,0:T(8,128)(2,1)}, u32[]{:S(2)}, u32[]{:S(2)}) collective-permute-start(bf16[2,64,4096]{2,1,0:T(8,128)(2,1)} %pad_maximum_fusion.5), channel_id=1, source_target_pairs={{0,8},{8,0},{16,24},{24,16},{1,9},{9,1},{17,25},{25,17},{2,10},{10... | collective-permute-start | bytes 3145736 | tf_op jit(solution)/shard_map/ppermute | solution.py:49
  371.1 23.0 %collective-permute-start.24 = (bf16[2,2,2,64,512]{4,3,0,1,2:T(8,128)(2,1)}, bf16[2,2,2,64,512]{4,3,0,1,2:T(8,128)(2,1)}, u32[]{:S(2)}, u32[]{:S(2)}) collective-permute-start(bf16[2,2,2,64,512]{4,3,0,1,2:T(8,128)(2,1)} %copy_bitcast_fusion.1), channel_id=1, source_target_pairs={{0,2},{2,0},{1,3},{3,1},{4,6},{6,4},{5,7},{7,5},{8,10},{10,8},{9,1... | collective-permute-start | bytes 1572872 | tf_op jit(solution)/shard_map/ppermute | solution.py:49
  412.2 27.1 %collective-permute-start.26 = (bf16[2,2,256,1024]{3,2,1,0:T(8,128)(2,1)}, bf16[2,2,256,1024]{3,2,1,0:T(8,128)(2,1)}, u32[]{:S(2)}, u32[]{:S(2)}) collective-permute-start(bf16[2,2,256,1024]{3,2,1,0:T(8,128)(2,1)} %copy_bitcast_fusion), channel_id=1, source_target_pairs={{0,1},{1,0},{2,3},{3,2},{4,5},{5,4},{6,7},{7,6},{8,9},{9,8},{10,11... | collective-permute-start | bytes 6291464 | tf_op jit(solution)/shard_map/ppermute | solution.py:49
  412.2 26.3 %collective-permute-start.29 = (bf16[64,4096]{1,0:T(8,128)(2,1)S(1)}, bf16[64,4096]{1,0:T(8,128)(2,1)S(1)}, u32[]{:S(2)}, u32[]{:S(2)}) collective-permute-start(bf16[64,4096]{1,0:T(8,128)(2,1)S(1)} %pad_maximum_fusion.9), channel_id=1, source_target_pairs={{0,16},{8,24},{16,0},{24,8},{1,17},{9,25},{17,1},{25,9},{2,18},{10... | collective-permute-start | bytes 1572872 | tf_op jit(solution)/shard_map/ppermute | solution.py:49
  412.2 30.8 %collective-permute-start.27 = (bf16[2,2,128,768]{3,2,1,0:T(8,128)(2,1)}, bf16[2,2,128,768]{3,2,1,0:T(8,128)(2,1)}, u32[]{:S(2)}, u32[]{:S(2)}) collective-permute-start(bf16[2,2,128,768]{3,2,1,0:T(8,128)(2,1)} %dynamic-slice_bitcast_fusion.6), channel_id=1, source_target_pairs={{0,4},{4,0},{1,5},{5,1},{2,6},{6,2},{3,7},{7,3},{8,12},{12,8},{9,1... | collective-permute-start | bytes 2359304 | tf_op jit(solution)/shard_map/ppermute | solution.py:49
  415.1 27.8 %collective-permute-start.28 = (bf16[2,2,64,512]{3,2,0,1:T(8,128)(2,1)}, bf16[2,2,64,512]{3,2,0,1:T(8,128)(2,1)S(1)}, u32[]{:S(2)}, u32[]{:S(2)}) collective-permute-start(bf16[2,2,64,512]{3,2,0,1:T(8,128)(2,1)} %fusion.37), channel_id=1, source_target_pairs={{0,4},{4,0},{1,5},{5,1},{2,6},{6,2},{3,7},{7,3},{8,12},{12,8},{9,1... | collective-permute-start | bytes 786440 | tf_op jit(solution)/shard_map/ppermute | solution.py:49
  442.4 43.9 %collective-permute-start.32 = (bf16[2,256,1024]{2,1,0:T(8,128)(2,1)}, bf16[2,256,1024]{2,1,0:T(8,128)(2,1)}, u32[]{:S(2)}, u32[]{:S(2)}) collective-permute-start(bf16[2,256,1024]{2,1,0:T(8,128)(2,1)} %fusion.5), channel_id=1, source_target_pairs={{0,2},{2,0},{1,3},{3,1},{4,6},{6,4},{5,7},{7,5},{8,10},{10,8},{9,1... | collective-permute-start | bytes 3145736 | tf_op jit(solution)/shard_map/ppermute | solution.py:49
  445.7 19.4 %collective-permute-start.30 = (bf16[2,128,768]{2,1,0:T(8,128)(2,1)}, bf16[2,128,768]{2,1,0:T(8,128)(2,1)}, u32[]{:S(2)}, u32[]{:S(2)}) collective-permute-start(bf16[2,128,768]{2,1,0:T(8,128)(2,1)} %fusion.30), channel_id=1, source_target_pairs={{0,8},{8,0},{16,24},{24,16},{1,9},{9,1},{17,25},{25,17},{2,10},{10... | collective-permute-start | bytes 1179656 | tf_op jit(solution)/shard_map/ppermute | solution.py:49
  451.5 19.7 %all-to-all-start.5 = ((bf16[32,26,128]{2,1,0:T(8,128)(2,1)}), bf16[32,26,128]{2,1,0:T(8,128)(2,1)S(1)}, u32[]{:S(2)}, u32[]{:S(2)}) async-start(bf16[32,26,128]{2,1,0:T(8,128)(2,1)} %fusion.53), calls=%async_computation.5 | async-start | bytes 524288 | tf_op jit(solution)/shard_map/all_to_all | solution.py:796
  458.5 3.5 collective-permute-start.36
  466.2 18.1 %collective-permute-start.31 = (bf16[128,768]{1,0:T(8,128)(2,1)S(1)}, bf16[128,768]{1,0:T(8,128)(2,1)S(1)}, u32[]{:S(2)}, u32[]{:S(2)}) collective-permute-start(bf16[128,768]{1,0:T(8,128)(2,1)S(1)} %fusion.49), channel_id=1, source_target_pairs={{0,16},{8,24},{16,0},{24,8},{1,17},{9,25},{17,1},{25,9},{2,18},{10... | collective-permute-start | bytes 589832 | tf_op jit(solution)/shard_map/ppermute | solution.py:49
  468.9 21.5 %copy-start.24 = (f32[512,1024]{1,0:T(8,128)S(1)}, f32[512,1024]{1,0:T(8,128)}, u32[]{:S(2)}) copy-start(f32[512,1024]{1,0:T(8,128)} %get-tuple-element.292) | copy-start | bytes 6291460
  469.6 6.9 %collective-permute-start.33 = (bf16[2,64,512]{2,1,0:T(8,128)(2,1)}, bf16[2,64,512]{2,1,0:T(8,128)(2,1)}, u32[]{:S(2)}, u32[]{:S(2)}) collective-permute-start(bf16[2,64,512]{2,1,0:T(8,128)(2,1)} %fusion.64), channel_id=1, source_target_pairs={{0,8},{8,0},{16,24},{24,16},{1,9},{9,1},{17,25},{25,17},{2,10},{10... | collective-permute-start | bytes 393224 | tf_op jit(solution)/shard_map/ppermute | solution.py:49
  477.4 5.9 %collective-permute-start.34 = (bf16[64,512]{1,0:T(8,128)(2,1)S(1)}, bf16[64,512]{1,0:T(8,128)(2,1)S(1)}, u32[]{:S(2)}, u32[]{:S(2)}) collective-permute-start(bf16[64,512]{1,0:T(8,128)(2,1)S(1)} %fusion.71), channel_id=1, source_target_pairs={{0,16},{8,24},{16,0},{24,8},{1,17},{9,25},{17,1},{25,9},{2,18},{10... | collective-permute-start | bytes 196616 | tf_op jit(solution)/shard_map/ppermute | solution.py:49
  484.2 1.3 collective-permute-start.35
  487.1 8.7 %all-to-all-start.4 = ((bf16[4,32,3,256]{3,1,2,0:T(8,128)(2,1)}), bf16[4,32,3,256]{3,1,2,0:T(8,128)(2,1)S(1)}, u32[]{:S(2)}, u32[]{:S(2)}) async-start(bf16[4,32,3,256]{3,1,2,0:T(8,128)(2,1)} %copy.314), calls=%async_computation.4 | async-start | bytes 393216 | tf_op jit(solution)/shard_map/all_to_all | solution.py:769
  (68 other events, 457.5 us)
Sparse Core Ops, SparseCore 0:
  39.7 148.9 all-gather.2

commit v3 on v2

--- a/solution.py
+++ b/solution.py
@@ -104,15 +104,23 @@
         return total(self.terms)
 
 
+def send_together(chains, step):
+    return jnp.concatenate([c.send(step) for c in chains], -1)
+
+
+def take_together(chains, got):
+    at = 0
+    for c in chains:
+        width = c.terms[0].shape[-1]
+        c.terms.append(got[..., at : at + width])
+        at += width
+
+
 def run_together(chains, steps):
     sends = []
     for step in steps:
-        parts = [c.send(step) for c in chains]
-        sends.append(jnp.concatenate(parts, -1))
-        got, at = swap(sends[-1], *step), 0
-        for c, part in zip(chains, parts):
-            c.terms.append(got[..., at : at + part.shape[-1]])
-            at += part.shape[-1]
+        sends.append(send_together(chains, step))
+        take_together(chains, swap(sends[-1], *step))
     return sends
 
 
@@ -419,7 +427,7 @@
             ],
         ),
         compiler_params=pltpu.CompilerParams(
-            dimension_semantics=("arbitrary",), vmem_limit_bytes=32 << 20
+            dimension_semantics=("arbitrary",), vmem_limit_bytes=56 << 20
         ),
         input_output_aliases={11: 0} if more else {},
         name="attend_back",
@@ -605,8 +613,9 @@
     w3 = 3 * width
     by_seq = by_seq.transpose(2, 1, 0, 3).reshape(S, R, w3)
     mixed = lax.all_to_all(by_seq, SEQ, split_axis=0, concat_axis=0, tiled=True)
-    mixed = gather_bits(mixed, "dz", 0, gate)
-    w_qkv = gather_bits(mixed, "dx", 1).reshape(D, w3)
+    z_first = gather_bits(gather_bits(mixed[..., : w3 // 2], "dz", 0, gate), "dx", 1)
+    x_first = gather_bits(gather_bits(mixed[..., w3 // 2 :], "dx"), "dz")
+    w_qkv = jnp.concatenate([z_first, x_first], -1).reshape(D, w3)
 
     row = lambda v: jnp.pad(v, (0, 128 - v.size))
     vectors = [
@@ -616,9 +625,8 @@
     n_vec = len(vectors)
     packed = jnp.concatenate([jnp.stack([row(v) for v in vectors]), position_proj.reshape(-1, 128)])
     n_pack = packed.shape[0]
-    for axis in reversed(ALL):
-        packed = gather_bits(packed, axis)
-    packed = packed.reshape(devices, n_pack, 128)
+    packed = jnp.broadcast_to(after(packed, gate[1])[None], (devices, n_pack, 128))
+    packed = lax.all_to_all(packed, ALL, split_axis=0, concat_axis=0, tiled=True)
     heads = lambda v: lax.dynamic_slice_in_dim(v.reshape(S, -1), seq, 1, 0)
     full = [packed[:, k, :R] for k in range(n_vec - 1)]
     full_content, full_posbias, full_vbias = full[:3]
@@ -748,20 +756,24 @@
             ff = [outer_y, outer_x, inner_y, inner_x]
             g_heads = after(g_heads, *run_together(ff, z_bits[:1]))
     gqkv = meet(gqkv, out_y, *ff).reshape(M * L, w3)
-    gqkv = after(gqkv, *run_together(ff, z_bits[1:]))
+    run_together(ff, z_bits[1:-1])
 
     g_qkv_w = dot(x_all, gqkv, 0, 0).astype(BF).reshape(two(z_dims + x_bit) + (S * R, w3))
     mixed = Chain([g_qkv_w], z_dims + x_bit)
     mixed.run(x_bit)
+    sent = send_together(ff, z_bits[-1])
     out_y.run(x_bit)
-    dx = after(gqkv, mixed.sends[0], out_y.sends[-1])
+    dx = after(gqkv, mixed.sends[0], sent, out_y.sends[-1])
     dx = dot(dx, w_qkv, 1, 1).astype(BF).reshape((M,) + two(yy_bits) + (2, T, D))
     dx = jnp.moveaxis(dx, 0, len(yy_bits) + 1)
     dx = Chain([dx], yy_bits + [("core", 1)]).run([("core", 1)] + yy_bits)
     colsums = (gc, ga, go, g_again, g_ashift, g_fgain, g_fshift, g_ib)
-    (small, colsums, _) = meet((small, colsums, dx.sends[-1]), mixed, out_y, *ff)
+    (small, colsums, _) = meet((small, colsums, dx.sends[-1]), mixed, out_y)
     mixed.run(z_bits)
-    out_y.terms = after(out_y.terms, mixed.sends[-1])
+    out_y.terms[-1], got, _ = lax.optimization_barrier(
+        (out_y.terms[-1], swap(sent, *z_bits[-1]), mixed.sends[-1])
+    )
+    take_together(ff, got)
     out_y.run(z_bits)
     gc, ga, go, g_again, g_ashift, g_fgain, g_fshift, g_ib = colsums
     gsm, gpp = sum(k[0] for k in small), sum(k[1] for k in small)

time: 515 us -> 487 us (0.946)
  waiting for transfers between devices: 165 us -> 135 us
  local copies, waits for them, and re-layouts: 55.7 us -> 43.2 us
  Pallas kernels: 90.1 us -> 97.9 us
  starting transfers between devices: 58.9 us -> 65.3 us
    ppermute x37 -> x35, waiting for transfers between devices: 135 us -> 98.5 us  [swap(): return lax.ppermute(x, axis, [(i, i ^ bit) for i in range(n)])]
    all_gather x1, waiting for transfers between devices: 4.07 us -> 14.5 us  [per_device(): big = lax.all_gather(big, CHIP, axis=0, tiled=True)]
    pallas_call x2, Pallas kernels: 28.6 us -> 35.9 us  [attention_backward(): pl.pallas_call(functools.partial(bwd_kernel, m), out_shape=(jax.ShapeDtyp...]
    all_to_all x1, waiting for transfers between devices: 7.23 us -> 0.01 us  [per_device(): lax.all_to_all(ctx.reshape(M, S, T, width), SEQ, split_axis=1, concat_axi...]
    unnamed x159, local copies, waits for them, and re-layouts: 15.4 us -> 10 us
    ppermute x37 -> x35, starting transfers between devices: 34.1 us -> 38 us  [swap(): return lax.ppermute(x, axis, [(i, i ^ bit) for i in range(n)])]
    squeeze x9 -> x7, local copies, waits for them, and re-layouts: 11.4 us -> 8.08 us  [send(): take = lambda t, k: lax.dynamic_index_in_dim(t, k, dim, keepdims=False)]
  transfers between devices with their start and end apart: 44 -> 43, of which waited for: 17 -> 16; matrix products, arithmetic and copies ran while one was open for 22% -> 22% of each run, Pallas kernels for 14% -> 16%
where the time goes in v3:
time: 487 us; the launch traced here: 480 us
  waiting for transfers between devices  135 us (28%)
  Pallas kernels  97.9 us (20%)
  other arithmetic  84.2 us (17%)
  starting transfers between devices  65.3 us (13%)
  local copies, waits for them, and re-layouts  43.2 us (9%)
  matrix products  32.1 us (7%)
  between operations  16.1 us (3%)
  blocking collectives  5.56 us (1%)
    ppermute x35, waiting for transfers between devices, swap(): return lax.ppermute(x, axis, [(i, i ^ bit) for i in range(n)])  98.5 us
    ppermute x35, starting transfers between devices, swap(): return lax.ppermute(x, axis, [(i, i ^ bit) for i in range(n)])  38 us
    pallas_call x2, Pallas kernels, attention_backward(): pl.pallas_call(functools.partial(bwd_kernel, m), out_shape=(jax.ShapeDtyp...  35.9 us
    dot_general x13, matrix products, dot(): lax.dot_general(a, b, (((ca,), (cb,)), ((), ())), preferred_element_type=...  32.1 us
    convert_element_type x18, other arithmetic, send(): out = total([take(t, 1 - mine) for t in self.terms]).astype(BF)  27.6 us
    pallas_call x1, Pallas kernels, ff_backward(): pl.pallas_call(ff_backward_kernel, out_shape=(jax.ShapeDtypeStruct((d, fh...  21.5 us
    pallas_call x1, Pallas kernels, ff_forward(): pl.pallas_call(ff_forward_kernel, out_shape=(jax.ShapeDtypeStruct((n2, fh...  20.3 us
    pallas_call x1, Pallas kernels, attention_forward(): pl.pallas_call(fwd_kernel, out_shape=(jax.ShapeDtypeStruct((M, L, width),...  20.1 us
  transfers between devices with their start and end apart: 43, of which 16 were waited for; matrix products, arithmetic and copies ran while one was open for 22% of the time, Pallas kernels for 16%

profile of v3, /device:TPU:0, one launch (start us, length us, event | category | flops | bytes accessed | tf_op | source)
XLA Modules:
  0.0 479.6 jit_solution(727912787560660844)
XLA Ops:
  10.9 3.5 all-to-all-start.3
  16.2 4.3 all-to-all-start
  21.6 5.6 %all-gather = s32[2,1,1024]{2,1,0:T(1,128)S(1)} all-gather(s32[2,1,256]{2,1,0:T(1,128)S(1)} %copy-done.59), channel_id=2, replica_groups=mesh['dz'=4,'dx'=2,'yy'=2,'core'=2] {'yy','core'}, dimensions={2}, use_global_device_ids=true | all-gather | bytes 10240 | tf_op jit(solution)/shard_map/all_gather | solution.py:610
  28.9 2.6 collective-permute-start.2
  32.3 4.3 collective-permute-done.2
  44.3 4.1 all-to-all-start.1
  49.2 2.8 collective-permute-start.6
  52.0 16.8 %collective-permute-done = bf16[2,256,1024]{2,1,0:T(8,128)(2,1)S(1)} collective-permute-done((bf16[2,256,1024]{2,1,0:T(8,128)(2,1)S(1)}, bf16[2,256,1024]{2,1,0:T(8,128)(2,1)S(1)}, u32[]{:S(2)}, u32[]{:S(2)}) %collective-permute-start) | collective-permute-done | bytes 1048608 | tf_op jit(solution)/shard_map/ppermute | solution.py:49
  70.8 6.9 %collective-permute-done.6 = bf16[2,4,32,384]{3,2,1,0:T(8,128)(2,1)} collective-permute-done((bf16[2,4,32,384]{3,2,1,0:T(8,128)(2,1)}, bf16[2,4,32,384]{3,2,1,0:T(8,128)(2,1)}, u32[]{:S(2)}, u32[]{:S(2)}) %collective-permute-start.6) | collective-permute-done | bytes 196640 | tf_op jit(solution)/shard_map/ppermute | solution.py:49
  80.6 2.1 collective-permute-start.3
  83.4 36.7 %collective-permute-done.3 = bf16[2,4,32,384]{3,2,1,0:T(8,128)(2,1)S(1)} collective-permute-done((bf16[2,4,32,384]{3,2,1,0:T(8,128)(2,1)S(1)}, bf16[2,4,32,384]{3,2,1,0:T(8,128)(2,1)S(1)}, u32[]{:S(2)}, u32[]{:S(2)}) %collective-permute-start.3) | collective-permute-done | bytes 196640 | tf_op jit(solution)/shard_map/ppermute | solution.py:49
  124.4 8.4 %collective-permute-done.4 = bf16[4,4,32,384]{3,2,1,0:T(8,128)(2,1)} collective-permute-done((bf16[4,4,32,384]{3,2,1,0:T(8,128)(2,1)S(1)}, bf16[4,4,32,384]{3,2,1,0:T(8,128)(2,1)}, u32[]{:S(2)}, u32[]{:S(2)}) %collective-permute-start.4) | collective-permute-done | bytes 393248 | tf_op jit(solution)/shard_map/ppermute | solution.py:49
  134.2 2.3 select_bitcast_fusion.1
  136.9 3.7 convolution_convert_fusion.1
  140.6 20.1 %attend.1 = (bf16[2,1024,256]{2,1,0:T(8,128)(2,1)S(1)}, bf16[2,1024,256]{2,1,0:T(8,128)(2,1)S(1)}, f32[2,2,2,8,1,128]{5,4,3,2,1,0:T(1,128)S(1)}) custom-call(s32[16]{0:T(128)S(1)} %reshape.1012.lohi, bf16[2,1024,768]{2,1,0:T(8,128)(2,1)S(1)} %bitcast.490, bf16[2,1024,768]{2,1,0:T(8,128)(2,1)S(1)} %bitcast.491, bf16[2,1024,768]{2,1,0:T(8,128)(2,1)S(1)} %bitcast.492, ...), custom_call_target="tpu_custom_call" | custom-call | tf_op jit(solution)/shard_map/attend/pallas_call | solution.py:362
  163.4 4.0 all-to-all-start.2
  167.4 14.5 %all-gather.3.cloned.1.call-done.wi_ref.wo_ref = bf16[1024,4608]{1,0:T(8,128)(2,1)} async-done(((bf16[64,4608]{1,0:T(8,128)(2,1)}), bf16[1024,4608]{1,0:T(8,128)(2,1)}) %all-gather.3.cloned.1.call-update) | async-done | bytes 9437200 | tf_op jit(solution)/shard_map/all_gather | solution.py:654
  184.9 2.3 fusion.95
  196.0 20.3 %feed.1 = (bf16[1024,2048]{1,0:T(8,128)(2,1)}, bf16[1024,2048]{1,0:T(8,128)(2,1)}, f32[512,1024]{1,0:T(8,128)}, bf16[512,1024]{1,0:T(8,128)(2,1)}) custom-call(bf16[512,1024]{1,0:T(8,128)(2,1)} %copy-done.1, bf16[512,1024]{1,0:T(8,128)(2,1)} %copy-done.6, bf16[1024,4608]{1,0:T(8,128)(2,1)} %all-gather.3.cloned.1.call-done.wi_ref.wo_ref, ...), custom_call_target="tpu_custom_call" | custom-call | tf_op jit(solution)/shard_map/feed/pallas_call | solution.py:530
  217.0 2.3 collective-permute-done.10
  219.3 2.9 fusion.101
  228.2 2.4 maximum_select_fusion.2
  231.0 3.6 fusion.17
  234.6 3.6 fusion.20
  242.7 2.7 pad_maximum_fusion.2.go_ref
  245.5 21.5 %feed_back.1 = (bf16[1024,1024]{1,0:T(8,128)(2,1)S(1)}, bf16[1024,1024]{1,0:T(8,128)(2,1)S(1)}, f32[1,2048]{1,0:T(1,128)S(1)}, f32[512,1024]{1,0:T(8,128)S(1)}, bf16[512,1024]{1,0:T(8,128)(2,1)S(1)}) custom-call(bf16[1024,1024]{1,0:T(8,128)(2,1)} %pad_maximum_fusion.2.go_ref, bf16[512,1024]{1,0:T(8,128)(2,1)S(1)} %copy-done.2, ...), custom_call_target="tpu_custom_call" | custom-call | tf_op jit(solution)/shard_map/feed_back/pallas_call | solution.py:553
  279.2 4.2 all-to-all-start.4
  290.2 18.2 %all-to-all-done.4 = bf16[4,512,256]{2,1,0:T(8,128)(2,1)} async-done(((bf16[4,512,256]{2,1,0:T(8,128)(2,1)}), bf16[4,512,256]{2,1,0:T(8,128)(2,1)}, u32[]{:S(2)}, u32[]{:S(2)}) %all-to-all-start.4) | async-done | bytes 1048608 | tf_op jit(solution)/shard_map/all_to_all | solution.py:730
  308.4 2.3 copy.320
  310.6 2.0 fusion.29
  313.3 2.2 fusion.28
  317.1 3.1 convolution_convert_fusion.3
  320.2 17.8 %attend_back.2 = (bf16[2,1024,768]{2,1,0:T(8,128)(2,1)}, f32[2,2,8,128]{3,2,1,0:T(8,128)}, f32[2,2,128,256]{3,2,1,0:T(8,128)}) custom-call(s32[16]{0:T(128)} %copy-done.12, bf16[2,1024,768]{2,1,0:T(8,128)(2,1)} %bitcast.493, bf16[2,1024,768]{2,1,0:T(8,128)(2,1)} %bitcast.494, bf16[2,1024,768]{2,1,0:T(8,128)(2,1)} %bitcast.495, ...), custom_call_target="tpu_custom_call" | custom-call | tf_op jit(solution)/shard_map/attend_back/pallas_call | solution.py:402
  345.4 2.5 add_convert_fusion
  351.1 18.1 %attend_back.3 = (bf16[2,1024,768]{2,1,0:T(8,128)(2,1)}, f32[2,2,8,128]{3,2,1,0:T(8,128)}, f32[2,2,128,256]{3,2,1,0:T(8,128)}) custom-call(s32[16]{0:T(128)} %copy-done.12, bf16[2,1024,768]{2,1,0:T(8,128)(2,1)} %bitcast.496, bf16[2,1024,768]{2,1,0:T(8,128)(2,1)} %bitcast.497, bf16[2,1024,768]{2,1,0:T(8,128)(2,1)} %bitcast.498, ...), custom_call_target="tpu_custom_call", output_to_operand_aliasing={{0}: (11, {})} | custom-call | tf_op jit(solution)/shard_map/attend_back/pallas_call | solution.py:402
  371.3 5.7 %convolution_convert_fusion.2 = bf16[1024,768]{1,0:T(8,128)(2,1)S(1)} fusion(bf16[2048,1024]{1,0:T(8,128)(2,1)S(1)} %bitcast.522, bf16[2048,768]{1,0:T(8,128)(2,1)} %bitcast.528), kind=kOutput, calls=%fused_computation.48 | convolution fusion | flops 3222011904 | bytes 8912896 | tf_op jit(solution)/shard_map/dot_general | solution.py:25
  384.8 3.8 convolution_convert_fusion
  391.3 2.0 collective-permute-start.25
  394.7 2.5 collective-permute-start.30
  397.2 2.9 fusion.5
  401.1 16.2 %collective-permute-done.26 = bf16[2,2,64,512]{3,2,0,1:T(8,128)(2,1)S(1)} collective-permute-done((bf16[2,2,64,512]{3,2,0,1:T(8,128)(2,1)S(1)}, bf16[2,2,64,512]{3,2,0,1:T(8,128)(2,1)S(1)}, u32[]{:S(2)}, u32[]{:S(2)}) %collective-permute-start.26) | collective-permute-done | bytes 262176 | tf_op jit(solution)/shard_map/ppermute | solution.py:49
  417.3 2.1 fusion.30
  429.3 3.8 all-to-all-start.6
  435.0 2.8 collective-permute-start.28
  445.0 2.6 all-to-all-done.6
  454.1 3.4 collective-permute-done.32
  461.4 3.4 all-to-all-start.5
  464.8 3.9 fusion.8
  (435 shorter events, 133.8 us)
Async XLA Ops:
  10.9 5.3 %all-to-all-start.3 = ((bf16[2,32,2560]{2,1,0:T(8,128)(2,1)}), bf16[2,32,2560]{2,1,0:T(8,128)(2,1)S(1)}, u32[]{:S(2)}, u32[]{:S(2)}) async-start(bf16[2,32,2560]{2,1,0:T(8,128)(2,1)} %pad_maximum_fusion.16), calls=%async_computation.3 | async-start | bytes 655360 | tf_op jit(solution)/shard_map/all_to_all | solution.py:650
  16.2 11.0 %all-to-all-start = ((bf16[4,32,768]{2,1,0:T(8,128)(2,1)}), bf16[4,32,768]{2,1,0:T(8,128)(2,1)S(1)}, u32[]{:S(2)}, u32[]{:S(2)}) async-start(bf16[4,32,768]{2,1,0:T(8,128)(2,1)} %reshape.1014), calls=%async_computation | async-start | bytes 393216 | tf_op jit(solution)/shard_map/all_to_all | solution.py:615
  20.5 161.4 %all-gather.3.cloned.1.call-start = ((), (), s32[]{:S(2)}) async-start(), calls=%async_computation.7 | async-start | bytes 10027008 | tf_op jit(solution)/shard_map/all_gather | solution.py:654
  27.2 5.1 %collective-permute-start.5 = (bf16[4,32,384]{2,1,0:T(8,128)(2,1)S(1)}, bf16[4,32,384]{2,1,0:T(8,128)(2,1)S(1)}, u32[]{:S(2)}, u32[]{:S(2)}) collective-permute-start(bf16[4,32,384]{2,1,0:T(8,128)(2,1)S(1)} %get-tuple-element.358), channel_id=1, source_target_pairs={{0,4},{4,0},{1,5},{5,1},{2,6},{6,2},{3,7},{7,3},{8,12},{12,8},{9,1... | collective-permute-start | bytes 294920 | tf_op jit(solution)/shard_map/ppermute | solution.py:49
  28.9 7.8 %collective-permute-start.2 = (bf16[4,32,384]{2,1,0:T(8,128)(2,1)S(1)}, bf16[4,32,384]{2,1,0:T(8,128)(2,1)S(1)}, u32[]{:S(2)}, u32[]{:S(2)}) collective-permute-start(bf16[4,32,384]{2,1,0:T(8,128)(2,1)S(1)} %get-tuple-element.359), channel_id=1, source_target_pairs={{0,16},{8,24},{16,0},{24,8},{1,17},{9,25},{17,1},{25,9},{2,18},{10... | collective-permute-start | bytes 294920 | tf_op jit(solution)/shard_map/ppermute | solution.py:49
  37.4 31.4 %collective-permute-start = (bf16[2,256,1024]{2,1,0:T(8,128)(2,1)S(1)}, bf16[2,256,1024]{2,1,0:T(8,128)(2,1)S(1)}, u32[]{:S(2)}, u32[]{:S(2)}) collective-permute-start(bf16[2,256,1024]{2,1,0:T(8,128)(2,1)S(1)} %bitcast.513), channel_id=1, source_target_pairs={{0,2},{2,0},{1,3},{3,1},{4,6},{6,4},{5,7},{7,5},{8,10},{10,8},{9,1... | collective-permute-start | bytes 3145736 | tf_op jit(solution)/shard_map/ppermute | solution.py:49
  44.3 35.2 %all-to-all-start.1 = ((bf16[32,26,128]{2,1,0:T(8,128)(2,1)}), bf16[32,26,128]{2,1,0:T(8,128)(2,1)S(1)}, u32[]{:S(2)}, u32[]{:S(2)}) async-start(bf16[32,26,128]{2,1,0:T(8,128)(2,1)} %broadcast_in_dim.110), calls=%async_computation.1 | async-start | bytes 524288 | tf_op jit(solution)/shard_map/all_to_all | solution.py:629
  49.2 28.5 %collective-permute-start.6 = (bf16[2,4,32,384]{3,2,1,0:T(8,128)(2,1)}, bf16[2,4,32,384]{3,2,1,0:T(8,128)(2,1)}, u32[]{:S(2)}, u32[]{:S(2)}) collective-permute-start(bf16[2,4,32,384]{3,2,1,0:T(8,128)(2,1)} %pad_maximum_fusion.18), channel_id=1, source_target_pairs={{0,16},{8,24},{16,0},{24,8},{1,17},{9,25},{17,1},{25,9},{2,18},{10... | collective-permute-start | bytes 589832 | tf_op jit(solution)/shard_map/ppermute | solution.py:49
  70.6 63.5 %collective-permute-start.1 = (bf16[2,2,256,1024]{3,2,1,0:T(8,128)(2,1)}, bf16[2,2,256,1024]{3,2,1,0:T(8,128)(2,1)}, u32[]{:S(2)}, u32[]{:S(2)}) collective-permute-start(bf16[2,2,256,1024]{3,2,1,0:T(8,128)(2,1)} %pad_maximum_fusion.1), channel_id=1, source_target_pairs={{0,1},{1,0},{2,3},{3,2},{4,5},{5,4},{6,7},{7,6},{8,9},{9,8},{10,11... | collective-permute-start | bytes 6291464 | tf_op jit(solution)/shard_map/ppermute | solution.py:49
  70.8 69.8 %copy-start.12 = (s32[16]{0:T(128)}, s32[16]{0:T(128)S(1)}, u32[]{:S(2)}) copy-start(s32[16]{0:T(128)S(1)} %reshape.1012.lohi) | copy-start | bytes 196
  70.8 69.7 %copy-start.10 = (f32[2,8,1,128]{3,2,1,0:T(1,128)}, f32[2,8,1,128]{3,2,1,0:T(1,128)S(1)}, u32[]{:S(2)}) copy-start(f32[2,8,1,128]{3,2,1,0:T(1,128)S(1)} %convert_element_type.787.segr_ref) | copy-start | bytes 24580
  79.5 43.5 %collective-permute-start.7 = (bf16[2,2,4,32,384]{4,3,2,1,0:T(8,128)(2,1)}, bf16[2,2,4,32,384]{4,3,2,1,0:T(8,128)(2,1)}, u32[]{:S(2)}, u32[]{:S(2)}) collective-permute-start(bf16[2,2,4,32,384]{4,3,2,1,0:T(8,128)(2,1)} %pad_maximum_fusion.15), channel_id=1, source_target_pairs={{0,8},{8,0},{16,24},{24,16},{1,9},{9,1},{17,25},{25,17},{2,10},{10... | collective-permute-start | bytes 1179656 | tf_op jit(solution)/shard_map/ppermute | solution.py:49
  80.6 39.6 %collective-permute-start.3 = (bf16[2,4,32,384]{3,2,1,0:T(8,128)(2,1)S(1)}, bf16[2,4,32,384]{3,2,1,0:T(8,128)(2,1)S(1)}, u32[]{:S(2)}, u32[]{:S(2)}) collective-permute-start(bf16[2,4,32,384]{3,2,1,0:T(8,128)(2,1)S(1)} %copy-done.50), channel_id=1, source_target_pairs={{0,8},{8,0},{16,24},{24,16},{1,9},{9,1},{17,25},{25,17},{2,10},{10... | collective-permute-start | bytes 589832 | tf_op jit(solution)/shard_map/ppermute | solution.py:49
  120.3 12.6 %collective-permute-start.4 = (bf16[4,4,32,384]{3,2,1,0:T(8,128)(2,1)S(1)}, bf16[4,4,32,384]{3,2,1,0:T(8,128)(2,1)}, u32[]{:S(2)}, u32[]{:S(2)}) collective-permute-start(bf16[4,4,32,384]{3,2,1,0:T(8,128)(2,1)S(1)} %bitcast.538), channel_id=1, source_target_pairs={{0,4},{4,0},{1,5},{5,1},{2,6},{6,2},{3,7},{7,3},{8,12},{12,8},{9,1... | collective-permute-start | bytes 1179656 | tf_op jit(solution)/shard_map/ppermute | solution.py:49
  140.5 20.2 %copy-start = (bf16[2048,768]{1,0:T(8,128)(2,1)}, bf16[2048,768]{1,0:T(8,128)(2,1)S(1)}, u32[]{:S(2)}) copy-start(bf16[2048,768]{1,0:T(8,128)(2,1)S(1)} %convolution_convert_fusion.1) | copy-start | bytes 9437188
  163.4 20.5 %all-to-all-start.2 = ((bf16[2,4,256,256]{3,2,0,1:T(8,128)(2,1)}), bf16[2,4,256,256]{3,2,0,1:T(8,128)(2,1)S(1)}, u32[]{:S(2)}, u32[]{:S(2)}) async-start(bf16[2,4,256,256]{3,2,0,1:T(8,128)(2,1)} %copy.311), calls=%async_computation.2 | async-start | bytes 2097152 | tf_op jit(solution)/shard_map/all_to_all | solution.py:683
  183.3 4.0 collective-permute-start.8
  192.3 2.8 collective-permute-start.9
  216.3 2.9 collective-permute-start.10
  227.7 2.9 collective-permute-start.11
  239.5 29.8 %collective-permute-start.12 = (bf16[2,2,2,64,1024]{4,3,2,1,0:T(8,128)(2,1)S(1)}, bf16[2,2,2,64,1024]{4,3,2,1,0:T(8,128)(2,1)S(1)}, u32[]{:S(2)}, u32[]{:S(2)}) collective-permute-start(bf16[2,2,2,64,1024]{4,3,2,1,0:T(8,128)(2,1)S(1)} %get-tuple-element.324), channel_id=1, source_target_pairs={{0,2},{2,0},{1,3},{3,1},{4,6},{6,4},{5,7},{7,5},{8,10},{10,8},{9,1... | collective-permute-start | bytes 3145736 | tf_op jit(solution)/shard_map/ppermute | solution.py:49
  242.1 27.1 %collective-permute-start.13 = (bf16[2,2,2,64,1024]{4,3,2,1,0:T(8,128)(2,1)S(1)}, bf16[2,2,2,64,1024]{4,3,2,1,0:T(8,128)(2,1)S(1)}, u32[]{:S(2)}, u32[]{:S(2)}) collective-permute-start(bf16[2,2,2,64,1024]{4,3,2,1,0:T(8,128)(2,1)S(1)} %get-tuple-element.322), channel_id=1, source_target_pairs={{0,4},{4,0},{1,5},{5,1},{2,6},{6,2},{3,7},{7,3},{8,12},{12,8},{9,1... | collective-permute-start | bytes 3145736 | tf_op jit(solution)/shard_map/ppermute | solution.py:49
  269.3 2.7 collective-permute-start.14
  269.4 41.3 %collective-permute-start.15 = (bf16[2,2,2,64,1024]{4,3,2,1,0:T(8,128)(2,1)}, bf16[2,2,2,64,1024]{4,3,2,1,0:T(8,128)(2,1)}, u32[]{:S(2)}, u32[]{:S(2)}) collective-permute-start(bf16[2,2,2,64,1024]{4,3,2,1,0:T(8,128)(2,1)} %dynamic-slice_bitcast_fusion.3), channel_id=1, source_target_pairs={{0,4},{4,0},{1,5},{5,1},{2,6},{6,2},{3,7},{7,3},{8,12},{12,8},{9,1... | collective-permute-start | bytes 3145736 | tf_op jit(solution)/shard_map/ppermute | solution.py:49
  270.8 39.8 %collective-permute-start.16 = (bf16[2,2,2,64,1024]{4,3,2,1,0:T(8,128)(2,1)}, bf16[2,2,2,64,1024]{4,3,2,1,0:T(8,128)(2,1)}, u32[]{:S(2)}, u32[]{:S(2)}) collective-permute-start(bf16[2,2,2,64,1024]{4,3,2,1,0:T(8,128)(2,1)} %dynamic-slice_bitcast_fusion.2), channel_id=1, source_target_pairs={{0,2},{2,0},{1,3},{3,1},{4,6},{6,4},{5,7},{7,5},{8,10},{10,8},{9,1... | collective-permute-start | bytes 3145736 | tf_op jit(solution)/shard_map/ppermute | solution.py:49
  279.2 29.2 %all-to-all-start.4 = ((bf16[4,512,256]{2,1,0:T(8,128)(2,1)}), bf16[4,512,256]{2,1,0:T(8,128)(2,1)}, u32[]{:S(2)}, u32[]{:S(2)}) async-start(bf16[4,512,256]{2,1,0:T(8,128)(2,1)} %pad_maximum_fusion.4), calls=%async_computation.4 | async-start | bytes 2097152 | tf_op jit(solution)/shard_map/all_to_all | solution.py:730
  285.9 52.1 %collective-permute-start.17 = (bf16[2,2,64,1024]{3,2,0,1:T(8,128)(2,1)}, bf16[2,2,64,1024]{3,2,0,1:T(8,128)(2,1)}, u32[]{:S(2)}, u32[]{:S(2)}) collective-permute-start(bf16[2,2,64,1024]{3,2,0,1:T(8,128)(2,1)} %copy.323), channel_id=1, source_target_pairs={{0,4},{4,0},{1,5},{5,1},{2,6},{6,2},{3,7},{7,3},{8,12},{12,8},{9,1... | collective-permute-start | bytes 1572872 | tf_op jit(solution)/shard_map/ppermute | solution.py:49
  288.3 49.8 %collective-permute-start.18 = (bf16[2,2,64,1024]{3,2,1,0:T(8,128)(2,1)}, bf16[2,2,64,1024]{3,2,1,0:T(8,128)(2,1)}, u32[]{:S(2)}, u32[]{:S(2)}) collective-permute-start(bf16[2,2,64,1024]{3,2,1,0:T(8,128)(2,1)} %fusion.32), channel_id=1, source_target_pairs={{0,2},{2,0},{1,3},{3,1},{4,6},{6,4},{5,7},{7,5},{8,10},{10,8},{9,1... | collective-permute-start | bytes 1572872 | tf_op jit(solution)/shard_map/ppermute | solution.py:49
  312.7 25.4 %collective-permute-start.19 = (bf16[2,2,64,1024]{3,2,1,0:T(8,128)(2,1)}, bf16[2,2,64,1024]{3,2,1,0:T(8,128)(2,1)}, u32[]{:S(2)}, u32[]{:S(2)}) collective-permute-start(bf16[2,2,64,1024]{3,2,1,0:T(8,128)(2,1)} %fusion.29), channel_id=1, source_target_pairs={{0,4},{4,0},{1,5},{5,1},{2,6},{6,2},{3,7},{7,3},{8,12},{12,8},{9,1... | collective-permute-start | bytes 1572872 | tf_op jit(solution)/shard_map/ppermute | solution.py:49
  315.5 22.6 %collective-permute-start.20 = (bf16[2,2,64,1024]{3,2,1,0:T(8,128)(2,1)}, bf16[2,2,64,1024]{3,2,1,0:T(8,128)(2,1)}, u32[]{:S(2)}, u32[]{:S(2)}) collective-permute-start(bf16[2,2,64,1024]{3,2,1,0:T(8,128)(2,1)} %fusion.28), channel_id=1, source_target_pairs={{0,2},{2,0},{1,3},{3,1},{4,6},{6,4},{5,7},{7,5},{8,10},{10,8},{9,1... | collective-permute-start | bytes 1572872 | tf_op jit(solution)/shard_map/ppermute | solution.py:49
  320.2 25.2 %collective-permute-start.21 = (bf16[1024,512]{1,0:T(8,128)(2,1)}, bf16[1024,512]{1,0:T(8,128)(2,1)}, u32[]{:S(2)}, u32[]{:S(2)}) collective-permute-start(bf16[1024,512]{1,0:T(8,128)(2,1)} %convolution_convert_fusion.3), channel_id=1, source_target_pairs={{0,1},{1,0},{2,3},{3,2},{4,5},{5,4},{6,7},{7,6},{8,9},{9,8},{10,11... | collective-permute-start | bytes 3145736 | tf_op jit(solution)/shard_map/ppermute | solution.py:49
  344.1 25.9 %collective-permute-start.23 = (bf16[2,64,4096]{2,1,0:T(8,128)(2,1)}, bf16[2,64,4096]{2,1,0:T(8,128)(2,1)}, u32[]{:S(2)}, u32[]{:S(2)}) collective-permute-start(bf16[2,64,4096]{2,1,0:T(8,128)(2,1)} %pad_maximum_fusion.5), channel_id=1, source_target_pairs={{0,8},{8,0},{16,24},{24,16},{1,9},{9,1},{17,25},{25,17},{2,10},{10... | collective-permute-start | bytes 3145736 | tf_op jit(solution)/shard_map/ppermute | solution.py:49
  349.7 21.6 %collective-permute-start.22 = (bf16[2,2,2,64,512]{4,3,2,1,0:T(8,128)(2,1)}, bf16[2,2,2,64,512]{4,3,2,1,0:T(8,128)(2,1)}, u32[]{:S(2)}, u32[]{:S(2)}) collective-permute-start(bf16[2,2,2,64,512]{4,3,2,1,0:T(8,128)(2,1)} %dynamic-slice_bitcast_fusion.7), channel_id=1, source_target_pairs={{0,2},{2,0},{1,3},{3,1},{4,6},{6,4},{5,7},{7,5},{8,10},{10,8},{9,1... | collective-permute-start | bytes 1572872 | tf_op jit(solution)/shard_map/ppermute | solution.py:49
  391.3 5.8 %collective-permute-start.24 = (bf16[2,2,256,1024]{3,2,1,0:T(8,128)(2,1)}, bf16[2,2,256,1024]{3,2,1,0:T(8,128)(2,1)}, u32[]{:S(2)}, u32[]{:S(2)}) collective-permute-start(bf16[2,2,256,1024]{3,2,1,0:T(8,128)(2,1)} %copy_bitcast_fusion), channel_id=1, source_target_pairs={{0,1},{1,0},{2,3},{3,2},{4,5},{5,4},{6,7},{7,6},{8,9},{9,8},{10,11... | collective-permute-start | bytes 6291464 | tf_op jit(solution)/shard_map/ppermute | solution.py:49
  391.3 26.0 %collective-permute-start.25 = (bf16[2,2,128,768]{3,2,1,0:T(8,128)(2,1)}, bf16[2,2,128,768]{3,2,1,0:T(8,128)(2,1)}, u32[]{:S(2)}, u32[]{:S(2)}) collective-permute-start(bf16[2,2,128,768]{3,2,1,0:T(8,128)(2,1)} %dynamic-slice_bitcast_fusion.6), channel_id=1, source_target_pairs={{0,4},{4,0},{1,5},{5,1},{2,6},{6,2},{3,7},{7,3},{8,12},{12,8},{9,1... | collective-permute-start | bytes 2359304 | tf_op jit(solution)/shard_map/ppermute | solution.py:49
  394.4 22.9 %collective-permute-start.26 = (bf16[2,2,64,512]{3,2,0,1:T(8,128)(2,1)S(1)}, bf16[2,2,64,512]{3,2,0,1:T(8,128)(2,1)S(1)}, u32[]{:S(2)}, u32[]{:S(2)}) collective-permute-start(bf16[2,2,64,512]{3,2,0,1:T(8,128)(2,1)S(1)} %copy.334), channel_id=1, source_target_pairs={{0,4},{4,0},{1,5},{5,1},{2,6},{6,2},{3,7},{7,3},{8,12},{12,8},{9,1... | collective-permute-start | bytes 786440 | tf_op jit(solution)/shard_map/ppermute | solution.py:49
  394.7 43.0 %collective-permute-start.30 = (bf16[64,4096]{1,0:T(8,128)(2,1)}, bf16[64,4096]{1,0:T(8,128)(2,1)}, u32[]{:S(2)}, u32[]{:S(2)}) collective-permute-start(bf16[64,4096]{1,0:T(8,128)(2,1)} %pad_maximum_fusion.12), channel_id=1, source_target_pairs={{0,16},{8,24},{16,0},{24,8},{1,17},{9,25},{17,1},{25,9},{2,18},{10... | collective-permute-start | bytes 1572872 | tf_op jit(solution)/shard_map/ppermute | solution.py:49
  400.1 24.3 %copy-start.57 = (f32[1024]{0:T(1024)S(1)}, f32[1024]{0:T(1024)}, u32[]{:S(2)}) copy-start(f32[1024]{0:T(1024)} %get-tuple-element.292) | copy-start | bytes 12292
  400.1 24.5 %copy-start.21 = (bf16[512,1024]{1,0:T(8,128)(2,1)S(1)}, bf16[512,1024]{1,0:T(8,128)(2,1)}, u32[]{:S(2)}) copy-start(bf16[512,1024]{1,0:T(8,128)(2,1)} %copy-done.20) | copy-start | bytes 3145732
  400.1 60.5 %collective-permute-start.29 = (bf16[2,256,1024]{2,1,0:T(8,128)(2,1)}, bf16[2,256,1024]{2,1,0:T(8,128)(2,1)}, u32[]{:S(2)}, u32[]{:S(2)}) collective-permute-start(bf16[2,256,1024]{2,1,0:T(8,128)(2,1)} %fusion.5), channel_id=1, source_target_pairs={{0,2},{2,0},{1,3},{3,1},{4,6},{6,4},{5,7},{7,5},{8,10},{10,8},{9,1... | collective-permute-start | bytes 3145736 | tf_op jit(solution)/shard_map/ppermute | solution.py:49
  419.4 13.7 %collective-permute-start.27 = (bf16[2,128,768]{2,1,0:T(8,128)(2,1)}, bf16[2,128,768]{2,1,0:T(8,128)(2,1)}, u32[]{:S(2)}, u32[]{:S(2)}) collective-permute-start(bf16[2,128,768]{2,1,0:T(8,128)(2,1)} %fusion.30), channel_id=1, source_target_pairs={{0,8},{8,0},{16,24},{24,16},{1,9},{9,1},{17,25},{25,17},{2,10},{10... | collective-permute-start | bytes 1179656 | tf_op jit(solution)/shard_map/ppermute | solution.py:49
  429.3 18.3 %all-to-all-start.6 = ((bf16[32,26,128]{2,1,0:T(8,128)(2,1)}), bf16[32,26,128]{2,1,0:T(8,128)(2,1)S(1)}, u32[]{:S(2)}, u32[]{:S(2)}) async-start(bf16[32,26,128]{2,1,0:T(8,128)(2,1)} %fusion.53), calls=%async_computation.6 | async-start | bytes 524288 | tf_op jit(solution)/shard_map/all_to_all | solution.py:808
  435.0 23.6 %collective-permute-start.28 = (bf16[128,768]{1,0:T(8,128)(2,1)}, bf16[128,768]{1,0:T(8,128)(2,1)}, u32[]{:S(2)}, u32[]{:S(2)}) collective-permute-start(bf16[128,768]{1,0:T(8,128)(2,1)} %fusion.49), channel_id=1, source_target_pairs={{0,16},{8,24},{16,0},{24,8},{1,17},{9,25},{17,1},{25,9},{2,18},{10... | collective-permute-start | bytes 589832 | tf_op jit(solution)/shard_map/ppermute | solution.py:49
  439.5 9.9 %collective-permute-start.31 = (bf16[2,64,512]{2,1,0:T(8,128)(2,1)}, bf16[2,64,512]{2,1,0:T(8,128)(2,1)S(1)}, u32[]{:S(2)}, u32[]{:S(2)}) collective-permute-start(bf16[2,64,512]{2,1,0:T(8,128)(2,1)} %fusion.60), channel_id=1, source_target_pairs={{0,8},{8,0},{16,24},{24,16},{1,9},{9,1},{17,25},{25,17},{2,10},{10... | collective-permute-start | bytes 393224 | tf_op jit(solution)/shard_map/ppermute | solution.py:49
  442.5 8.6 %collective-permute-start.34 = (bf16[32,2048]{1,0:T(8,128)(2,1)S(1)}, bf16[32,2048]{1,0:T(8,128)(2,1)S(1)}, u32[]{:S(2)}, u32[]{:S(2)}) collective-permute-start(bf16[32,2048]{1,0:T(8,128)(2,1)S(1)} %fusion.66), channel_id=1, source_target_pairs={{0,1},{1,0},{2,3},{3,2},{4,5},{5,4},{6,7},{7,6},{8,9},{9,8},{10,11... | collective-permute-start | bytes 393224 | tf_op jit(solution)/shard_map/ppermute | solution.py:49
  451.0 6.5 %collective-permute-start.32 = (bf16[64,512]{1,0:T(8,128)(2,1)}, bf16[64,512]{1,0:T(8,128)(2,1)}, u32[]{:S(2)}, u32[]{:S(2)}) collective-permute-start(bf16[64,512]{1,0:T(8,128)(2,1)} %fusion.71), channel_id=1, source_target_pairs={{0,16},{8,24},{16,0},{24,8},{1,17},{9,25},{17,1},{25,9},{2,18},{10... | collective-permute-start | bytes 196616 | tf_op jit(solution)/shard_map/ppermute | solution.py:49
  458.5 1.4 collective-permute-start.33
  461.4 8.7 %all-to-all-start.5 = ((bf16[4,32,3,256]{3,1,2,0:T(8,128)(2,1)}), bf16[4,32,3,256]{3,1,2,0:T(8,128)(2,1)S(1)}, u32[]{:S(2)}, u32[]{:S(2)}) async-start(bf16[4,32,3,256]{3,1,2,0:T(8,128)(2,1)} %copy.336), calls=%async_computation.5 | async-start | bytes 393216 | tf_op jit(solution)/shard_map/all_to_all | solution.py:781
  (67 other events, 592.0 us)
Sparse Core Ops, SparseCore 0:
  37.5 144.3 all-gather.2

commit v4 on v3

--- a/solution.py
+++ b/solution.py
@@ -427,7 +427,7 @@
             ],
         ),
         compiler_params=pltpu.CompilerParams(
-            dimension_semantics=("arbitrary",), vmem_limit_bytes=56 << 20
+            dimension_semantics=("arbitrary",), vmem_limit_bytes=46 << 20
         ),
         input_output_aliases={11: 0} if more else {},
         name="attend_back",

time: 487 us -> 479 us (0.984)
  starting transfers between devices: 65.3 us -> 59.3 us
    ppermute x35, starting transfers between devices: 38 us -> 32.7 us  [swap(): return lax.ppermute(x, axis, [(i, i ^ bit) for i in range(n)])]
    unnamed x159 -> x169, local copies, waits for them, and re-layouts: 10 us -> 13.1 us
  transfers between devices with their start and end apart: 43 -> 43, of which waited for: 16 -> 17; matrix products, arithmetic and copies ran while one was open for 22% -> 22% of each run, Pallas kernels for 16% -> 16%
where the time goes in v4:
time: 479 us; the launch traced here: 472 us
  waiting for transfers between devices  136 us (28%)
  Pallas kernels  97.9 us (20%)
  other arithmetic  81.5 us (17%)
  starting transfers between devices  59.3 us (12%)
  local copies, waits for them, and re-layouts  47.1 us (10%)
  matrix products  28.7 us (6%)
  between operations  16.1 us (3%)
  blocking collectives  5.56 us (1%)
    ppermute x35, waiting for transfers between devices, swap(): return lax.ppermute(x, axis, [(i, i ^ bit) for i in range(n)])  102 us
    pallas_call x2, Pallas kernels, attention_backward(): pl.pallas_call(functools.partial(bwd_kernel, m), out_shape=(jax.ShapeDtyp...  34.6 us
    ppermute x35, starting transfers between devices, swap(): return lax.ppermute(x, axis, [(i, i ^ bit) for i in range(n)])  32.7 us
    dot_general x13, matrix products, dot(): lax.dot_general(a, b, (((ca,), (cb,)), ((), ())), preferred_element_type=...  28.7 us
    convert_element_type x18, other arithmetic, send(): out = total([take(t, 1 - mine) for t in self.terms]).astype(BF)  27.8 us
    pallas_call x1, Pallas kernels, ff_backward(): pl.pallas_call(ff_backward_kernel, out_shape=(jax.ShapeDtypeStruct((d, fh...  21.5 us
    pallas_call x1, Pallas kernels, attention_forward(): pl.pallas_call(fwd_kernel, out_shape=(jax.ShapeDtypeStruct((M, L, width),...  21.5 us
    pallas_call x1, Pallas kernels, ff_forward(): pl.pallas_call(ff_forward_kernel, out_shape=(jax.ShapeDtypeStruct((n2, fh...  20.3 us
  transfers between devices with their start and end apart: 43, of which 17 were waited for; matrix products, arithmetic and copies ran while one was open for 22% of the time, Pallas kernels for 16%

profile of v4, /device:TPU:0, one launch (start us, length us, event | category | flops | bytes accessed | tf_op | source)
XLA Modules:
  0.0 472.3 jit_solution(2616230457398982186)
XLA Ops:
  10.9 3.5 all-to-all-start.3
  16.2 4.3 all-to-all-start
  21.6 5.6 %all-gather = s32[2,1,1024]{2,1,0:T(1,128)S(1)} all-gather(s32[2,1,256]{2,1,0:T(1,128)S(1)} %copy-done.65), channel_id=2, replica_groups=mesh['dz'=4,'dx'=2,'yy'=2,'core'=2] {'yy','core'}, dimensions={2}, use_global_device_ids=true | all-gather | bytes 10240 | tf_op jit(solution)/shard_map/all_gather | solution.py:610
  28.9 2.6 collective-permute-start.2
  32.3 4.3 collective-permute-done.2
  37.4 2.0 collective-permute-start
  44.3 4.1 all-to-all-start.1
  49.2 2.8 collective-permute-start.6
  52.0 16.9 %collective-permute-done = bf16[2,256,1024]{2,1,0:T(8,128)(2,1)} collective-permute-done((bf16[2,256,1024]{2,1,0:T(8,128)(2,1)S(1)}, bf16[2,256,1024]{2,1,0:T(8,128)(2,1)}, u32[]{:S(2)}, u32[]{:S(2)}) %collective-permute-start) | collective-permute-done | bytes 1048608 | tf_op jit(solution)/shard_map/ppermute | solution.py:49
  72.0 5.7 %collective-permute-done.6 = bf16[2,4,32,384]{3,2,1,0:T(8,128)(2,1)} collective-permute-done((bf16[2,4,32,384]{3,2,1,0:T(8,128)(2,1)}, bf16[2,4,32,384]{3,2,1,0:T(8,128)(2,1)}, u32[]{:S(2)}, u32[]{:S(2)}) %collective-permute-start.6) | collective-permute-done | bytes 196640 | tf_op jit(solution)/shard_map/ppermute | solution.py:49
  80.6 2.1 collective-permute-start.3
  83.4 36.8 %collective-permute-done.3 = bf16[2,4,32,384]{3,2,1,0:T(8,128)(2,1)S(1)} collective-permute-done((bf16[2,4,32,384]{3,2,1,0:T(8,128)(2,1)S(1)}, bf16[2,4,32,384]{3,2,1,0:T(8,128)(2,1)S(1)}, u32[]{:S(2)}, u32[]{:S(2)}) %collective-permute-start.3) | collective-permute-done | bytes 196640 | tf_op jit(solution)/shard_map/ppermute | solution.py:49
  125.0 10.7 %collective-permute-done.4 = bf16[4,4,32,384]{3,2,1,0:T(8,128)(2,1)} collective-permute-done((bf16[4,4,32,384]{3,2,1,0:T(8,128)(2,1)}, bf16[4,4,32,384]{3,2,1,0:T(8,128)(2,1)}, u32[]{:S(2)}, u32[]{:S(2)}) %collective-permute-start.4) | collective-permute-done | bytes 393248 | tf_op jit(solution)/shard_map/ppermute | solution.py:49
  137.1 2.1 select_bitcast_fusion.1
  139.7 3.6 convolution_convert_fusion.1
  143.4 21.5 %attend.1 = (bf16[2,1024,256]{2,1,0:T(8,128)(2,1)S(1)}, bf16[2,1024,256]{2,1,0:T(8,128)(2,1)S(1)}, f32[2,2,2,8,1,128]{5,4,3,2,1,0:T(1,128)S(1)}) custom-call(s32[16]{0:T(128)S(1)} %reshape.1012.lohi, bf16[2,1024,768]{2,1,0:T(8,128)(2,1)S(1)} %bitcast.490, bf16[2,1024,768]{2,1,0:T(8,128)(2,1)S(1)} %bitcast.491, bf16[2,1024,768]{2,1,0:T(8,128)(2,1)S(1)} %bitcast.492, ...), custom_call_target="tpu_custom_call" | custom-call | tf_op jit(solution)/shard_map/attend/pallas_call | solution.py:362
  166.9 4.0 all-to-all-start.2
  171.0 11.0 %all-gather.3.cloned.1.call-done.wi_ref.wo_ref = bf16[1024,4608]{1,0:T(8,128)(2,1)} async-done(((bf16[64,4608]{1,0:T(8,128)(2,1)}), bf16[1024,4608]{1,0:T(8,128)(2,1)}) %all-gather.3.cloned.1.call-update) | async-done | bytes 9437200 | tf_op jit(solution)/shard_map/all_gather | solution.py:654
  186.4 2.3 fusion.95
  188.8 2.0 fusion.109
  197.5 20.3 %feed.1 = (bf16[1024,2048]{1,0:T(8,128)(2,1)}, bf16[1024,2048]{1,0:T(8,128)(2,1)}, f32[512,1024]{1,0:T(8,128)}, bf16[512,1024]{1,0:T(8,128)(2,1)}) custom-call(bf16[512,1024]{1,0:T(8,128)(2,1)} %copy-done.1, bf16[512,1024]{1,0:T(8,128)(2,1)} %copy-done.7, bf16[1024,4608]{1,0:T(8,128)(2,1)} %all-gather.3.cloned.1.call-done.wi_ref.wo_ref, ...), custom_call_target="tpu_custom_call" | custom-call | tf_op jit(solution)/shard_map/feed/pallas_call | solution.py:530
  218.3 2.5 collective-permute-done.10
  220.8 2.9 fusion.101
  229.7 2.4 maximum_select_fusion.2
  233.1 2.4 fusion.17
  235.5 3.6 fusion.20
  245.3 21.5 %feed_back.1 = (bf16[1024,1024]{1,0:T(8,128)(2,1)S(1)}, bf16[1024,1024]{1,0:T(8,128)(2,1)S(1)}, f32[1,2048]{1,0:T(1,128)S(1)}, f32[512,1024]{1,0:T(8,128)S(1)}, bf16[512,1024]{1,0:T(8,128)(2,1)S(1)}) custom-call(bf16[1024,1024]{1,0:T(8,128)(2,1)} %pad_maximum_fusion.2.go_ref, bf16[512,1024]{1,0:T(8,128)(2,1)S(1)} %copy-done.2, ...), custom_call_target="tpu_custom_call" | custom-call | tf_op jit(solution)/shard_map/feed_back/pallas_call | solution.py:553
  278.4 4.3 all-to-all-start.4
  286.0 2.1 fusion.32
  290.0 17.9 %all-to-all-done.4 = bf16[4,512,256]{2,1,0:T(8,128)(2,1)} async-done(((bf16[4,512,256]{2,1,0:T(8,128)(2,1)}), bf16[4,512,256]{2,1,0:T(8,128)(2,1)}, u32[]{:S(2)}, u32[]{:S(2)}) %all-to-all-start.4) | async-done | bytes 1048608 | tf_op jit(solution)/shard_map/all_to_all | solution.py:730
  309.2 2.0 fusion.29
  312.1 2.2 fusion.28
  315.4 3.1 convolution_convert_fusion.3
  318.6 17.1 %attend_back.2 = (bf16[2,1024,768]{2,1,0:T(8,128)(2,1)S(1)}, f32[2,2,8,128]{3,2,1,0:T(8,128)S(1)}, f32[2,2,128,256]{3,2,1,0:T(8,128)S(1)}) custom-call(s32[16]{0:T(128)S(1)} %reshape.1012.lohi, bf16[2,1024,768]{2,1,0:T(8,128)(2,1)} %bitcast.493, bf16[2,1024,768]{2,1,0:T(8,128)(2,1)} %bitcast.494, bf16[2,1024,768]{2,1,0:T(8,128)(2,1)} %bitcast.495, ...), custom_call_target="tpu_custom_call" | custom-call | tf_op jit(solution)/shard_map/attend_back/pallas_call | solution.py:402
  343.4 2.4 add_convert_fusion
  351.0 17.5 %attend_back.3 = (bf16[2,1024,768]{2,1,0:T(8,128)(2,1)S(1)}, f32[2,2,8,128]{3,2,1,0:T(8,128)S(1)}, f32[2,2,128,256]{3,2,1,0:T(8,128)S(1)}) custom-call(s32[16]{0:T(128)S(1)} %reshape.1012.lohi, bf16[2,1024,768]{2,1,0:T(8,128)(2,1)} %bitcast.496, bf16[2,1024,768]{2,1,0:T(8,128)(2,1)} %bitcast.497, ...), custom_call_target="tpu_custom_call", output_to_operand_aliasing={{0}: (11, {})} | custom-call | tf_op jit(solution)/shard_map/attend_back/pallas_call | solution.py:402
  370.1 3.5 convolution_convert_fusion.2
  381.3 3.7 convolution_convert_fusion
  385.0 2.0 copy-done.33
  389.8 2.1 collective-permute-start.26
  393.6 3.0 fusion.5
  397.2 17.2 %collective-permute-done.26 = bf16[2,2,64,512]{3,2,0,1:T(8,128)(2,1)S(1)} collective-permute-done((bf16[2,2,64,512]{3,2,0,1:T(8,128)(2,1)S(1)}, bf16[2,2,64,512]{3,2,0,1:T(8,128)(2,1)S(1)}, u32[]{:S(2)}, u32[]{:S(2)}) %collective-permute-start.26) | collective-permute-done | bytes 262176 | tf_op jit(solution)/shard_map/ppermute | solution.py:49
  414.4 2.1 fusion.30
  422.7 3.0 all-to-all-start.6
  436.4 3.9 all-to-all-done.6
  447.0 3.3 collective-permute-done.32
  454.1 3.4 all-to-all-start.5
  457.5 3.9 fusion.8
  (445 shorter events, 132.9 us)
Async XLA Ops:
  10.9 5.3 %all-to-all-start.3 = ((bf16[2,32,2560]{2,1,0:T(8,128)(2,1)}), bf16[2,32,2560]{2,1,0:T(8,128)(2,1)S(1)}, u32[]{:S(2)}, u32[]{:S(2)}) async-start(bf16[2,32,2560]{2,1,0:T(8,128)(2,1)} %pad_maximum_fusion.16), calls=%async_computation.3 | async-start | bytes 655360 | tf_op jit(solution)/shard_map/all_to_all | solution.py:650
  16.2 11.0 %all-to-all-start = ((bf16[4,32,768]{2,1,0:T(8,128)(2,1)}), bf16[4,32,768]{2,1,0:T(8,128)(2,1)S(1)}, u32[]{:S(2)}, u32[]{:S(2)}) async-start(bf16[4,32,768]{2,1,0:T(8,128)(2,1)} %reshape.1014), calls=%async_computation | async-start | bytes 393216 | tf_op jit(solution)/shard_map/all_to_all | solution.py:615
  20.5 161.4 %all-gather.3.cloned.1.call-start = ((), (), s32[]{:S(2)}) async-start(), calls=%async_computation.7 | async-start | bytes 10027008 | tf_op jit(solution)/shard_map/all_gather | solution.py:654
  27.2 5.1 %collective-permute-start.5 = (bf16[4,32,384]{2,1,0:T(8,128)(2,1)S(1)}, bf16[4,32,384]{2,1,0:T(8,128)(2,1)S(1)}, u32[]{:S(2)}, u32[]{:S(2)}) collective-permute-start(bf16[4,32,384]{2,1,0:T(8,128)(2,1)S(1)} %get-tuple-element.358), channel_id=1, source_target_pairs={{0,4},{4,0},{1,5},{5,1},{2,6},{6,2},{3,7},{7,3},{8,12},{12,8},{9,1... | collective-permute-start | bytes 294920 | tf_op jit(solution)/shard_map/ppermute | solution.py:49
  28.9 7.8 %collective-permute-start.2 = (bf16[4,32,384]{2,1,0:T(8,128)(2,1)S(1)}, bf16[4,32,384]{2,1,0:T(8,128)(2,1)S(1)}, u32[]{:S(2)}, u32[]{:S(2)}) collective-permute-start(bf16[4,32,384]{2,1,0:T(8,128)(2,1)S(1)} %get-tuple-element.359), channel_id=1, source_target_pairs={{0,16},{8,24},{16,0},{24,8},{1,17},{9,25},{17,1},{25,9},{2,18},{10... | collective-permute-start | bytes 294920 | tf_op jit(solution)/shard_map/ppermute | solution.py:49
  37.4 31.5 %collective-permute-start = (bf16[2,256,1024]{2,1,0:T(8,128)(2,1)S(1)}, bf16[2,256,1024]{2,1,0:T(8,128)(2,1)}, u32[]{:S(2)}, u32[]{:S(2)}) collective-permute-start(bf16[2,256,1024]{2,1,0:T(8,128)(2,1)S(1)} %bitcast.517), channel_id=1, source_target_pairs={{0,2},{2,0},{1,3},{3,1},{4,6},{6,4},{5,7},{7,5},{8,10},{10,8},{9,1... | collective-permute-start | bytes 3145736 | tf_op jit(solution)/shard_map/ppermute | solution.py:49
  44.3 35.2 %all-to-all-start.1 = ((bf16[32,26,128]{2,1,0:T(8,128)(2,1)}), bf16[32,26,128]{2,1,0:T(8,128)(2,1)S(1)}, u32[]{:S(2)}, u32[]{:S(2)}) async-start(bf16[32,26,128]{2,1,0:T(8,128)(2,1)} %broadcast_in_dim.110), calls=%async_computation.1 | async-start | bytes 524288 | tf_op jit(solution)/shard_map/all_to_all | solution.py:629
  49.2 28.5 %collective-permute-start.6 = (bf16[2,4,32,384]{3,2,1,0:T(8,128)(2,1)}, bf16[2,4,32,384]{3,2,1,0:T(8,128)(2,1)}, u32[]{:S(2)}, u32[]{:S(2)}) collective-permute-start(bf16[2,4,32,384]{3,2,1,0:T(8,128)(2,1)} %pad_maximum_fusion.18), channel_id=1, source_target_pairs={{0,16},{8,24},{16,0},{24,8},{1,17},{9,25},{17,1},{25,9},{2,18},{10... | collective-permute-start | bytes 589832 | tf_op jit(solution)/shard_map/ppermute | solution.py:49
  71.8 65.3 %collective-permute-start.1 = (bf16[2,2,256,1024]{3,2,1,0:T(8,128)(2,1)}, bf16[2,2,256,1024]{3,2,1,0:T(8,128)(2,1)}, u32[]{:S(2)}, u32[]{:S(2)}) collective-permute-start(bf16[2,2,256,1024]{3,2,1,0:T(8,128)(2,1)} %pad_maximum_fusion.1), channel_id=1, source_target_pairs={{0,1},{1,0},{2,3},{3,2},{4,5},{5,4},{6,7},{7,6},{8,9},{9,8},{10,11... | collective-permute-start | bytes 6291464 | tf_op jit(solution)/shard_map/ppermute | solution.py:49
  79.5 44.2 %collective-permute-start.7 = (bf16[2,2,4,32,384]{4,3,2,1,0:T(8,128)(2,1)}, bf16[2,2,4,32,384]{4,3,2,1,0:T(8,128)(2,1)}, u32[]{:S(2)}, u32[]{:S(2)}) collective-permute-start(bf16[2,2,4,32,384]{4,3,2,1,0:T(8,128)(2,1)} %pad_maximum_fusion.15), channel_id=1, source_target_pairs={{0,8},{8,0},{16,24},{24,16},{1,9},{9,1},{17,25},{25,17},{2,10},{10... | collective-permute-start | bytes 1179656 | tf_op jit(solution)/shard_map/ppermute | solution.py:49
  79.5 43.1 %copy-start.35 = (bf16[32,26,128]{2,1,0:T(8,128)(2,1)}, bf16[32,26,128]{2,1,0:T(8,128)(2,1)S(1)}, u32[]{:S(2)}) copy-start(bf16[32,26,128]{2,1,0:T(8,128)(2,1)S(1)} %all-to-all-done.1) | copy-start | bytes 638980
  80.6 39.6 %collective-permute-start.3 = (bf16[2,4,32,384]{3,2,1,0:T(8,128)(2,1)S(1)}, bf16[2,4,32,384]{3,2,1,0:T(8,128)(2,1)S(1)}, u32[]{:S(2)}, u32[]{:S(2)}) collective-permute-start(bf16[2,4,32,384]{3,2,1,0:T(8,128)(2,1)S(1)} %copy-done.55), channel_id=1, source_target_pairs={{0,8},{8,0},{16,24},{24,16},{1,9},{9,1},{17,25},{25,17},{2,10},{10... | collective-permute-start | bytes 589832 | tf_op jit(solution)/shard_map/ppermute | solution.py:49
  121.0 14.7 %collective-permute-start.4 = (bf16[4,4,32,384]{3,2,1,0:T(8,128)(2,1)}, bf16[4,4,32,384]{3,2,1,0:T(8,128)(2,1)}, u32[]{:S(2)}, u32[]{:S(2)}) collective-permute-start(bf16[4,4,32,384]{3,2,1,0:T(8,128)(2,1)} %bitcast.18), channel_id=1, source_target_pairs={{0,4},{4,0},{1,5},{5,1},{2,6},{6,2},{3,7},{7,3},{8,12},{12,8},{9,1... | collective-permute-start | bytes 1179656 | tf_op jit(solution)/shard_map/ppermute | solution.py:49
  143.4 21.5 %copy-start = (bf16[2048,768]{1,0:T(8,128)(2,1)}, bf16[2048,768]{1,0:T(8,128)(2,1)S(1)}, u32[]{:S(2)}) copy-start(bf16[2048,768]{1,0:T(8,128)(2,1)S(1)} %convolution_convert_fusion.1) | copy-start | bytes 9437188
  166.9 18.5 %all-to-all-start.2 = ((bf16[2,4,256,256]{3,2,0,1:T(8,128)(2,1)}), bf16[2,4,256,256]{3,2,0,1:T(8,128)(2,1)S(1)}, u32[]{:S(2)}, u32[]{:S(2)}) async-start(bf16[2,4,256,256]{3,2,0,1:T(8,128)(2,1)} %copy.311), calls=%async_computation.2 | async-start | bytes 2097152 | tf_op jit(solution)/shard_map/all_to_all | solution.py:683
  183.3 5.5 %collective-permute-start.8 = (bf16[1024,512]{1,0:T(8,128)(2,1)S(1)}, bf16[1024,512]{1,0:T(8,128)(2,1)}, u32[]{:S(2)}, u32[]{:S(2)}) collective-permute-start(bf16[1024,512]{1,0:T(8,128)(2,1)S(1)} %slice.244), channel_id=1, source_target_pairs={{0,1},{1,0},{2,3},{3,2},{4,5},{5,4},{6,7},{7,6},{8,9},{9,8},{10,11... | collective-permute-start | bytes 3145736 | tf_op jit(solution)/shard_map/ppermute | solution.py:49
  193.9 2.7 collective-permute-start.9
  217.8 2.9 collective-permute-start.10
  229.2 2.9 collective-permute-start.11
  240.3 28.7 %collective-permute-start.12 = (bf16[2,2,2,64,1024]{4,3,2,1,0:T(8,128)(2,1)S(1)}, bf16[2,2,2,64,1024]{4,3,2,1,0:T(8,128)(2,1)S(1)}, u32[]{:S(2)}, u32[]{:S(2)}) collective-permute-start(bf16[2,2,2,64,1024]{4,3,2,1,0:T(8,128)(2,1)S(1)} %get-tuple-element.324), channel_id=1, source_target_pairs={{0,2},{2,0},{1,3},{3,1},{4,6},{6,4},{5,7},{7,5},{8,10},{10,8},{9,1... | collective-permute-start | bytes 3145736 | tf_op jit(solution)/shard_map/ppermute | solution.py:49
  242.9 26.2 %collective-permute-start.13 = (bf16[2,2,2,64,1024]{4,3,2,1,0:T(8,128)(2,1)S(1)}, bf16[2,2,2,64,1024]{4,3,2,1,0:T(8,128)(2,1)}, u32[]{:S(2)}, u32[]{:S(2)}) collective-permute-start(bf16[2,2,2,64,1024]{4,3,2,1,0:T(8,128)(2,1)S(1)} %get-tuple-element.322), channel_id=1, source_target_pairs={{0,4},{4,0},{1,5},{5,1},{2,6},{6,2},{3,7},{7,3},{8,12},{12,8},{9,1... | collective-permute-start | bytes 3145736 | tf_op jit(solution)/shard_map/ppermute | solution.py:49
  266.8 42.3 %copy-start.11 = (bf16[1024,1024]{1,0:T(8,128)(2,1)}, bf16[1024,1024]{1,0:T(8,128)(2,1)S(1)}, u32[]{:S(2)}) copy-start(bf16[1024,1024]{1,0:T(8,128)(2,1)S(1)} %get-tuple-element.103) | copy-start | bytes 6291460
  269.0 2.7 collective-permute-start.14
  269.1 40.0 %collective-permute-start.15 = (bf16[2,2,2,64,1024]{4,3,2,1,0:T(8,128)(2,1)}, bf16[2,2,2,64,1024]{4,3,2,1,0:T(8,128)(2,1)}, u32[]{:S(2)}, u32[]{:S(2)}) collective-permute-start(bf16[2,2,2,64,1024]{4,3,2,1,0:T(8,128)(2,1)} %dynamic-slice_bitcast_fusion.3), channel_id=1, source_target_pairs={{0,4},{4,0},{1,5},{5,1},{2,6},{6,2},{3,7},{7,3},{8,12},{12,8},{9,1... | collective-permute-start | bytes 3145736 | tf_op jit(solution)/shard_map/ppermute | solution.py:49
  270.3 38.9 %collective-permute-start.16 = (bf16[2,2,2,64,1024]{4,3,2,1,0:T(8,128)(2,1)}, bf16[2,2,2,64,1024]{4,3,2,1,0:T(8,128)(2,1)}, u32[]{:S(2)}, u32[]{:S(2)}) collective-permute-start(bf16[2,2,2,64,1024]{4,3,2,1,0:T(8,128)(2,1)} %dynamic-slice_bitcast_fusion.2), channel_id=1, source_target_pairs={{0,2},{2,0},{1,3},{3,1},{4,6},{6,4},{5,7},{7,5},{8,10},{10,8},{9,1... | collective-permute-start | bytes 3145736 | tf_op jit(solution)/shard_map/ppermute | solution.py:49
  278.4 29.4 %all-to-all-start.4 = ((bf16[4,512,256]{2,1,0:T(8,128)(2,1)}), bf16[4,512,256]{2,1,0:T(8,128)(2,1)}, u32[]{:S(2)}, u32[]{:S(2)}) async-start(bf16[4,512,256]{2,1,0:T(8,128)(2,1)} %pad_maximum_fusion.4), calls=%async_computation.4 | async-start | bytes 2097152 | tf_op jit(solution)/shard_map/all_to_all | solution.py:730
  284.9 50.8 %collective-permute-start.17 = (bf16[2,2,64,1024]{3,2,0,1:T(8,128)(2,1)}, bf16[2,2,64,1024]{3,2,0,1:T(8,128)(2,1)}, u32[]{:S(2)}, u32[]{:S(2)}) collective-permute-start(bf16[2,2,64,1024]{3,2,0,1:T(8,128)(2,1)} %copy.323), channel_id=1, source_target_pairs={{0,4},{4,0},{1,5},{5,1},{2,6},{6,2},{3,7},{7,3},{8,12},{12,8},{9,1... | collective-permute-start | bytes 1572872 | tf_op jit(solution)/shard_map/ppermute | solution.py:49
  288.0 47.7 %collective-permute-start.18 = (bf16[2,2,64,1024]{3,2,1,0:T(8,128)(2,1)}, bf16[2,2,64,1024]{3,2,1,0:T(8,128)(2,1)}, u32[]{:S(2)}, u32[]{:S(2)}) collective-permute-start(bf16[2,2,64,1024]{3,2,1,0:T(8,128)(2,1)} %fusion.32), channel_id=1, source_target_pairs={{0,2},{2,0},{1,3},{3,1},{4,6},{6,4},{5,7},{7,5},{8,10},{10,8},{9,1... | collective-permute-start | bytes 1572872 | tf_op jit(solution)/shard_map/ppermute | solution.py:49
  311.2 24.5 %collective-permute-start.19 = (bf16[2,2,64,1024]{3,2,1,0:T(8,128)(2,1)}, bf16[2,2,64,1024]{3,2,1,0:T(8,128)(2,1)}, u32[]{:S(2)}, u32[]{:S(2)}) collective-permute-start(bf16[2,2,64,1024]{3,2,1,0:T(8,128)(2,1)} %fusion.29), channel_id=1, source_target_pairs={{0,4},{4,0},{1,5},{5,1},{2,6},{6,2},{3,7},{7,3},{8,12},{12,8},{9,1... | collective-permute-start | bytes 1572872 | tf_op jit(solution)/shard_map/ppermute | solution.py:49
  314.3 21.4 %collective-permute-start.20 = (bf16[2,2,64,1024]{3,2,1,0:T(8,128)(2,1)}, bf16[2,2,64,1024]{3,2,1,0:T(8,128)(2,1)}, u32[]{:S(2)}, u32[]{:S(2)}) collective-permute-start(bf16[2,2,64,1024]{3,2,1,0:T(8,128)(2,1)} %fusion.28), channel_id=1, source_target_pairs={{0,2},{2,0},{1,3},{3,1},{4,6},{6,4},{5,7},{7,5},{8,10},{10,8},{9,1... | collective-permute-start | bytes 1572872 | tf_op jit(solution)/shard_map/ppermute | solution.py:49
  318.5 24.9 %collective-permute-start.21 = (bf16[1024,512]{1,0:T(8,128)(2,1)}, bf16[1024,512]{1,0:T(8,128)(2,1)}, u32[]{:S(2)}, u32[]{:S(2)}) collective-permute-start(bf16[1024,512]{1,0:T(8,128)(2,1)} %convolution_convert_fusion.3), channel_id=1, source_target_pairs={{0,1},{1,0},{2,3},{3,2},{4,5},{5,4},{6,7},{7,6},{8,9},{9,8},{10,11... | collective-permute-start | bytes 3145736 | tf_op jit(solution)/shard_map/ppermute | solution.py:49
  342.4 26.1 %collective-permute-start.23 = (bf16[2,64,4096]{2,1,0:T(8,128)(2,1)}, bf16[2,64,4096]{2,1,0:T(8,128)(2,1)}, u32[]{:S(2)}, u32[]{:S(2)}) collective-permute-start(bf16[2,64,4096]{2,1,0:T(8,128)(2,1)} %pad_maximum_fusion.5), channel_id=1, source_target_pairs={{0,8},{8,0},{16,24},{24,16},{1,9},{9,1},{17,25},{25,17},{2,10},{10... | collective-permute-start | bytes 3145736 | tf_op jit(solution)/shard_map/ppermute | solution.py:49
  347.7 22.4 %collective-permute-start.22 = (bf16[2,2,2,64,512]{4,3,2,1,0:T(8,128)(2,1)}, bf16[2,2,2,64,512]{4,3,2,1,0:T(8,128)(2,1)}, u32[]{:S(2)}, u32[]{:S(2)}) collective-permute-start(bf16[2,2,2,64,512]{4,3,2,1,0:T(8,128)(2,1)} %dynamic-slice_bitcast_fusion.7), channel_id=1, source_target_pairs={{0,2},{2,0},{1,3},{3,1},{4,6},{6,4},{5,7},{7,5},{8,10},{10,8},{9,1... | collective-permute-start | bytes 1572872 | tf_op jit(solution)/shard_map/ppermute | solution.py:49
  388.6 5.1 %collective-permute-start.24 = (bf16[2,2,256,1024]{3,2,1,0:T(8,128)(2,1)}, bf16[2,2,256,1024]{3,2,1,0:T(8,128)(2,1)}, u32[]{:S(2)}, u32[]{:S(2)}) collective-permute-start(bf16[2,2,256,1024]{3,2,1,0:T(8,128)(2,1)} %copy_bitcast_fusion), channel_id=1, source_target_pairs={{0,1},{1,0},{2,3},{3,2},{4,5},{5,4},{6,7},{7,6},{8,9},{9,8},{10,11... | collective-permute-start | bytes 6291464 | tf_op jit(solution)/shard_map/ppermute | solution.py:49
  388.6 25.8 %collective-permute-start.25 = (bf16[2,2,128,768]{3,2,1,0:T(8,128)(2,1)}, bf16[2,2,128,768]{3,2,1,0:T(8,128)(2,1)}, u32[]{:S(2)}, u32[]{:S(2)}) collective-permute-start(bf16[2,2,128,768]{3,2,1,0:T(8,128)(2,1)} %dynamic-slice_bitcast_fusion.6), channel_id=1, source_target_pairs={{0,4},{4,0},{1,5},{5,1},{2,6},{6,2},{3,7},{7,3},{8,12},{12,8},{9,1... | collective-permute-start | bytes 2359304 | tf_op jit(solution)/shard_map/ppermute | solution.py:49
  389.8 24.6 %collective-permute-start.26 = (bf16[2,2,64,512]{3,2,0,1:T(8,128)(2,1)S(1)}, bf16[2,2,64,512]{3,2,0,1:T(8,128)(2,1)S(1)}, u32[]{:S(2)}, u32[]{:S(2)}) collective-permute-start(bf16[2,2,64,512]{3,2,0,1:T(8,128)(2,1)S(1)} %copy.334), channel_id=1, source_target_pairs={{0,4},{4,0},{1,5},{5,1},{2,6},{6,2},{3,7},{7,3},{8,12},{12,8},{9,1... | collective-permute-start | bytes 786440 | tf_op jit(solution)/shard_map/ppermute | solution.py:49
  392.1 26.6 %copy-start.28 = (bf16[512,1024]{1,0:T(8,128)(2,1)S(1)}, bf16[512,1024]{1,0:T(8,128)(2,1)}, u32[]{:S(2)}) copy-start(bf16[512,1024]{1,0:T(8,128)(2,1)} %copy-done.27) | copy-start | bytes 3145732
  392.1 38.3 %collective-permute-start.30 = (bf16[64,4096]{1,0:T(8,128)(2,1)}, bf16[64,4096]{1,0:T(8,128)(2,1)}, u32[]{:S(2)}, u32[]{:S(2)}) collective-permute-start(bf16[64,4096]{1,0:T(8,128)(2,1)} %pad_maximum_fusion.12), channel_id=1, source_target_pairs={{0,16},{8,24},{16,0},{24,8},{1,17},{9,25},{17,1},{25,9},{2,18},{10... | collective-permute-start | bytes 1572872 | tf_op jit(solution)/shard_map/ppermute | solution.py:49
  396.6 22.5 %copy-start.23 = (bf16[512,1024]{1,0:T(8,128)(2,1)S(1)}, bf16[512,1024]{1,0:T(8,128)(2,1)}, u32[]{:S(2)}) copy-start(bf16[512,1024]{1,0:T(8,128)(2,1)} %copy-done.22) | copy-start | bytes 3145732
  396.6 56.6 %collective-permute-start.29 = (bf16[2,256,1024]{2,1,0:T(8,128)(2,1)}, bf16[2,256,1024]{2,1,0:T(8,128)(2,1)}, u32[]{:S(2)}, u32[]{:S(2)}) collective-permute-start(bf16[2,256,1024]{2,1,0:T(8,128)(2,1)} %fusion.5), channel_id=1, source_target_pairs={{0,2},{2,0},{1,3},{3,1},{4,6},{6,4},{5,7},{7,5},{8,10},{10,8},{9,1... | collective-permute-start | bytes 3145736 | tf_op jit(solution)/shard_map/ppermute | solution.py:49
  416.4 11.2 %collective-permute-start.27 = (bf16[2,128,768]{2,1,0:T(8,128)(2,1)}, bf16[2,128,768]{2,1,0:T(8,128)(2,1)}, u32[]{:S(2)}, u32[]{:S(2)}) collective-permute-start(bf16[2,128,768]{2,1,0:T(8,128)(2,1)} %fusion.30), channel_id=1, source_target_pairs={{0,8},{8,0},{16,24},{24,16},{1,9},{9,1},{17,25},{25,17},{2,10},{10... | collective-permute-start | bytes 1179656 | tf_op jit(solution)/shard_map/ppermute | solution.py:49
  422.7 17.6 %all-to-all-start.6 = ((bf16[32,26,128]{2,1,0:T(8,128)(2,1)}), bf16[32,26,128]{2,1,0:T(8,128)(2,1)S(1)}, u32[]{:S(2)}, u32[]{:S(2)}) async-start(bf16[32,26,128]{2,1,0:T(8,128)(2,1)} %fusion.53), calls=%async_computation.6 | async-start | bytes 524288 | tf_op jit(solution)/shard_map/all_to_all | solution.py:808
  428.8 22.5 %collective-permute-start.28 = (bf16[128,768]{1,0:T(8,128)(2,1)S(1)}, bf16[128,768]{1,0:T(8,128)(2,1)S(1)}, u32[]{:S(2)}, u32[]{:S(2)}) collective-permute-start(bf16[128,768]{1,0:T(8,128)(2,1)S(1)} %fusion.49), channel_id=1, source_target_pairs={{0,16},{8,24},{16,0},{24,8},{1,17},{9,25},{17,1},{25,9},{2,18},{10... | collective-permute-start | bytes 589832 | tf_op jit(solution)/shard_map/ppermute | solution.py:49
  431.4 10.7 %collective-permute-start.31 = (bf16[2,64,512]{2,1,0:T(8,128)(2,1)S(1)}, bf16[2,64,512]{2,1,0:T(8,128)(2,1)S(1)}, u32[]{:S(2)}, u32[]{:S(2)}) collective-permute-start(bf16[2,64,512]{2,1,0:T(8,128)(2,1)S(1)} %fusion.60), channel_id=1, source_target_pairs={{0,8},{8,0},{16,24},{24,16},{1,9},{9,1},{17,25},{25,17},{2,10},{10... | collective-permute-start | bytes 393224 | tf_op jit(solution)/shard_map/ppermute | solution.py:49
  434.0 9.9 %collective-permute-start.34 = (bf16[32,2048]{1,0:T(8,128)(2,1)S(1)}, bf16[32,2048]{1,0:T(8,128)(2,1)S(1)}, u32[]{:S(2)}, u32[]{:S(2)}) collective-permute-start(bf16[32,2048]{1,0:T(8,128)(2,1)S(1)} %fusion.66), channel_id=1, source_target_pairs={{0,1},{1,0},{2,3},{3,2},{4,5},{5,4},{6,7},{7,6},{8,9},{9,8},{10,11... | collective-permute-start | bytes 393224 | tf_op jit(solution)/shard_map/ppermute | solution.py:49
  443.7 6.5 %collective-permute-start.32 = (bf16[64,512]{1,0:T(8,128)(2,1)}, bf16[64,512]{1,0:T(8,128)(2,1)}, u32[]{:S(2)}, u32[]{:S(2)}) collective-permute-start(bf16[64,512]{1,0:T(8,128)(2,1)} %fusion.71), channel_id=1, source_target_pairs={{0,16},{8,24},{16,0},{24,8},{1,17},{9,25},{17,1},{25,9},{2,18},{10... | collective-permute-start | bytes 196616 | tf_op jit(solution)/shard_map/ppermute | solution.py:49
  451.3 1.3 collective-permute-start.33
  454.1 8.7 %all-to-all-start.5 = ((bf16[4,32,3,256]{3,1,2,0:T(8,128)(2,1)}), bf16[4,32,3,256]{3,1,2,0:T(8,128)(2,1)S(1)}, u32[]{:S(2)}, u32[]{:S(2)}) async-start(bf16[4,32,3,256]{3,1,2,0:T(8,128)(2,1)} %copy.336), calls=%async_computation.5 | async-start | bytes 393216 | tf_op jit(solution)/shard_map/all_to_all | solution.py:781
  (72 other events, 572.5 us)
Sparse Core Ops, SparseCore 0:
  37.5 144.3 all-gather.2
